TPU v7x, 512 devices: a whole 4x8x8 slice. The times are simulated.
512 devices in a mesh: col: 128 (over z, y, core), row: 4 (over x).
Axes of the slice: x: 4, y: 8, z: 8, core: 2. Of those that a mesh axis runs over, the one named last changes fastest.
Arguments:
- panel: int32 [128], replicated, may hold values from 0 to 127, each once
- centres_cols: bfloat16 [65536, 1024], P('col'), may hold values from -1 to 1
- centres_rows: bfloat16 [2048, 1024], P(('row', 'col')), may hold values from -1 to 1
- diag_inverse: float32 [65536, 512], P('col'), as said below
- trailing: float32 [2048, 65536], P('row', 'col'), may hold values from -6 to 6
Outputs:
- updated: float32 [2048, 65536], P('row', 'col')
Inputs may be any that keep to these rules, and one draw needn't show every extreme that they name: panel holds each of 0 to 127 once. Each 512 x 512 block of diag_inverse is lower triangular with a positive diagonal.
All inputs are finite; a program needn't handle non-finite values.
Results may differ from a plain program's by a relative error of at most 0.0003.
Values may be sent and summed in bfloat16 or wider, within the bound.
No kernel may reach another device: no remote copies, remote signals or barrier semaphores. Data moves between devices by JAX's collectives and lax.ppermute only.
A program may use at most 64 MiB of HBM per device.

v0:
```python
import math

import jax
import jax.numpy as jnp
from jax import lax
from jax.sharding import PartitionSpec as P

LAYERS = 3


def broadcast(shard, axis, root):
    mine = lax.axis_index(axis) == root
    return lax.psum(jnp.where(mine, shard, jnp.zeros_like(shard)), axis)


def kernel(left, right):
    gram = lax.dot_general(
        left, right, (((1,), (1,)), ((), ())), preferred_element_type=jnp.float32
    )
    left_f = left.astype(jnp.float32)
    right_f = right.astype(jnp.float32)
    inv_left = 1.0 / jnp.sqrt(jnp.sum(left_f * left_f, axis=1) + 1e-06)
    inv_right = 1.0 / jnp.sqrt(jnp.sum(right_f * right_f, axis=1) + 1e-06)
    cosine = gram * inv_left[:, None] * inv_right[None, :]
    theta = cosine
    rho_now = cosine
    for layer in range(LAYERS):
        angle_now = jnp.arccos(rho_now)
        zero_order = (math.pi - angle_now) / math.pi
        rho_next = (jnp.sqrt(1.0 - rho_now * rho_now) + (math.pi - angle_now) * rho_now) / math.pi
        theta = theta * zero_order + rho_next
        rho_now = rho_next
    return theta / (inv_left[:, None] * inv_right[None, :])


def apply_inverse(values, inverse):
    return lax.dot_general(
        values,
        inverse,
        (((1,), (1,)), ((), ())),
        precision=lax.Precision.HIGHEST,
        preferred_element_type=jnp.float32,
    )


def on_device(panel, centres_cols, centres_rows, diag_inverse, trailing):
    col_count = lax.axis_size("col")
    target_rank = col_count // 4
    block_ids = jnp.arange(col_count, dtype=jnp.int32)
    panel_at = jnp.sum(jnp.where(panel == target_rank, block_ids, 0))
    panel_x = broadcast(centres_cols, "col", panel_at)
    panel_inv = broadcast(diag_inverse, "col", panel_at)

    def panel_rows_of(piece):
        return apply_inverse(kernel(piece, panel_x), panel_inv)

    rows_l = panel_rows_of(lax.all_gather(centres_rows, "col", axis=0, tiled=True))
    cols_l = panel_rows_of(centres_cols)
    update = lax.dot_general(
        rows_l,
        cols_l,
        (((1,), (1,)), ((), ())),
        precision=lax.Precision.HIGHEST,
        preferred_element_type=jnp.float32,
    )
    block_here = lax.axis_index("col")
    own_rank = lax.dynamic_index_in_dim(panel, block_here, 0, keepdims=False)
    return jnp.where(own_rank > target_rank, trailing - update, trailing)


def solution(mesh):
    return jax.shard_map(
        on_device,
        mesh=mesh,
        in_specs=(P(), P("col", None), P(("row", "col"), None), P("col", None), P("row", "col")),
        out_specs=P("row", "col"),
        check_vma=False,
    )
```

profile of v0, /device:TPU:1, one launch (start us, length us, event | category | flops | bytes accessed | tf_op | source)
XLA Modules:
  0.0 512.0 jit_solution(12042767771723486847)
XLA Ops:
  6.5 0.0 all-reduce.3.cloned.1.call-start
  6.5 1.3 fusion.110
  8.5 1.1 broadcast_select_fusion
  9.5 0.0 copy-start.2
  9.6 0.0 all-reduce.3.cloned.1.call-update
  9.6 0.0 all-reduce.5.cloned.1.call-start
  9.6 1.1 copy-done.2
  10.8 1.1 broadcast_select_fusion.1
  11.8 0.0 copy-start.5
  11.8 0.0 copy-start
  11.8 0.0 all-reduce.5.cloned.1.call-update
  11.9 0.0 all-gather.3.cloned.1.call-start
  11.9 0.7 all-gather.3.cloned.1.call-update
  12.6 0.0 copy-done.5
  12.6 0.6 dynamic_slice.4
  13.8 0.0 copy-done
  13.9 0.3 multiply_reduce_fusion
  14.1 197.4 %all-reduce.3.cloned.1.call-done = bf16[512,1024]{1,0:T(8,128)(2,1)} async-done(((bf16[512,1024]{1,0:T(8,128)(2,1)}), bf16[512,1024]{1,0:T(8,128)(2,1)}) %all-reduce.3.cloned.1.call-update) | async-done | bytes 1048592 | tf_op jit(solution)/shard_map/psum | solution.py:13
  211.6 0.0 copy-start.3
  211.6 1.6 multiply_reduce_fusion.1
  213.2 0.0 copy-done.3
  213.2 0.7 fusion.1
  213.9 193.9 %all-reduce.5.cloned.1.call-done = f32[512,512]{1,0:T(8,128)} async-done(((f32[512,512]{1,0:T(8,128)}), f32[512,512]{1,0:T(8,128)}) %all-reduce.5.cloned.1.call-update) | async-done | bytes 1048592 | tf_op jit(solution)/shard_map/psum | solution.py:13
  407.8 12.7 %fusion.4 = f32[512,512]{1,0:T(8,128)S(1)} fusion(f32[512,512]{1,0:T(8,128)} %all-reduce.5.cloned.1.call-done, f32[512,512]{0,1:T(8,128)S(1)} %fusion.1, f32[512]{0:T(512)S(1)} %add_rsqrt_fusion, f32[512]{0:T(512)S(1)} %add_rsqrt_fusion.1), kind=kOutput, calls=%fused_computation.10 | convolution fusion | flops 1620574208 | bytes 3149824 | tf_op jit(solution)/shard_map/dot_general | solution.py:37
  420.5 67.7 %all-gather.3.cloned.1.call-done = bf16[128,4,1024]{2,1,0:T(4,128)(2,1)} async-done(((bf16[1,4,1024]{2,1,0:T(4,128)(2,1)}), bf16[128,4,1024]{2,1,0:T(4,128)(2,1)}) %all-gather.3.cloned.1.call-update) | async-done | bytes 1048592 | tf_op jit(solution)/shard_map/all_gather | solution.py:57
  488.2 1.3 reshape.15
  489.6 0.3 multiply_reduce_fusion.2
  489.8 0.0 copy-start.4
  489.9 0.7 fusion.3
  490.6 0.5 copy-done.4
  491.1 0.0 copy-start.1
  491.1 11.5 %fusion.52 = f32[512,512]{1,0:T(8,128)S(1)} fusion(f32[512,512]{1,0:T(8,128)S(1)} %copy-done.4, f32[512,512]{0,1:T(8,128)S(1)} %fusion.3, f32[512]{0:T(512)S(1)} %add_rsqrt_fusion.1, f32[512]{0:T(512)S(1)} %add_rsqrt_fusion.2), kind=kOutput, calls=%fused_computation.58 | convolution fusion | flops 1620574208 | bytes 3149824 | tf_op jit(solution)/shard_map/dot_general | solution.py:37
  502.6 0.0 copy-done.1
  502.6 2.8 subtract_select_fusion
  (3 shorter events, 0.0 us)
Async XLA Ops:
  6.5 205.0 %all-reduce.3.cloned.1.call-start = ((), (), s32[]{:S(2)}) async-start(), calls=%async_computation | async-start | bytes 2097152 | tf_op jit(solution)/shard_map/psum | solution.py:13
  9.5 1.2 copy-start.2
  9.6 398.3 %all-reduce.5.cloned.1.call-start = ((), (), s32[]{:S(2)}) async-start(), calls=%async_computation.1 | async-start | bytes 2097152 | tf_op jit(solution)/shard_map/psum | solution.py:13
  11.8 0.8 copy-start.5
  11.8 2.0 copy-start
  11.9 476.3 %all-gather.3.cloned.1.call-start = ((), (), s32[]{:S(2)}) async-start(), calls=%async_computation.2 | async-start | bytes 1056768 | tf_op jit(solution)/shard_map/all_gather | solution.py:57
  211.6 1.6 copy-start.3
  489.8 1.2 copy-start.4
  491.1 11.5 %copy-start.1 = (f32[512,512]{1,0:T(8,128)S(1)}, f32[512,512]{1,0:T(8,128)}, u32[]{:S(2)}) copy-start(f32[512,512]{1,0:T(8,128)} %param.9) | copy-start | bytes 3145732
Sparse Core Ops, SparseCore 0:
  10.6 200.9 all-reduce.2
  214.8 193.0 all-reduce.4
  410.9 77.2 all-gather.2
where the time goes:
time: 512 us
  waiting for transfers between devices  460 us (90%)
  matrix products  28.5 us (6%)
  between operations  14.5 us (3%)
  other arithmetic  5.59 us (1%)
    psum x2, waiting for transfers between devices, broadcast(): return lax.psum(jnp.where(mine, shard, jnp.zeros_like(shard)), axis)  391 us
    all_gather x1, waiting for transfers between devices, on_device(): lax.all_gather(centres_rows, 'col', axis=0, tiled=True)  67.7 us
    dot_general x2, matrix products, apply_inverse(): lax.dot_general(values, inverse, (((1,), (1,)), ((), ())), precision=lax....  24.2 us
  transfers between devices with their start and end apart: 3, of which 3 were waited for; matrix products, arithmetic and copies ran while one was open for 3% of the time, Pallas kernels for 0%

commit v1 on v0

v1 whole, which is shorter than its diff:
```python
import math

import jax
import jax.numpy as jnp
from jax import lax
from jax.sharding import Mesh, PartitionSpec as P

LAYERS = 3
CORES = 2


def repeat_gather(piece, axis, count):
    return lax.all_to_all(jnp.broadcast_to(piece[None], (count,) + piece.shape), axis, 0, 0)


def split(values):
    high = lax.reduce_precision(values, 8, 7)
    return high.astype(jnp.bfloat16), (values - high).astype(jnp.bfloat16)


def dot_t(left, right):
    return lax.dot_general(left, right, (((1,), (1,)), ((), ())), preferred_element_type=jnp.float32)


def dot_pair(left, right):
    return dot_t(left[0], right[0]) + (dot_t(left[0], right[1]) + dot_t(left[1], right[0]))


def norms(pieces):
    total = 0.0
    for piece in pieces:
        wide = piece.astype(jnp.float32)
        total = total + jnp.sum(wide * wide, axis=1)
    return jnp.sqrt(total + 1e-06)


def kernel(left, right):
    gram = sum(dot_t(a, b) for a, b in zip(left, right))
    norm_left, norm_right = norms(left)[:, None], norms(right)[None, :]
    rho = jnp.clip(gram * (1.0 / norm_left) * (1.0 / norm_right), -1.0, 1.0)
    theta = rho
    for layer in range(LAYERS):
        angle = jnp.arccos(rho)
        zero_order = (math.pi - angle) / math.pi
        rho_next = (jnp.sqrt(1.0 - rho * rho) + (math.pi - angle) * rho) / math.pi
        theta = theta * zero_order + rho_next
        rho = rho_next
    return theta * (norm_left * norm_right)


def lanes_first(block):
    return jnp.concatenate([block[:, 128 * i : 128 * (i + 1)] for i in range(block.shape[1] // 128)], axis=0)


def on_device(chips, row_count, panel, centres_cols, centres_rows, diag_inverse, trailing):
    size, width = centres_cols.shape
    blocks = panel.shape[0]
    target_rank = blocks // 4
    half = width // CORES
    quarter = size // row_count
    own_rows = centres_rows.shape[0]
    panel_at = jnp.sum(jnp.where(panel == target_rank, jnp.arange(blocks, dtype=jnp.int32), 0))
    owner_chip, owner_core = panel_at // CORES, panel_at % CORES
    chip, core, row = lax.axis_index("chip"), lax.axis_index("core"), lax.axis_index("row")
    swap = [(0, 1), (1, 0)]

    def share(which):
        x = lax.dynamic_slice(centres_cols, (row * quarter, which * half), (quarter, half))
        inv = lax.dynamic_slice_in_dim(diag_inverse, row * quarter + which * (quarter // CORES), quarter // CORES, 0)
        high, low = split(inv)
        mine = lax.dynamic_slice_in_dim(centres_rows, which * half, half, 1)
        return jnp.concatenate([lanes_first(x), lanes_first(high), lanes_first(low)], axis=0), mine

    kept, rows_kept = share(core)
    sent, rows_sent = share(1 - core)
    n_panel = kept.shape[0]
    swapped = lax.ppermute(jnp.concatenate([sent, lanes_first(rows_sent)], axis=0), "core", swap)
    taken = jnp.where(core == owner_core, kept, swapped[:n_panel])
    groups = half // 128
    rows_got = swapped[n_panel:].reshape(groups, own_rows, 128)
    rows_own = lanes_first(rows_kept).reshape(groups, own_rows, 128)
    first = core == 0
    rows_chip = jnp.concatenate(
        [jnp.where(first, rows_own, rows_got), jnp.where(first, rows_got, rows_own)], axis=1
    ).reshape(groups * CORES * own_rows, 128)

    per_chip = n_panel // chips
    outgoing = jnp.concatenate(
        [taken.reshape(chips, per_chip, 128), jnp.broadcast_to(rows_chip[None], (chips,) + rows_chip.shape)], axis=1
    )
    incoming = lax.all_to_all(outgoing, "chip", 0, 0)
    piece = lax.dynamic_index_in_dim(incoming, owner_chip, 0, keepdims=False)[:per_chip]
    rows_half = incoming[:, per_chip:].reshape(chips, groups, CORES * own_rows, 128)
    rows_half = rows_half.transpose(0, 2, 1, 3).reshape(chips * CORES * own_rows, half)
    rows_other = lax.ppermute(rows_half, "core", swap)

    mine = repeat_gather(piece, "chip", chips).reshape(n_panel, 128)
    all_mine = repeat_gather(mine, "row", row_count)
    all_other = lax.ppermute(all_mine, "core", swap)

    def unpack(got):
        n_x = quarter * groups
        x = got[:, :n_x].reshape(row_count, groups, quarter, 128)
        x = x.transpose(0, 2, 1, 3).reshape(size, half)
        inv = got[:, n_x:].reshape(row_count, 2, size // 128, quarter // CORES, 128)
        inv = inv.transpose(1, 0, 3, 2, 4).reshape(2, size // CORES, size)
        return x, inv

    x_own, inv_own = unpack(all_mine)
    x_other, inv_other = unpack(all_other)
    panel_x = (x_own, x_other)
    cols = (
        lax.dynamic_slice_in_dim(centres_cols, core * half, half, 1),
        lax.dynamic_slice_in_dim(centres_cols, (1 - core) * half, half, 1),
    )
    inverse = [jnp.concatenate([inv_own[i], inv_other[i]], axis=0) for i in range(2)]
    rows_l = dot_pair(split(kernel((rows_half, rows_other), panel_x)), inverse)
    cols_l = dot_pair(split(kernel(cols, panel_x)), inverse)
    update = dot_pair(split(rows_l), split(cols_l))
    own_rank = lax.dynamic_index_in_dim(panel, chip * CORES + core, 0, keepdims=False)
    return jnp.where(own_rank > target_rank, trailing - update, trailing)


def solution(mesh):
    col_count, row_count = mesh.devices.shape
    chips = col_count // CORES
    fine = Mesh(mesh.devices.reshape(chips, CORES, row_count), ("chip", "core", "row"))

    def step(*arrays):
        return on_device(chips, row_count, *arrays)

    col = ("chip", "core")
    return jax.shard_map(
        step,
        mesh=fine,
        in_specs=(P(), P(col, None), P(("row",) + col, None), P(col, None), P("row", col)),
        out_specs=P("row", col),
        check_vma=False,
    )
```

time: 512 us -> 122 us (0.24)
  waiting for transfers between devices: 460 us -> 39.4 us
  starting transfers between devices: 0.09 us -> 41.5 us
  between operations: 14.5 us -> 3.81 us
  local copies, waits for them, and re-layouts: 3.59 us -> 9.89 us
  matrix products: 28.5 us -> 23.2 us
    psum x2 -> x0, waiting for transfers between devices: 391 us -> none  [broadcast(): return lax.psum(jnp.where(mine, shard, jnp.zeros_like(shard)), axis)]
    all_gather x1 -> x0, waiting for transfers between devices: 67.7 us -> none  [on_device(): lax.all_gather(centres_rows, 'col', axis=0, tiled=True)]
    all_to_all x0 -> x3, waiting for transfers between devices: none -> 39.4 us  [the longest x1 21.9 us: on_device(): incoming = lax.all_to_all(outgoing, 'chip', 0, 0)]
    all_to_all x0 -> x3, starting transfers between devices: none -> 22.5 us  [the longest x2 11.5 us: repeat_gather(): lax.all_to_all(jnp.broadcast_to(piece[None], (count,) + piece.shape), axi...]
    ppermute x0 -> x3, starting transfers between devices: none -> 19.1 us  [the longest x1 8.78 us: on_device(): lax.ppermute(jnp.concatenate([sent, lanes_first(rows_sent)], axis=0), 'co...]
    dot_general x5 -> x13, matrix products: 28.5 us -> 23.2 us  [dot_t(): lax.dot_general(left, right, (((1,), (1,)), ((), ())), preferred_element_...]
  transfers between devices with their start and end apart: 3 -> 6, of which waited for: 3 -> 3; matrix products, arithmetic and copies ran while one was open for 3% -> 5% of each run, Pallas kernels for 0% -> 0%
where the time goes in v1:
time: 122 us
  starting transfers between devices  41.5 us (34%)
  waiting for transfers between devices  39.4 us (32%)
  matrix products  23.2 us (19%)
  local copies, waits for them, and re-layouts  9.89 us (8%)
  between operations  3.81 us (3%)
  other arithmetic  3.75 us (3%)
    dot_general x13, matrix products, dot_t(): lax.dot_general(left, right, (((1,), (1,)), ((), ())), preferred_element_...  23.2 us
    all_to_all x1, waiting for transfers between devices, on_device(): incoming = lax.all_to_all(outgoing, 'chip', 0, 0)  21.9 us
    all_to_all x2, waiting for transfers between devices, repeat_gather(): lax.all_to_all(jnp.broadcast_to(piece[None], (count,) + piece.shape), axi...  17.5 us
    all_to_all x2, starting transfers between devices, repeat_gather(): lax.all_to_all(jnp.broadcast_to(piece[None], (count,) + piece.shape), axi...  11.5 us
    all_to_all x1, starting transfers between devices, on_device(): incoming = lax.all_to_all(outgoing, 'chip', 0, 0)  10.9 us
    ppermute x1, starting transfers between devices, on_device(): lax.ppermute(jnp.concatenate([sent, lanes_first(rows_sent)], axis=0), 'co...  8.78 us
    ppermute x1, starting transfers between devices, on_device(): all_other = lax.ppermute(all_mine, 'core', swap)  7 us
    unnamed x20, local copies, waits for them, and re-layouts  4.01 us
  transfers between devices with their start and end apart: 6, of which 3 were waited for; matrix products, arithmetic and copies ran while one was open for 5% of the time, Pallas kernels for 0%

profile of v1, /device:TPU:1, one launch (start us, length us, event | category | flops | bytes accessed | tf_op | source)
XLA Modules:
  0.0 121.7 jit_solution(2472251142072350307)
XLA Ops:
  0.0 1.0 fusion.35
  1.1 0.8 constant_dynamic-update-slice_fusion.11
  1.8 0.8 constant_dynamic-update-slice_fusion.10
  2.6 0.8 constant_dynamic-update-slice_fusion.9
  3.4 0.8 constant_dynamic-update-slice_fusion.8
  4.4 0.2 concatenate.22
  4.6 8.8 %collective-permute-start = (bf16[1040,128]{1,0:T(8,128)(2,1)S(1)}, bf16[1040,128]{1,0:T(8,128)(2,1)S(1)}, u32[]{:S(2)}, u32[]{:S(2)}) collective-permute-start(bf16[1040,128]{1,0:T(8,128)(2,1)S(1)} %concatenate.22), channel_id=1, source_target_pairs={{0,4},{4,0},{1,5},{5,1},{2,6},{6,2},{3,7},{7,3},{8,12},{12,8},{9,1... | collective-permute-start | bytes 798728 | tf_op jit(solution)/shard_map/ppermute | solution.py:77
  13.4 0.7 fusion.43
  16.4 0.9 pad_maximum_fusion
  17.3 10.9 %all-to-all-start = ((bf16[64,48,128]{2,1,0:T(8,128)(2,1)}), bf16[64,48,128]{2,1,0:T(8,128)(2,1)S(1)}, u32[]{:S(2)}, u32[]{:S(2)}) async-start(bf16[64,48,128]{2,1,0:T(8,128)(2,1)} %pad_maximum_fusion), calls=%async_computation | async-start | bytes 1572864 | tf_op jit(solution)/shard_map/all_to_all | solution.py:91
  29.0 21.9 %all-to-all-done = bf16[64,48,128]{2,1,0:T(8,128)(2,1)S(1)} async-done(((bf16[64,48,128]{2,1,0:T(8,128)(2,1)}), bf16[64,48,128]{2,1,0:T(8,128)(2,1)S(1)}, u32[]{:S(2)}, u32[]{:S(2)}) %all-to-all-start) | async-done | bytes 786464 | tf_op jit(solution)/shard_map/all_to_all | solution.py:91
  50.9 0.7 broadcast_in_dim.34
  51.6 7.4 %all-to-all-start.1 = ((bf16[64,16,128]{2,1,0:T(8,128)(2,1)}), bf16[64,16,128]{2,1,0:T(8,128)(2,1)S(1)}, u32[]{:S(2)}, u32[]{:S(2)}) async-start(bf16[64,16,128]{2,1,0:T(8,128)(2,1)} %broadcast_in_dim.34), calls=%async_computation.1 | async-start | bytes 524288 | tf_op jit(solution)/shard_map/all_to_all | solution.py:13
  59.0 0.8 slice_bitcast_fusion
  59.9 3.3 %collective-permute-start.1 = (bf16[512,512]{1,0:T(8,128)(2,1)}, bf16[512,512]{1,0:T(8,128)(2,1)S(1)}, u32[]{:S(2)}, u32[]{:S(2)}) collective-permute-start(bf16[512,512]{1,0:T(8,128)(2,1)} %slice_bitcast_fusion), channel_id=1, source_target_pairs={{0,4},{4,0},{1,5},{5,1},{2,6},{6,2},{3,7},{7,3},{8,12},{12,8},{9,1... | collective-permute-start | bytes 1572872 | tf_op jit(solution)/shard_map/ppermute | solution.py:95
  63.2 8.4 %all-to-all-done.1 = bf16[64,16,128]{2,1,0:T(8,128)(2,1)S(1)} async-done(((bf16[64,16,128]{2,1,0:T(8,128)(2,1)}), bf16[64,16,128]{2,1,0:T(8,128)(2,1)S(1)}, u32[]{:S(2)}, u32[]{:S(2)}) %all-to-all-start.1) | async-done | bytes 262176 | tf_op jit(solution)/shard_map/all_to_all | solution.py:13
  71.5 1.1 broadcast_in_dim.36
  72.6 4.1 %all-to-all-start.2 = ((bf16[4,1024,128]{2,1,0:T(8,128)(2,1)}), bf16[4,1024,128]{2,1,0:T(8,128)(2,1)S(1)}, u32[]{:S(2)}, u32[]{:S(2)}) async-start(bf16[4,1024,128]{2,1,0:T(8,128)(2,1)} %broadcast_in_dim.36), calls=%async_computation.2 | async-start | bytes 2097152 | tf_op jit(solution)/shard_map/all_to_all | solution.py:13
  76.8 0.6 dynamic_slice.32
  78.0 0.3 multiply_reduce_fusion
  78.3 0.2 multiply_reduce_fusion.5
  78.5 0.1 reduce_sum.75
  78.6 0.2 multiply_reduce_fusion.4
  78.8 9.1 %all-to-all-done.2 = bf16[4,1024,128]{2,1,0:T(8,128)(2,1)S(1)} async-done(((bf16[4,1024,128]{2,1,0:T(8,128)(2,1)}), bf16[4,1024,128]{2,1,0:T(8,128)(2,1)S(1)}, u32[]{:S(2)}, u32[]{:S(2)}) %all-to-all-start.2) | async-done | bytes 1048608 | tf_op jit(solution)/shard_map/all_to_all | solution.py:13
  88.0 7.0 %collective-permute-start.2 = (bf16[4,1024,128]{2,1,0:T(8,128)(2,1)S(1)}, bf16[4,1024,128]{2,1,0:T(8,128)(2,1)S(1)}, u32[]{:S(2)}, u32[]{:S(2)}) collective-permute-start(bf16[4,1024,128]{2,1,0:T(8,128)(2,1)S(1)} %all-to-all-done.2), channel_id=1, source_target_pairs={{0,4},{4,0},{1,5},{5,1},{2,6},{6,2},{3,7},{7,3},{8,12},{12,8},{9,1... | collective-permute-start | bytes 3145736 | tf_op jit(solution)/shard_map/ppermute | solution.py:99
  95.0 0.2 multiply_reduce_fusion.3
  95.2 0.4 copy.12
  95.6 0.2 copy.14
  95.9 0.2 copy.16
  96.1 0.5 fusion.20
  96.6 0.5 fusion.22
  97.2 0.2 multiply_reduce_fusion.2
  97.4 0.4 copy.13
  97.8 0.2 copy.15
  98.1 0.2 copy.17
  98.3 8.5 %multiply_multiply_fusion.1 = f32[512,512]{1,0:T(8,128)S(1)} fusion(f32[512,512]{1,0:T(8,128)S(1)} %fusion.22, bf16[512,512]{1,0:T(8,128)(2,1)S(1)} %collective-permute-done.1, f32[512]{0:T(512)S(1)} %get-tuple-element.47, f32[512]{0:T(512)S(1)} %get-tuple-element.45, f32[512]{0:T(512)S(1)} %get-tuple-element.46, f32[512]{0:T(512)S(1)} %get-tuple-element.44, ...), kind=kOutput, calls=%fused_computation.30 | convolution fusion | flops 279445504 | bytes 3153920 | tf_op jit(solution)/shard_map/dot_general | solution.py:22
  106.8 0.5 fusion.31
  107.3 0.3 bitcast_dynamic-update-slice_fusion
  107.6 0.5 fusion.30
  108.0 8.5 %multiply_multiply_fusion = f32[512,512]{1,0:T(8,128)S(1)} fusion(f32[512,512]{1,0:T(8,128)S(1)} %fusion.20, f32[512]{0:T(512)S(1)} %get-tuple-element.43, f32[512]{0:T(512)S(1)} %get-tuple-element.42, f32[512]{0:T(512)S(1)} %get-tuple-element.47, f32[512]{0:T(512)S(1)} %get-tuple-element.46, bf16[64,8,4,128]{3,2,1,0:T(4,128)(2,1)S(1)} %bitcast.85, ...), kind=kOutput, calls=%fused_computation.27 | convolution fusion | flops 279445504 | bytes 3153924 | tf_op jit(solution)/shard_map/dot_general | solution.py:22
  116.5 0.5 fusion.34
  117.0 0.5 fusion.33
  117.5 0.5 fusion.5
  118.0 0.5 fusion.1
  118.5 0.5 fusion.32
  119.0 0.5 fusion.13
  119.5 0.7 copy-done.1
  120.2 1.5 %subtract_select_fusion = f32[512,512]{1,0:T(8,128)} fusion(f32[512,512]{1,0:T(8,128)S(1)} %copy-done.1, f32[512,512]{1,0:T(8,128)S(1)} %fusion.32, f32[512,512]{1,0:T(8,128)S(1)} %fusion.13, f32[512,512]{1,0:T(8,128)S(1)} %fusion.5, pred[]{:T(512)} %bitcast, f32[512,512]{1,0:T(8,128)S(1)} %fusion.1), kind=kOutput, calls=%fused_computation | convolution fusion | flops 270794752 | bytes 6291457 | tf_op jit(solution)/shard_map/dot_general | solution.py:22
  (35 shorter events, 0.6 us)
Async XLA Ops:
  0.0 4.3 %copy-start.2 = (bf16[4,1024]{1,0:T(4,128)(2,1)S(1)}, bf16[4,1024]{1,0:T(4,128)(2,1)}, u32[]{:S(2)}) copy-start(bf16[4,1024]{1,0:T(4,128)(2,1)} %param.7) | copy-start | bytes 24580
  0.0 13.4 %copy-start.3 = (s32[128]{0:T(128)S(1)}, s32[128]{0:T(128)}, u32[]{:S(2)}) copy-start(s32[128]{0:T(128)} %param.5) | copy-start | bytes 1540
  4.6 11.6 %collective-permute-start = (bf16[1040,128]{1,0:T(8,128)(2,1)S(1)}, bf16[1040,128]{1,0:T(8,128)(2,1)S(1)}, u32[]{:S(2)}, u32[]{:S(2)}) collective-permute-start(bf16[1040,128]{1,0:T(8,128)(2,1)S(1)} %concatenate.22), channel_id=1, source_target_pairs={{0,4},{4,0},{1,5},{5,1},{2,6},{6,2},{3,7},{7,3},{8,12},{12,8},{9,1... | collective-permute-start | bytes 798728 | tf_op jit(solution)/shard_map/ppermute | solution.py:77
  17.3 33.6 %all-to-all-start = ((bf16[64,48,128]{2,1,0:T(8,128)(2,1)}), bf16[64,48,128]{2,1,0:T(8,128)(2,1)S(1)}, u32[]{:S(2)}, u32[]{:S(2)}) async-start(bf16[64,48,128]{2,1,0:T(8,128)(2,1)} %pad_maximum_fusion), calls=%async_computation | async-start | bytes 1572864 | tf_op jit(solution)/shard_map/all_to_all | solution.py:91
  51.6 19.9 %all-to-all-start.1 = ((bf16[64,16,128]{2,1,0:T(8,128)(2,1)}), bf16[64,16,128]{2,1,0:T(8,128)(2,1)S(1)}, u32[]{:S(2)}, u32[]{:S(2)}) async-start(bf16[64,16,128]{2,1,0:T(8,128)(2,1)} %broadcast_in_dim.34), calls=%async_computation.1 | async-start | bytes 524288 | tf_op jit(solution)/shard_map/all_to_all | solution.py:13
  59.9 18.7 %collective-permute-start.1 = (bf16[512,512]{1,0:T(8,128)(2,1)}, bf16[512,512]{1,0:T(8,128)(2,1)S(1)}, u32[]{:S(2)}, u32[]{:S(2)}) collective-permute-start(bf16[512,512]{1,0:T(8,128)(2,1)} %slice_bitcast_fusion), channel_id=1, source_target_pairs={{0,4},{4,0},{1,5},{5,1},{2,6},{6,2},{3,7},{7,3},{8,12},{12,8},{9,1... | collective-permute-start | bytes 1572872 | tf_op jit(solution)/shard_map/ppermute | solution.py:95
  72.6 5.4 %copy-start = (bf16[512,1024]{1,0:T(8,128)(2,1)S(1)}, bf16[512,1024]{1,0:T(8,128)(2,1)}, u32[]{:S(2)}) copy-start(bf16[512,1024]{1,0:T(8,128)(2,1)} %param.6) | copy-start | bytes 3145732
  72.6 15.3 %all-to-all-start.2 = ((bf16[4,1024,128]{2,1,0:T(8,128)(2,1)}), bf16[4,1024,128]{2,1,0:T(8,128)(2,1)S(1)}, u32[]{:S(2)}, u32[]{:S(2)}) async-start(bf16[4,1024,128]{2,1,0:T(8,128)(2,1)} %broadcast_in_dim.36), calls=%async_computation.2 | async-start | bytes 2097152 | tf_op jit(solution)/shard_map/all_to_all | solution.py:13
  88.0 9.1 %collective-permute-start.2 = (bf16[4,1024,128]{2,1,0:T(8,128)(2,1)S(1)}, bf16[4,1024,128]{2,1,0:T(8,128)(2,1)S(1)}, u32[]{:S(2)}, u32[]{:S(2)}) collective-permute-start(bf16[4,1024,128]{2,1,0:T(8,128)(2,1)S(1)} %all-to-all-done.2), channel_id=1, source_target_pairs={{0,4},{4,0},{1,5},{5,1},{2,6},{6,2},{3,7},{7,3},{8,12},{12,8},{9,1... | collective-permute-start | bytes 3145736 | tf_op jit(solution)/shard_map/ppermute | solution.py:99
  119.0 1.2 %copy-start.1 = (f32[512,512]{1,0:T(8,128)S(1)}, f32[512,512]{1,0:T(8,128)}, u32[]{:S(2)}) copy-start(f32[512,512]{1,0:T(8,128)} %param.9) | copy-start | bytes 3145732

commit v2 on v1

v2 whole, which is shorter than its diff:
```python
import math

import jax
import jax.numpy as jnp
from jax import lax
from jax.experimental import pallas as pl
from jax.experimental.pallas import tpu as pltpu
from jax.sharding import Mesh, PartitionSpec as P

LAYERS = 3
CORES = 2
LANES = 128
STEP = 128
WIDE = (0.4999999720071538, -0.06830646500676399, 0.028277340639243406, -0.01566003030791659,
        0.008837209300279753, -0.003820798788545866, 0.0008313362870811599)
NARROW = (0.4999769000530011, -0.06803611787881512, 0.026989768593852003, -0.012483028758839653,
          0.004564983607401579, -0.0008544733222650566)


def repeat_gather(piece, axis, count):
    return lax.all_to_all(jnp.broadcast_to(piece[None], (count,) + piece.shape), axis, 0, 0)


def split(values):
    high = values.astype(jnp.bfloat16)
    return high, (values - high.astype(jnp.float32)).astype(jnp.bfloat16)


def dot_t(left, right):
    return lax.dot_general(left, right, (((1,), (1,)), ((), ())), preferred_element_type=jnp.float32)


def root(x):
    return x * lax.rsqrt(jnp.maximum(x, 1e-30))


def arccos_over_pi(x, coefs):
    total = coefs[-1]
    for coef in coefs[-2::-1]:
        total = total * x + coef
    return root(1.0 - x) * total


def layers(rho):
    theta = rho
    for layer in range(LAYERS):
        if layer == 0:
            angle = arccos_over_pi(jnp.abs(rho), WIDE)
            zero_order = jnp.where(rho < 0.0, angle, 1.0 - angle)
        else:
            zero_order = 1.0 - arccos_over_pi(rho, WIDE if layer == 1 else NARROW)
        first_order = root((1.0 - rho) * (1.0 + rho)) * (1.0 / math.pi) + zero_order * rho
        theta = theta * zero_order + first_order
        rho = jnp.minimum(first_order, 1.0)
    return theta


def prep_body(at_ref, x_ref, inv_ref, kept_ref, sent_ref):
    size, half = x_ref.shape[0], x_ref.shape[1] // CORES
    rows = inv_ref.shape[0] // CORES
    core = at_ref[1]
    for out_ref, which in ((kept_ref, core), (sent_ref, 1 - core)):
        for i in range(half // LANES):
            at = pl.multiple_of(which * half + LANES * i, LANES)
            out_ref[size * i : size * (i + 1), :] = x_ref[:, pl.ds(at, LANES)]
        base = size * (half // LANES)
        for i in range(inv_ref.shape[1] // LANES):
            at = pl.multiple_of(which * rows, rows)
            high, low = split(inv_ref[pl.ds(at, rows), LANES * i : LANES * (i + 1)])
            out_ref[base + rows * i : base + rows * (i + 1), :] = high
            shift = base + rows * (inv_ref.shape[1] // LANES)
            out_ref[shift + rows * i : shift + rows * (i + 1), :] = low


def prep(at, centres_cols, diag_inverse, quarter):
    size, width = centres_cols.shape
    total = (quarter * width // CORES + 2 * quarter // CORES * size) // LANES
    out = jax.ShapeDtypeStruct((total, LANES), jnp.bfloat16)
    whole = pl.BlockSpec((total, LANES), lambda i, at: (0, 0))
    return pl.pallas_call(
        prep_body,
        grid_spec=pltpu.PrefetchScalarGridSpec(
            num_scalar_prefetch=1,
            grid=(1,),
            in_specs=[
                pl.BlockSpec((quarter, width), lambda i, at: (at[0], 0)),
                pl.BlockSpec((quarter, size), lambda i, at: (at[0], 0)),
            ],
            out_specs=[whole, whole],
        ),
        out_shape=[out, out],
        name="prep",
    )(at, centres_cols, diag_inverse)


def update_body(at_ref, cols_ref, rows_ref, mine_ref, other_ref, trailing_ref, out_ref,
                x_ref, high_ref, low_ref, left_ref, left_low_ref, right_ref, right_low_ref):
    size, width = cols_ref.shape
    half = width // CORES
    quarters = mine_ref.shape[0]
    quarter = size // quarters
    part = quarter // CORES
    groups, inv_groups = half // LANES, size // LANES
    core = at_ref[1]
    for k, (got, which) in enumerate(((mine_ref, core), (other_ref, 1 - core))):
        for q in range(quarters):
            for i in range(groups):
                at = pl.multiple_of(which * half + LANES * i, LANES)
                x_ref[quarter * q : quarter * (q + 1), pl.ds(at, LANES)] = got[q, quarter * i : quarter * (i + 1), :]
            to = (k * quarters + q) * part
            for n, inv_ref in enumerate((high_ref, low_ref)):
                for i in range(inv_groups):
                    base = quarter * groups + (n * inv_groups + i) * part
                    inv_ref[to : to + part, LANES * i : LANES * (i + 1)] = got[q, base : base + part, :]

    x = x_ref[...]
    wide = x.astype(jnp.float32)
    ones = jnp.ones((8, width), jnp.bfloat16)
    square, square_low = split(wide * wide)
    sums = dot_t(ones, square) + dot_t(ones, square_low)
    norm_x = jnp.sqrt(sums[:1] + 1e-06)
    inv_x = 1.0 / norm_x

    for from_ref, to_ref, to_low_ref in ((cols_ref, right_ref, right_low_ref), (rows_ref, left_ref, left_low_ref)):
        for s in range(0, size, STEP):
            block = from_ref[s : s + STEP, :]
            gram = dot_t(block, x_ref[...])
            block = block.astype(jnp.float32)
            norm = jnp.sqrt(jnp.sum(block * block, axis=1, keepdims=True) + 1e-06)
            cosine = jnp.clip(gram * (1.0 / norm) * inv_x, -1.0, 1.0)
            values, values_low = split(layers(cosine) * (norm * norm_x))
            solved = dot_t(values, high_ref[...]) + (dot_t(values, low_ref[...]) + dot_t(values_low, high_ref[...]))
            solved, solved_low = split(solved)
            to_ref[s : s + STEP, :] = solved
            to_low_ref[s : s + STEP, :] = solved_low

    later = at_ref[2] > 0
    for s in range(0, size, STEP):
        left, left_low = left_ref[s : s + STEP, :], left_low_ref[s : s + STEP, :]
        update = dot_t(left, right_ref[...]) + (dot_t(left, right_low_ref[...]) + dot_t(left_low, right_ref[...]))
        old = trailing_ref[s : s + STEP, :]
        out_ref[s : s + STEP, :] = jnp.where(later, old - update, old)


def update(at, cols, rows, mine, other, trailing):
    size, width = cols.shape
    square = pltpu.VMEM((size, size), jnp.bfloat16)
    vmem = pl.BlockSpec(memory_space=pltpu.VMEM)
    return pl.pallas_call(
        update_body,
        in_specs=[pl.BlockSpec(memory_space=pltpu.SMEM)] + [vmem] * 5,
        out_specs=vmem,
        out_shape=jax.ShapeDtypeStruct(trailing.shape, trailing.dtype),
        scratch_shapes=[pltpu.VMEM((size, width), jnp.bfloat16)] + [square] * 6,
        compiler_params=pltpu.CompilerParams(vmem_limit_bytes=32 * 2**20),
        name="update",
    )(at, cols, rows, mine, other, trailing)


def on_device(chips, row_count, panel, centres_cols, centres_rows, diag_inverse, trailing):
    size, width = centres_cols.shape
    blocks = panel.shape[0]
    target_rank = blocks // 4
    quarter = size // row_count
    panel_at = jnp.sum(jnp.where(panel == target_rank, jnp.arange(blocks, dtype=jnp.int32), 0))
    owner_chip, owner_core = panel_at // CORES, panel_at % CORES
    chip, core, row = lax.axis_index("chip"), lax.axis_index("core"), lax.axis_index("row")
    own_rank = lax.dynamic_index_in_dim(panel, chip * CORES + core, 0, keepdims=False)
    at = jnp.stack([row, core, (own_rank > target_rank).astype(jnp.int32)]).astype(jnp.int32)
    swap = [(0, 1), (1, 0)]

    rows = lax.all_gather(centres_rows, ("chip", "core"), axis=0, tiled=True)

    kept, sent = prep(at, centres_cols, diag_inverse, quarter)
    taken = jnp.where(core == owner_core, kept, lax.ppermute(sent, "core", swap))
    per_chip = taken.shape[0] // chips
    incoming = lax.all_to_all(taken.reshape(chips, per_chip, LANES), "chip", 0, 0)
    piece = lax.dynamic_index_in_dim(incoming, owner_chip, 0, keepdims=False)

    mine = repeat_gather(piece, "chip", chips).reshape(taken.shape)
    all_mine = repeat_gather(mine, "row", row_count)
    all_other = lax.ppermute(all_mine, "core", swap)
    return update(at, centres_cols, rows, all_mine, all_other, trailing)


def solution(mesh):
    col_count, row_count = mesh.devices.shape
    chips = col_count // CORES
    fine = Mesh(mesh.devices.reshape(chips, CORES, row_count), ("chip", "core", "row"))

    def step(*arrays):
        return on_device(chips, row_count, *arrays)

    col = ("chip", "core")
    return jax.shard_map(
        step,
        mesh=fine,
        in_specs=(P(), P(col, None), P(("row",) + col, None), P(col, None), P("row", col)),
        out_specs=P("row", col),
        check_vma=False,
    )
```

time: 122 us -> 168 us (1.38)
  waiting for transfers between devices: 39.4 us -> 75.8 us
  matrix products: 23.2 us -> 0 us
  Pallas kernels: 0 us -> 20.4 us
  blocking collectives: 0 us -> 15.9 us
  between operations: 3.81 us -> 16.9 us
  starting transfers between devices: 41.5 us -> 30.4 us
  local copies, waits for them, and re-layouts: 9.89 us -> 4.86 us
    all_gather x0 -> x1, waiting for transfers between devices: none -> 48.7 us  [on_device(): rows = lax.all_gather(centres_rows, ('chip', 'core'), axis=0, tiled=True)]
    dot_general x13 -> x0, matrix products: 23.2 us -> none  [dot_t(): lax.dot_general(left, right, (((1,), (1,)), ((), ())), preferred_element_...]
    pallas_call x0 -> x2, Pallas kernels: none -> 20.4 us  [the longest x1 17.9 us: update(): pl.pallas_call(update_body, in_specs=[pl.BlockSpec(memory_space=pltpu.SME...]
    all_to_all x0 -> x1, blocking collectives: none -> 15.9 us  [repeat_gather(): lax.all_to_all(jnp.broadcast_to(piece[None], (count,) + piece.shape), axi...]
    all_to_all x1, waiting for transfers between devices: 21.9 us -> 13.7 us  [on_device(): lax.all_to_all(taken.reshape(chips, per_chip, LANES), 'chip', 0, 0)]
    all_to_all x2 -> x1, starting transfers between devices: 11.5 us -> 4.62 us  [repeat_gather(): lax.all_to_all(jnp.broadcast_to(piece[None], (count,) + piece.shape), axi...]
    all_to_all x2 -> x1, waiting for transfers between devices: 17.5 us -> 12.6 us  [repeat_gather(): lax.all_to_all(jnp.broadcast_to(piece[None], (count,) + piece.shape), axi...]
    ppermute x2 -> x1, starting transfers between devices: 12.1 us -> 8.77 us  [on_device(): lax.ppermute(sent, 'core', swap)]
  transfers between devices with their start and end apart: 6 -> 5, of which waited for: 3 -> 3; matrix products, arithmetic and copies ran while one was open for 5% -> 1% of each run, Pallas kernels for 0% -> 0%
where the time goes in v2:
time: 168 us; the launch traced here: 167 us
  waiting for transfers between devices  75.8 us (45%)
  starting transfers between devices  30.4 us (18%)
  Pallas kernels  20.4 us (12%)
  between operations  16.9 us (10%)
  blocking collectives  15.9 us (9%)
  local copies, waits for them, and re-layouts  4.86 us (3%)
  other arithmetic  3.06 us (2%)
    all_gather x1, waiting for transfers between devices, on_device(): rows = lax.all_gather(centres_rows, ('chip', 'core'), axis=0, tiled=True)  48.7 us
    pallas_call x1, Pallas kernels, update(): pl.pallas_call(update_body, in_specs=[pl.BlockSpec(memory_space=pltpu.SME...  17.9 us
    all_to_all x1, blocking collectives, repeat_gather(): lax.all_to_all(jnp.broadcast_to(piece[None], (count,) + piece.shape), axi...  15.9 us
    all_to_all x1, waiting for transfers between devices, on_device(): lax.all_to_all(taken.reshape(chips, per_chip, LANES), 'chip', 0, 0)  13.7 us
    all_to_all x1, waiting for transfers between devices, repeat_gather(): lax.all_to_all(jnp.broadcast_to(piece[None], (count,) + piece.shape), axi...  12.6 us
    all_to_all x1, starting transfers between devices, on_device(): lax.all_to_all(taken.reshape(chips, per_chip, LANES), 'chip', 0, 0)  10.9 us
    ppermute x1, starting transfers between devices, on_device(): lax.ppermute(sent, 'core', swap)  8.77 us
    ppermute x1, starting transfers between devices, on_device(): all_other = lax.ppermute(all_mine, 'core', swap)  6.03 us
  transfers between devices with their start and end apart: 5, of which 3 were waited for; matrix products, arithmetic and copies ran while one was open for 1% of the time, Pallas kernels for 0%

profile of v2, /device:TPU:1, one launch (start us, length us, event | category | flops | bytes accessed | tf_op | source)
XLA Modules:
  0.0 167.3 jit_solution(11525261318978523435)
XLA Ops:
  6.5 0.0 copy-start.3
  6.5 0.7 copy-done.3
  7.2 0.6 dynamic_slice.8
  8.4 0.7 pad_add_fusion.at_ref
  9.1 2.6 %prep.1 = (bf16[1024,128]{1,0:T(8,128)(2,1)}, bf16[1024,128]{1,0:T(8,128)(2,1)}) custom-call(s32[3]{0:T(128)} %pad_add_fusion.at_ref, bf16[512,1024]{1,0:T(8,128)(2,1)} %cols_ref.1, f32[512,512]{1,0:T(8,128)} %inv_ref.1), custom_call_target="tpu_custom_call" | custom-call | tf_op jit(solution)/shard_map/prep/pallas_call | solution.py:80
  11.7 8.8 %collective-permute-start = (bf16[1024,128]{1,0:T(8,128)(2,1)}, bf16[1024,128]{1,0:T(8,128)(2,1)S(1)}, u32[]{:S(2)}, u32[]{:S(2)}) collective-permute-start(bf16[1024,128]{1,0:T(8,128)(2,1)} %get-tuple-element.8), channel_id=1, source_target_pairs={{0,4},{4,0},{1,5},{5,1},{2,6},{6,2},{3,7},{7,3},{8,12},{12,8},{9,1... | collective-permute-start | bytes 786440 | tf_op jit(solution)/shard_map/ppermute | solution.py:175
  20.4 0.7 fusion
  23.2 0.0 collective-permute-done
  23.2 1.7 %broadcast_select_fusion = bf16[1024,128]{1,0:T(8,128)(2,1)} fusion(bf16[1024,128]{1,0:T(8,128)(2,1)} %get-tuple-element.7, bf16[1024,128]{1,0:T(8,128)(2,1)S(1)} %collective-permute-done, pred[]{:T(512)S(6)} %eq.13), kind=kLoop, calls=%fused_computation | loop fusion | flops 131072 | bytes 786433 | tf_op jit(solution)/shard_map/jit(_where)/select_n | solution.py:175
  24.9 10.9 %all-to-all-start = ((bf16[64,16,128]{2,1,0:T(8,128)(2,1)}), bf16[64,16,128]{2,1,0:T(8,128)(2,1)S(1)}, u32[]{:S(2)}, u32[]{:S(2)}) async-start(bf16[64,16,128]{2,1,0:T(8,128)(2,1)} %bitcast.3), calls=%async_computation | async-start | bytes 524288 | tf_op jit(solution)/shard_map/all_to_all | solution.py:177
  36.6 13.7 %all-to-all-done = bf16[64,16,128]{2,1,0:T(8,128)(2,1)S(1)} async-done(((bf16[64,16,128]{2,1,0:T(8,128)(2,1)}), bf16[64,16,128]{2,1,0:T(8,128)(2,1)S(1)}, u32[]{:S(2)}, u32[]{:S(2)}) %all-to-all-start) | async-done | bytes 262176 | tf_op jit(solution)/shard_map/all_to_all | solution.py:177
  50.3 0.7 broadcast_in_dim.21
  51.0 4.6 %all-to-all-start.1 = ((bf16[64,16,128]{2,1,0:T(8,128)(2,1)}), bf16[64,16,128]{2,1,0:T(8,128)(2,1)S(1)}, u32[]{:S(2)}, u32[]{:S(2)}) async-start(bf16[64,16,128]{2,1,0:T(8,128)(2,1)} %broadcast_in_dim.21), calls=%async_computation.1 | async-start | bytes 524288 | tf_op jit(solution)/shard_map/all_to_all | solution.py:21
  55.7 0.0 all-gather.3.cloned.1.call-start
  55.7 0.7 all-gather.3.cloned.1.call-update
  56.4 12.6 %all-to-all-done.1 = bf16[64,16,128]{2,1,0:T(8,128)(2,1)S(1)} async-done(((bf16[64,16,128]{2,1,0:T(8,128)(2,1)}), bf16[64,16,128]{2,1,0:T(8,128)(2,1)S(1)}, u32[]{:S(2)}, u32[]{:S(2)}) %all-to-all-start.1) | async-done | bytes 262176 | tf_op jit(solution)/shard_map/all_to_all | solution.py:21
  69.1 0.1 broadcast_in_dim.23
  69.2 15.9 %all_to_all.15.mine_ref = bf16[4,1024,128]{2,1,0:T(8,128)(2,1)S(1)} all-to-all(bf16[4,1024,128]{2,1,0:T(8,128)(2,1)S(1)} %broadcast_in_dim.23), channel_id=1, replica_groups=mesh['chip'=64,'core'=2,'row'=4] {'row'}, dimensions={0} | all-to-all | bytes 2097152 | tf_op jit(solution)/shard_map/all_to_all | solution.py:21
  85.1 0.0 copy-start
  85.1 0.0 copy-start.2
  85.1 6.0 %collective-permute-start.1 = (bf16[4,1024,128]{2,1,0:T(8,128)(2,1)S(1)}, bf16[4,1024,128]{2,1,0:T(8,128)(2,1)}, u32[]{:S(2)}, u32[]{:S(2)}) collective-permute-start(bf16[4,1024,128]{2,1,0:T(8,128)(2,1)S(1)} %all_to_all.15.mine_ref), channel_id=1, source_target_pairs={{0,4},{4,0},{1,5},{5,1},{2,6},{6,2},{3,7},{7,3},{8,12},{12,8},{9,1... | collective-permute-start | bytes 3145736 | tf_op jit(solution)/shard_map/ppermute | solution.py:182
  91.1 48.7 %all-gather.3.cloned.1.call-done = bf16[128,4,1024]{2,1,0:T(4,128)(2,1)} async-done(((bf16[1,4,1024]{2,1,0:T(4,128)(2,1)}), bf16[128,4,1024]{2,1,0:T(4,128)(2,1)}) %all-gather.3.cloned.1.call-update) | async-done | bytes 1048592 | tf_op jit(solution)/shard_map/all_gather | solution.py:172
  139.8 1.5 reshape.10.rows_ref
  141.4 0.0 collective-permute-done.1.other_ref
  141.4 0.0 copy-done
  141.4 0.0 copy-done.2
  141.4 0.0 copy-start.1
  141.4 1.2 copy-done.1
  142.6 17.9 %update.1 = f32[512,512]{1,0:T(8,128)} custom-call(s32[3]{0:T(128)S(1)} %copy-done.2, bf16[512,1024]{1,0:T(8,128)(2,1)S(1)} %copy-done, bf16[512,1024]{1,0:T(8,128)(2,1)S(1)} %reshape.10.rows_ref, bf16[4,1024,128]{2,1,0:T(8,128)(2,1)S(1)} %all_to_all.15.mine_ref, bf16[4,1024,128]{2,1,0:T(8,128)(2,1)} %collective-permute-done.1.other_ref, ...), custom_call_target="tpu_custom_call" | custom-call | tf_op jit(solution)/shard_map/update/pallas_call | solution.py:149
  (1 shorter events, 0.0 us)
Async XLA Ops:
  6.5 0.7 copy-start.3
  11.7 11.6 %collective-permute-start = (bf16[1024,128]{1,0:T(8,128)(2,1)}, bf16[1024,128]{1,0:T(8,128)(2,1)S(1)}, u32[]{:S(2)}, u32[]{:S(2)}) collective-permute-start(bf16[1024,128]{1,0:T(8,128)(2,1)} %get-tuple-element.8), channel_id=1, source_target_pairs={{0,4},{4,0},{1,5},{5,1},{2,6},{6,2},{3,7},{7,3},{8,12},{12,8},{9,1... | collective-permute-start | bytes 786440 | tf_op jit(solution)/shard_map/ppermute | solution.py:175
  24.9 25.4 %all-to-all-start = ((bf16[64,16,128]{2,1,0:T(8,128)(2,1)}), bf16[64,16,128]{2,1,0:T(8,128)(2,1)S(1)}, u32[]{:S(2)}, u32[]{:S(2)}) async-start(bf16[64,16,128]{2,1,0:T(8,128)(2,1)} %bitcast.3), calls=%async_computation | async-start | bytes 524288 | tf_op jit(solution)/shard_map/all_to_all | solution.py:177
  51.0 18.0 %all-to-all-start.1 = ((bf16[64,16,128]{2,1,0:T(8,128)(2,1)}), bf16[64,16,128]{2,1,0:T(8,128)(2,1)S(1)}, u32[]{:S(2)}, u32[]{:S(2)}) async-start(bf16[64,16,128]{2,1,0:T(8,128)(2,1)} %broadcast_in_dim.21), calls=%async_computation.1 | async-start | bytes 524288 | tf_op jit(solution)/shard_map/all_to_all | solution.py:21
  55.7 84.2 %all-gather.3.cloned.1.call-start = ((), (), s32[]{:S(2)}) async-start(), calls=%async_computation.3 | async-start | bytes 1056768 | tf_op jit(solution)/shard_map/all_gather | solution.py:172
  85.1 56.3 %copy-start = (bf16[512,1024]{1,0:T(8,128)(2,1)S(1)}, bf16[512,1024]{1,0:T(8,128)(2,1)}, u32[]{:S(2)}) copy-start(bf16[512,1024]{1,0:T(8,128)(2,1)} %cols_ref.1) | copy-start | bytes 3145732
  85.1 56.3 %copy-start.2 = (s32[3]{0:T(128)S(1)}, s32[3]{0:T(128)}, u32[]{:S(2)}) copy-start(s32[3]{0:T(128)} %pad_add_fusion.at_ref) | copy-start | bytes 40
  85.1 56.3 %collective-permute-start.1 = (bf16[4,1024,128]{2,1,0:T(8,128)(2,1)S(1)}, bf16[4,1024,128]{2,1,0:T(8,128)(2,1)}, u32[]{:S(2)}, u32[]{:S(2)}) collective-permute-start(bf16[4,1024,128]{2,1,0:T(8,128)(2,1)S(1)} %all_to_all.15.mine_ref), channel_id=1, source_target_pairs={{0,4},{4,0},{1,5},{5,1},{2,6},{6,2},{3,7},{7,3},{8,12},{12,8},{9,1... | collective-permute-start | bytes 3145736 | tf_op jit(solution)/shard_map/ppermute | solution.py:182
  141.4 1.2 copy-start.1
Sparse Core Ops, SparseCore 0:
  59.5 80.2 all-gather.2

commit v3 on v2

v3 whole, which is shorter than its diff:
```python
import math

import jax
import jax.numpy as jnp
from jax import lax
from jax.experimental import pallas as pl
from jax.experimental.pallas import tpu as pltpu
from jax.sharding import Mesh, PartitionSpec as P

LAYERS = 3
CORES = 2
LANES = 128
STEP = 64
WIDE = (0.4999999720071538, -0.06830646500676399, 0.028277340639243406, -0.01566003030791659,
        0.008837209300279753, -0.003820798788545866, 0.0008313362870811599)
NARROW = (0.4999769000530011, -0.06803611787881512, 0.026989768593852003, -0.012483028758839653,
          0.004564983607401579, -0.0008544733222650566)


def repeat_gather(piece, axis, count):
    return lax.all_to_all(jnp.broadcast_to(piece[None], (count,) + piece.shape), axis, 0, 0)


def split(values):
    high = values.astype(jnp.bfloat16)
    return high, (values - high.astype(jnp.float32)).astype(jnp.bfloat16)


def dot_t(left, right):
    return lax.dot_general(left, right, (((1,), (1,)), ((), ())), preferred_element_type=jnp.float32)


def poly(x, coefs):
    total = coefs[-1]
    for coef in coefs[-2::-1]:
        total = total * x + coef
    return total


def layers(rho):
    theta = rho
    for layer in range(LAYERS):
        size = jnp.abs(rho) if layer == 0 else rho
        rest = jnp.maximum(1.0 - size, 1e-30)
        below = rest * lax.rsqrt(rest)
        above = 1.0 + size
        above = above * lax.rsqrt(above) * (1.0 / math.pi)
        angle = below * poly(size, NARROW if layer == 2 else WIDE)
        zero_order = 1.0 - angle
        if layer == 0:
            zero_order = jnp.where(rho < 0.0, angle, zero_order)
        rho_next = below * above + zero_order * rho
        theta = theta * zero_order + rho_next
        rho = rho_next
    return theta


def prep_body(x_hbm, inv_hbm, rows_ref, kept_ref, sent_ref, x_ref, inv_ref, sems):
    row, core = lax.axis_index("row"), lax.axis_index("core")
    size, width = x_ref.shape
    take = pl.ds(pl.multiple_of(row * size, size), size)
    copy_x = pltpu.make_async_copy(x_hbm.at[take, :], x_ref, sems.at[0])
    copy_inv = pltpu.make_async_copy(inv_hbm.at[take, :], inv_ref, sems.at[1])
    copy_x.start()
    copy_inv.start()
    half, groups = width // CORES, inv_ref.shape[1] // LANES
    rows = size // CORES
    base = size * (half // LANES)
    end = base + 2 * rows * groups
    count = rows_ref.shape[0]
    for out_ref in (kept_ref, sent_ref):
        out_ref[end:, :] = jnp.zeros((kept_ref.shape[0] - end, LANES), jnp.bfloat16)
        for which in range(CORES):

            @pl.when(core == which)
            def _():
                for i in range(width // LANES):
                    to = end + CORES * count * i + count * which
                    out_ref[to : to + count, :] = rows_ref[:, LANES * i : LANES * (i + 1)]

    copy_x.wait()
    for out_ref, which in ((kept_ref, core), (sent_ref, 1 - core)):
        for i in range(half // LANES):
            at = pl.multiple_of(which * half + LANES * i, LANES)
            out_ref[size * i : size * (i + 1), :] = x_ref[:, pl.ds(at, LANES)]
    copy_inv.wait()
    for out_ref, which in ((kept_ref, core), (sent_ref, 1 - core)):
        for i in range(groups):
            at = pl.multiple_of(which * rows, rows)
            high, low = split(inv_ref[pl.ds(at, rows), LANES * i : LANES * (i + 1)])
            out_ref[base + rows * i : base + rows * (i + 1), :] = high
            shift = base + rows * groups
            out_ref[shift + rows * i : shift + rows * (i + 1), :] = low


VMEM = pl.BlockSpec(memory_space=pltpu.VMEM)
SMEM = pl.BlockSpec(memory_space=pltpu.SMEM)
ANY = pl.BlockSpec(memory_space=pl.ANY)


def prep(centres_cols, diag_inverse, centres_rows, quarter):
    size, width = centres_cols.shape
    total = (quarter * width // CORES + 2 * quarter // CORES * size + CORES * centres_rows.size) // LANES
    out = jax.ShapeDtypeStruct((total, LANES), jnp.bfloat16)
    return pl.pallas_call(
        prep_body,
        in_specs=[ANY, ANY, VMEM],
        out_specs=[VMEM, VMEM],
        out_shape=[out, out],
        scratch_shapes=[
            pltpu.VMEM((quarter, width), jnp.bfloat16),
            pltpu.VMEM((quarter, size), jnp.float32),
            pltpu.SemaphoreType.DMA((2,)),
        ],
        name="prep",
    )(centres_cols, diag_inverse, centres_rows)


def first_body(at_ref, kept_ref, got_ref, out_ref, later_ref):
    chips, length, _ = out_ref.shape
    per_chip = length // 2
    total = chips * per_chip
    kept = at_ref[3] > 0
    out_ref[:, :per_chip, :] = jnp.where(kept, kept_ref[:total], got_ref[:total]).reshape(chips, per_chip, LANES)
    for n in range(2):
        at = pl.ds(pl.multiple_of(total + (2 * at_ref[1] + n) * per_chip, per_chip), per_chip)
        rows = (kept_ref[at, :].astype(jnp.float32) + got_ref[at, :].astype(jnp.float32)).astype(jnp.bfloat16)
        if n == 0:
            out_ref[:, per_chip:, :] = jnp.broadcast_to(rows[None], (chips, per_chip, LANES))
        else:
            later_ref[...] = rows


def first_operand(at, kept, got, chips, per_chip):
    return pl.pallas_call(
        first_body,
        in_specs=[SMEM, VMEM, VMEM],
        out_specs=[VMEM, VMEM],
        out_shape=[
            jax.ShapeDtypeStruct((chips, 2 * per_chip, LANES), jnp.bfloat16),
            jax.ShapeDtypeStruct((per_chip, LANES), jnp.bfloat16),
        ],
        name="first_operand",
    )(at, kept, got)


def second_body(at_ref, came_ref, rows_ref, out_ref):
    chips, length, _ = out_ref.shape
    per_chip = length // 2
    piece = came_ref[at_ref[4], :per_chip, :]
    out_ref[:, :per_chip, :] = jnp.broadcast_to(piece[None], (chips, per_chip, LANES))
    out_ref[:, per_chip:, :] = jnp.broadcast_to(rows_ref[...][None], (chips, per_chip, LANES))


def second_operand(at, came, rows):
    return pl.pallas_call(
        second_body,
        in_specs=[SMEM, VMEM, VMEM],
        out_specs=VMEM,
        out_shape=jax.ShapeDtypeStruct(came.shape, came.dtype),
        name="second_operand",
    )(at, came, rows)


def third_body(came_ref, out_ref):
    per_chip = came_ref.shape[1] // 2
    piece = came_ref[:, :per_chip, :].reshape(out_ref.shape[1:])
    for q in range(out_ref.shape[0]):
        out_ref[q] = piece


def third_operand(came, row_count):
    chips, length, _ = came.shape
    return pl.pallas_call(
        third_body,
        in_specs=[VMEM],
        out_specs=VMEM,
        out_shape=jax.ShapeDtypeStruct((row_count, chips * length // 2, LANES), came.dtype),
        name="third_operand",
    )(came)


def update_body(at_ref, cols_ref, col_norm_ref, rows_own_ref, rows_other_ref, row_norm_ref, mine_ref, other_ref, trailing_ref, out_ref,
                x_ref, high_ref, low_ref, left_ref, left_low_ref, right_ref, right_low_ref,
                rows_ref, k_ref, k_low_ref, gram_ref, norm_ref, inv_ref):
    size, width = cols_ref.shape
    half = width // CORES
    quarters = mine_ref.shape[0]
    quarter = size // quarters
    part = quarter // CORES
    groups, inv_groups = half // LANES, size // LANES
    core = at_ref[1]
    for k, (got, which) in enumerate(((mine_ref, core), (other_ref, 1 - core))):
        for q in range(quarters):
            for i in range(groups):
                at = pl.multiple_of(which * half + LANES * i, LANES)
                x_ref[quarter * q : quarter * (q + 1), pl.ds(at, LANES)] = got[q, quarter * i : quarter * (i + 1), :]
            to = (k * quarters + q) * part
            for n, part_ref in enumerate((high_ref, low_ref)):
                for i in range(inv_groups):
                    base = quarter * groups + (n * inv_groups + i) * part
                    part_ref[to : to + part, LANES * i : LANES * (i + 1)] = got[q, base : base + part, :]

    for got, which in ((rows_own_ref, core), (rows_other_ref, 1 - core)):
        rows_ref[:, pl.ds(pl.multiple_of(which * half, half), half)] = got[...]

    wide = x_ref[...].astype(jnp.float32)
    norm_x = jnp.sqrt(jnp.sum(wide * wide, axis=1, keepdims=True) + 1e-06)
    norm_x = jnp.broadcast_to(norm_x, (size, LANES)).T[:STEP]
    norm_ref[...] = norm_x
    inv_ref[...] = 1.0 / norm_x

    for from_ref, from_norm_ref, to_ref, to_low_ref in (
        (cols_ref, col_norm_ref, right_ref, right_low_ref),
        (rows_ref, row_norm_ref, left_ref, left_low_ref),
    ):
        gram_ref[...] = dot_t(from_ref[...], x_ref[...])

        @pl.loop(0, size // STEP)
        def _(i):
            at = pl.ds(pl.multiple_of(i * STEP, STEP), STEP)
            norm = jnp.concatenate([from_norm_ref[at, :]] * (size // LANES), axis=1)
            cosine = gram_ref[at, :] * (1.0 / norm) * inv_ref[...]
            values = layers(jnp.clip(cosine, -1.0, 1.0)) * (norm * norm_ref[...])
            values, values_low = split(values)
            k_ref[at, :] = values
            k_low_ref[at, :] = values_low

        solved = dot_t(k_ref[...], high_ref[...]) + (dot_t(k_ref[...], low_ref[...]) + dot_t(k_low_ref[...], high_ref[...]))
        solved, solved_low = split(solved)
        to_ref[...] = solved
        to_low_ref[...] = solved_low

    update = dot_t(left_ref[...], right_ref[...]) + (dot_t(left_ref[...], right_low_ref[...]) + dot_t(left_low_ref[...], right_ref[...]))
    old = trailing_ref[...]
    out_ref[...] = jnp.where(at_ref[2] > 0, old - update, old)


def norms(*pieces):
    total = 1e-06
    for piece in pieces:
        wide = piece.astype(jnp.float32)
        total += jnp.sum(wide * wide, axis=1, keepdims=True)
    return jnp.broadcast_to(jnp.sqrt(total), (pieces[0].shape[0], LANES))


def update(at, cols, rows_own, rows_other, mine, other, trailing):
    size, width = cols.shape
    square = pltpu.VMEM((size, size), jnp.bfloat16)
    vectors = pltpu.VMEM((size, width), jnp.bfloat16)
    return pl.pallas_call(
        update_body,
        in_specs=[SMEM] + [VMEM] * 8,
        out_specs=VMEM,
        out_shape=jax.ShapeDtypeStruct(trailing.shape, trailing.dtype),
        scratch_shapes=[vectors]
        + [square] * 6
        + [vectors]
        + [square] * 2
        + [pltpu.VMEM((size, size), jnp.float32)]
        + [pltpu.VMEM((STEP, size), jnp.float32)] * 2,
        compiler_params=pltpu.CompilerParams(vmem_limit_bytes=32 * 2**20),
        name="update",
    )(at, cols, norms(cols), rows_own, rows_other, norms(rows_own, rows_other), mine, other, trailing)


def on_device(chips, row_count, panel, centres_cols, centres_rows, diag_inverse, trailing):
    size, width = centres_cols.shape
    blocks = panel.shape[0]
    target_rank = blocks // 4
    quarter = size // row_count
    panel_at = jnp.sum(jnp.where(panel == target_rank, jnp.arange(blocks, dtype=jnp.int32), 0))
    owner_chip, owner_core = panel_at // CORES, panel_at % CORES
    chip, core, row = lax.axis_index("chip"), lax.axis_index("core"), lax.axis_index("row")
    own_rank = lax.dynamic_index_in_dim(panel, chip * CORES + core, 0, keepdims=False)
    flags = [row, core, own_rank > target_rank, core == owner_core, owner_chip]
    at = jnp.stack([flag.astype(jnp.int32) for flag in flags])
    swap = [(0, 1), (1, 0)]

    kept, sent = prep(centres_cols, diag_inverse, centres_rows, quarter)
    got = lax.ppermute(sent, "core", swap)
    per_chip = (2 * width * quarter // CORES) // (LANES * chips)
    outgoing, rows_later = first_operand(at, kept, got, chips, per_chip)
    first = lax.all_to_all(outgoing, "chip", 0, 0)
    second = lax.all_to_all(second_operand(at, first, rows_later), "chip", 0, 0)
    all_mine = lax.all_to_all(third_operand(second, row_count), "row", 0, 0)

    tiles = [got_rows[:, i : i + 8] for got_rows in (first, second) for i in range(per_chip, 2 * per_chip, 8)]
    rows_own = jnp.concatenate([tile.reshape(size, LANES) for tile in tiles], axis=1)
    rows_other = lax.ppermute(rows_own, "core", swap)
    all_other = lax.ppermute(all_mine, "core", swap)
    return update(at, centres_cols, rows_own, rows_other, all_mine, all_other, trailing)


def solution(mesh):
    col_count, row_count = mesh.devices.shape
    chips = col_count // CORES
    fine = Mesh(mesh.devices.reshape(chips, CORES, row_count), ("chip", "core", "row"))

    def step(*arrays):
        return on_device(chips, row_count, *arrays)

    col = ("chip", "core")
    return jax.shard_map(
        step,
        mesh=fine,
        in_specs=(P(), P(col, None), P(("row",) + col, None), P(col, None), P("row", col)),
        out_specs=P("row", col),
        check_vma=False,
    )
```

time: 168 us -> 115 us (0.68)
  waiting for transfers between devices: 75.8 us -> 12.2 us
  blocking collectives: 15.9 us -> 52.2 us
  between operations: 16.9 us -> 3.4 us
  starting transfers between devices: 30.4 us -> 22.3 us
  local copies, waits for them, and re-layouts: 4.86 us -> 2.35 us
  other arithmetic: 3.06 us -> 1.33 us
    all_gather x1 -> x0, waiting for transfers between devices: 48.7 us -> none  [on_device(): rows = lax.all_gather(centres_rows, ('chip', 'core'), axis=0, tiled=True)]
    all_to_all x1 -> x2, blocking collectives: 15.9 us -> 52.2 us  [the longest x1 29 us: on_device(): first = lax.all_to_all(outgoing, 'chip', 0, 0)]
    all_to_all x2 -> x1, waiting for transfers between devices: 26.4 us -> 10.6 us  [on_device(): all_mine = lax.all_to_all(third_operand(second, row_count), 'row', 0, 0)]
    all_to_all x2 -> x1, starting transfers between devices: 15.6 us -> 4.14 us  [on_device(): all_mine = lax.all_to_all(third_operand(second, row_count), 'row', 0, 0)]
    unnamed x9 -> x14, local copies, waits for them, and re-layouts: 3.4 us -> 0.73 us
    ppermute x1 -> x2, starting transfers between devices: 8.77 us -> 10.8 us  [the longest x1 8.79 us: on_device(): got = lax.ppermute(sent, 'core', swap)]
    select_n x1 -> x0, other arithmetic: 1.69 us -> none  [on_device(): jnp.where(core == owner_core, kept, lax.ppermute(sent, 'core', swap))]
    pallas_call x2 -> x5, Pallas kernels: 20.4 us -> 21.1 us  [the longest x1 12.5 us: update(): pl.pallas_call(update_body, in_specs=[SMEM] + [VMEM] * 8, out_specs=VMEM,...]
  transfers between devices with their start and end apart: 5 -> 4, of which waited for: 3 -> 2; matrix products, arithmetic and copies ran while one was open for 1% -> 2% of each run, Pallas kernels for 0% -> 0%
where the time goes in v3:
time: 115 us
  blocking collectives  52.2 us (45%)
  starting transfers between devices  22.3 us (19%)
  Pallas kernels  21.1 us (18%)
  waiting for transfers between devices  12.2 us (11%)
  between operations  3.4 us (3%)
  local copies, waits for them, and re-layouts  2.35 us (2%)
  other arithmetic  1.33 us (1%)
    all_to_all x1, blocking collectives, on_device(): first = lax.all_to_all(outgoing, 'chip', 0, 0)  29 us
    all_to_all x1, blocking collectives, on_device(): second = lax.all_to_all(second_operand(at, first, rows_later), 'chip', 0, 0)  23.2 us
    pallas_call x1, Pallas kernels, update(): pl.pallas_call(update_body, in_specs=[SMEM] + [VMEM] * 8, out_specs=VMEM,...  12.5 us
    all_to_all x1, waiting for transfers between devices, on_device(): all_mine = lax.all_to_all(third_operand(second, row_count), 'row', 0, 0)  10.6 us
    ppermute x1, starting transfers between devices, on_device(): got = lax.ppermute(sent, 'core', swap)  8.79 us
    ppermute x1, starting transfers between devices, on_device(): all_other = lax.ppermute(all_mine, 'core', swap)  7.29 us
    all_to_all x1, starting transfers between devices, on_device(): all_mine = lax.all_to_all(third_operand(second, row_count), 'row', 0, 0)  4.14 us
    pallas_call x1, Pallas kernels, prep(): pl.pallas_call(prep_body, in_specs=[ANY, ANY, VMEM], out_specs=[VMEM, VME...  2.57 us
  transfers between devices with their start and end apart: 4, of which 2 were waited for; matrix products, arithmetic and copies ran while one was open for 2% of the time, Pallas kernels for 0%

profile of v3, /device:TPU:1, one launch (start us, length us, event | category | flops | bytes accessed | tf_op | source)
XLA Modules:
  0.0 114.8 jit_solution(3003028637294335374)
XLA Ops:
  0.0 0.0 copy-start.6
  0.0 2.6 %prep.1 = (bf16[1088,128]{1,0:T(8,128)(2,1)}, bf16[1088,128]{1,0:T(8,128)(2,1)}) custom-call(bf16[512,1024]{1,0:T(8,128)(2,1)} %cols_ref.1, f32[512,512]{1,0:T(8,128)} %inv_hbm.1, bf16[4,1024]{1,0:T(4,128)(2,1)} %rows_ref.1), custom_call_target="tpu_custom_call" | custom-call | tf_op jit(solution)/shard_map/prep/pallas_call | solution.py:105
  2.6 8.8 %collective-permute-start = (bf16[1088,128]{1,0:T(8,128)(2,1)}, bf16[1088,128]{1,0:T(8,128)(2,1)S(1)}, u32[]{:S(2)}, u32[]{:S(2)}) collective-permute-start(bf16[1088,128]{1,0:T(8,128)(2,1)} %get-tuple-element.10), channel_id=1, source_target_pairs={{0,4},{4,0},{1,5},{5,1},{2,6},{6,2},{3,7},{7,3},{8,12},{12,8},{9,1... | collective-permute-start | bytes 835592 | tf_op jit(solution)/shard_map/ppermute | solution.py:281
  11.4 0.0 copy-done.6
  11.4 0.7 fusion
  14.6 0.7 dynamic_slice.4
  16.0 0.7 stack.24.at_ref
  16.6 0.0 collective-permute-done.got_ref
  16.7 0.0 copy-start.5
  16.7 0.7 copy-done.5
  17.4 1.9 %first_operand.1 = (bf16[64,32,128]{2,1,0:T(8,128)(2,1)}, bf16[16,128]{1,0:T(8,128)(2,1)}) custom-call(s32[5]{0:T(128)} %stack.24.at_ref, bf16[1088,128]{1,0:T(8,128)(2,1)} %get-tuple-element.9.kept_ref, bf16[1088,128]{1,0:T(8,128)(2,1)} %copy-done.5), custom_call_target="tpu_custom_call" | custom-call | tf_op jit(solution)/shard_map/first_operand/pallas_call | solution.py:135
  19.3 29.0 %all_to_all.15.came_ref = bf16[64,32,128]{2,1,0:T(8,128)(2,1)} all-to-all(bf16[64,32,128]{2,1,0:T(8,128)(2,1)} %get-tuple-element.11), channel_id=1, replica_groups=mesh['chip'=64,'core'=2,'row'=4] {'chip'}, dimensions={0} | all-to-all | bytes 1048576 | tf_op jit(solution)/shard_map/all_to_all | solution.py:284
  48.3 1.9 %second_operand.1 = bf16[64,32,128]{2,1,0:T(8,128)(2,1)} custom-call(s32[5]{0:T(128)} %stack.24.at_ref, bf16[64,32,128]{2,1,0:T(8,128)(2,1)} %all_to_all.15.came_ref, bf16[16,128]{1,0:T(8,128)(2,1)} %get-tuple-element.12.rows_ref), custom_call_target="tpu_custom_call" | custom-call | tf_op jit(solution)/shard_map/second_operand/pallas_call | solution.py:156
  50.2 23.2 %all_to_all.16.came_ref = bf16[64,32,128]{2,1,0:T(8,128)(2,1)} all-to-all(bf16[64,32,128]{2,1,0:T(8,128)(2,1)} %second_operand.1), channel_id=1, replica_groups=mesh['chip'=64,'core'=2,'row'=4] {'chip'}, dimensions={0} | all-to-all | bytes 1048576 | tf_op jit(solution)/shard_map/all_to_all | solution.py:285
  73.4 2.1 %third_operand.1 = bf16[4,1024,128]{2,1,0:T(8,128)(2,1)} custom-call(bf16[64,32,128]{2,1,0:T(8,128)(2,1)} %all_to_all.16.came_ref), custom_call_target="tpu_custom_call" | custom-call | tf_op jit(solution)/shard_map/third_operand/pallas_call | solution.py:174
  75.5 0.0 copy-start.4
  75.5 0.0 copy-start.3
  75.5 4.1 %all-to-all-start.2 = ((bf16[4,1024,128]{2,1,0:T(8,128)(2,1)}), bf16[4,1024,128]{2,1,0:T(8,128)(2,1)S(1)}, u32[]{:S(2)}, u32[]{:S(2)}) async-start(bf16[4,1024,128]{2,1,0:T(8,128)(2,1)} %third_operand.1), calls=%async_computation.2 | async-start | bytes 2097152 | tf_op jit(solution)/shard_map/all_to_all | solution.py:286
  79.7 0.0 copy-done.4
  79.7 0.0 copy-start
  79.7 10.6 %all-to-all-done.2.mine_ref = bf16[4,1024,128]{2,1,0:T(8,128)(2,1)S(1)} async-done(((bf16[4,1024,128]{2,1,0:T(8,128)(2,1)}), bf16[4,1024,128]{2,1,0:T(8,128)(2,1)S(1)}, u32[]{:S(2)}, u32[]{:S(2)}) %all-to-all-start.2) | async-done | bytes 1048608 | tf_op jit(solution)/shard_map/all_to_all | solution.py:286
  90.3 7.3 %collective-permute-start.2 = (bf16[4,1024,128]{2,1,0:T(8,128)(2,1)S(1)}, bf16[4,1024,128]{2,1,0:T(8,128)(2,1)S(1)}, u32[]{:S(2)}, u32[]{:S(2)}) collective-permute-start(bf16[4,1024,128]{2,1,0:T(8,128)(2,1)S(1)} %all-to-all-done.2.mine_ref), channel_id=1, source_target_pairs={{0,4},{4,0},{1,5},{5,1},{2,6},{6,2},{3,7},{7,3},{8,12},{12,8},{9,1... | collective-permute-start | bytes 3145736 | tf_op jit(solution)/shard_map/ppermute | solution.py:291
  97.6 0.0 copy-done.3
  97.7 0.2 multiply_reduce_fusion.2
  97.9 0.0 copy-start.1
  97.9 0.0 copy-start.2
  97.9 2.1 %collective-permute-start.1 = (bf16[512,512]{1,0:T(8,128)(2,1)S(1)}, bf16[512,512]{1,0:T(8,128)(2,1)S(1)}, u32[]{:S(2)}, u32[]{:S(2)}) collective-permute-start(bf16[512,512]{1,0:T(8,128)(2,1)S(1)} %get-tuple-element.14.rows_own_ref), channel_id=1, source_target_pairs={{0,4},{4,0},{1,5},{5,1},{2,6},{6,2},{3,7},{7,3},{8,12},{12,8},{9,1... | collective-permute-start | bytes 1572872 | tf_op jit(solution)/shard_map/ppermute | solution.py:290
  99.9 0.0 copy-done
  99.9 0.3 multiply_reduce_fusion
  100.2 1.6 %collective-permute-done.1.rows_other_ref = bf16[512,512]{1,0:T(8,128)(2,1)S(1)} collective-permute-done((bf16[512,512]{1,0:T(8,128)(2,1)S(1)}, bf16[512,512]{1,0:T(8,128)(2,1)S(1)}, u32[]{:S(2)}, u32[]{:S(2)}) %collective-permute-start.1) | collective-permute-done | bytes 524320 | tf_op jit(solution)/shard_map/ppermute | solution.py:290
  101.8 0.2 multiply_reduce_fusion.1
  102.0 0.0 collective-permute-done.2.other_ref
  102.0 0.1 broadcast_in_dim.9.col_norm_ref
  102.1 0.1 broadcast_in_dim.10.row_norm_ref
  102.3 0.0 copy-done.1
  102.3 0.0 copy-done.2
  102.3 12.5 %update.1 = f32[512,512]{1,0:T(8,128)} custom-call(s32[5]{0:T(128)S(1)} %copy-done.2, bf16[512,1024]{1,0:T(8,128)(2,1)S(1)} %copy-done, f32[512,128]{1,0:T(8,128)S(1)} %broadcast_in_dim.9.col_norm_ref, bf16[512,512]{1,0:T(8,128)(2,1)S(1)} %get-tuple-element.14.rows_own_ref, bf16[512,512]{1,0:T(8,128)(2,1)S(1)} %collective-permute-done.1.rows_other_ref, ...), custom_call_target="tpu_custom_call" | custom-call | tf_op jit(solution)/shard_map/update/pallas_call | solution.py:251
  (4 shorter events, 0.1 us)
Async XLA Ops:
  0.0 11.4 %copy-start.6 = (s32[128]{0:T(128)S(1)}, s32[128]{0:T(128)}, u32[]{:S(2)}) copy-start(s32[128]{0:T(128)} %param.5) | copy-start | bytes 1540
  2.6 14.1 %collective-permute-start = (bf16[1088,128]{1,0:T(8,128)(2,1)}, bf16[1088,128]{1,0:T(8,128)(2,1)S(1)}, u32[]{:S(2)}, u32[]{:S(2)}) collective-permute-start(bf16[1088,128]{1,0:T(8,128)(2,1)} %get-tuple-element.10), channel_id=1, source_target_pairs={{0,4},{4,0},{1,5},{5,1},{2,6},{6,2},{3,7},{7,3},{8,12},{12,8},{9,1... | collective-permute-start | bytes 835592 | tf_op jit(solution)/shard_map/ppermute | solution.py:281
  16.7 0.7 copy-start.5
  75.5 4.2 %copy-start.4 = (bf16[64,32,128]{2,1,0:T(8,128)(2,1)S(1)}, bf16[64,32,128]{2,1,0:T(8,128)(2,1)}, u32[]{:S(2)}) copy-start(bf16[64,32,128]{2,1,0:T(8,128)(2,1)} %all_to_all.15.came_ref) | copy-start | bytes 1572868
  75.5 22.1 %copy-start.3 = (bf16[64,32,128]{2,1,0:T(8,128)(2,1)S(1)}, bf16[64,32,128]{2,1,0:T(8,128)(2,1)}, u32[]{:S(2)}) copy-start(bf16[64,32,128]{2,1,0:T(8,128)(2,1)} %all_to_all.16.came_ref) | copy-start | bytes 1572868
  75.5 14.8 %all-to-all-start.2 = ((bf16[4,1024,128]{2,1,0:T(8,128)(2,1)}), bf16[4,1024,128]{2,1,0:T(8,128)(2,1)S(1)}, u32[]{:S(2)}, u32[]{:S(2)}) async-start(bf16[4,1024,128]{2,1,0:T(8,128)(2,1)} %third_operand.1), calls=%async_computation.2 | async-start | bytes 2097152 | tf_op jit(solution)/shard_map/all_to_all | solution.py:286
  79.7 20.3 %copy-start = (bf16[512,1024]{1,0:T(8,128)(2,1)S(1)}, bf16[512,1024]{1,0:T(8,128)(2,1)}, u32[]{:S(2)}) copy-start(bf16[512,1024]{1,0:T(8,128)(2,1)} %cols_ref.1) | copy-start | bytes 3145732
  90.3 11.7 %collective-permute-start.2 = (bf16[4,1024,128]{2,1,0:T(8,128)(2,1)S(1)}, bf16[4,1024,128]{2,1,0:T(8,128)(2,1)S(1)}, u32[]{:S(2)}, u32[]{:S(2)}) collective-permute-start(bf16[4,1024,128]{2,1,0:T(8,128)(2,1)S(1)} %all-to-all-done.2.mine_ref), channel_id=1, source_target_pairs={{0,4},{4,0},{1,5},{5,1},{2,6},{6,2},{3,7},{7,3},{8,12},{12,8},{9,1... | collective-permute-start | bytes 3145736 | tf_op jit(solution)/shard_map/ppermute | solution.py:291
  97.9 4.4 %copy-start.1 = (f32[512,512]{1,0:T(8,128)S(1)}, f32[512,512]{1,0:T(8,128)}, u32[]{:S(2)}) copy-start(f32[512,512]{1,0:T(8,128)} %trailing_ref.1) | copy-start | bytes 3145732
  97.9 4.4 %copy-start.2 = (s32[5]{0:T(128)S(1)}, s32[5]{0:T(128)}, u32[]{:S(2)}) copy-start(s32[5]{0:T(128)} %stack.24.at_ref) | copy-start | bytes 64
  97.9 3.9 %collective-permute-start.1 = (bf16[512,512]{1,0:T(8,128)(2,1)S(1)}, bf16[512,512]{1,0:T(8,128)(2,1)S(1)}, u32[]{:S(2)}, u32[]{:S(2)}) collective-permute-start(bf16[512,512]{1,0:T(8,128)(2,1)S(1)} %get-tuple-element.14.rows_own_ref), channel_id=1, source_target_pairs={{0,4},{4,0},{1,5},{5,1},{2,6},{6,2},{3,7},{7,3},{8,12},{12,8},{9,1... | collective-permute-start | bytes 1572872 | tf_op jit(solution)/shard_map/ppermute | solution.py:290

commit v4 on v3

--- a/solution.py
+++ b/solution.py
@@ -95,7 +95,8 @@
 
 VMEM = pl.BlockSpec(memory_space=pltpu.VMEM)
 SMEM = pl.BlockSpec(memory_space=pltpu.SMEM)
-ANY = pl.BlockSpec(memory_space=pl.ANY)
+HBM = pl.BlockSpec(memory_space=pltpu.HBM)
+SMALL = pltpu.CompilerParams(vmem_limit_bytes=4 * 2**20)
 
 
 def prep(centres_cols, diag_inverse, centres_rows, quarter):
@@ -104,7 +105,7 @@
     out = jax.ShapeDtypeStruct((total, LANES), jnp.bfloat16)
     return pl.pallas_call(
         prep_body,
-        in_specs=[ANY, ANY, VMEM],
+        in_specs=[HBM, HBM, VMEM],
         out_specs=[VMEM, VMEM],
         out_shape=[out, out],
         scratch_shapes=[
@@ -112,6 +113,7 @@
             pltpu.VMEM((quarter, size), jnp.float32),
             pltpu.SemaphoreType.DMA((2,)),
         ],
+        compiler_params=SMALL,
         name="prep",
     )(centres_cols, diag_inverse, centres_rows)
 
@@ -140,6 +142,7 @@
             jax.ShapeDtypeStruct((chips, 2 * per_chip, LANES), jnp.bfloat16),
             jax.ShapeDtypeStruct((per_chip, LANES), jnp.bfloat16),
         ],
+        compiler_params=SMALL,
         name="first_operand",
     )(at, kept, got)
 
@@ -158,6 +161,7 @@
         in_specs=[SMEM, VMEM, VMEM],
         out_specs=VMEM,
         out_shape=jax.ShapeDtypeStruct(came.shape, came.dtype),
+        compiler_params=SMALL,
         name="second_operand",
     )(at, came, rows)
 
@@ -176,6 +180,7 @@
         in_specs=[VMEM],
         out_specs=VMEM,
         out_shape=jax.ShapeDtypeStruct((row_count, chips * length // 2, LANES), came.dtype),
+        compiler_params=SMALL,
         name="third_operand",
     )(came)
 
@@ -259,7 +264,7 @@
         + [square] * 2
         + [pltpu.VMEM((size, size), jnp.float32)]
         + [pltpu.VMEM((STEP, size), jnp.float32)] * 2,
-        compiler_params=pltpu.CompilerParams(vmem_limit_bytes=32 * 2**20),
+        compiler_params=pltpu.CompilerParams(vmem_limit_bytes=20 * 2**20),
         name="update",
     )(at, cols, norms(cols), rows_own, rows_other, norms(rows_own, rows_other), mine, other, trailing)
 

time: 115 us -> 110 us (0.957)
  Pallas kernels: 21.1 us -> 15.1 us
  local copies, waits for them, and re-layouts: 2.35 us -> 4.2 us
    unnamed x14 -> x12, local copies, waits for them, and re-layouts: 0.73 us -> 3.16 us
    pallas_call x1, Pallas kernels: 2.57 us -> 0.18 us  [prep(): pl.pallas_call(prep_body, in_specs=[HBM, HBM, VMEM], out_specs=[VMEM, VME...]
    pallas_call x1, Pallas kernels: 1.91 us -> 0.61 us  [second_operand(): pl.pallas_call(second_body, in_specs=[SMEM, VMEM, VMEM], out_specs=VMEM,...]
    pallas_call x1, Pallas kernels: 1.93 us -> 0.63 us  [first_operand(): pl.pallas_call(first_body, in_specs=[SMEM, VMEM, VMEM], out_specs=[VMEM,...]
where the time goes in v4:
time: 110 us
  blocking collectives  51.6 us (47%)
  starting transfers between devices  22.1 us (20%)
  Pallas kernels  15.1 us (14%)
  waiting for transfers between devices  12.2 us (11%)
  local copies, waits for them, and re-layouts  4.2 us (4%)
  between operations  3.46 us (3%)
  other arithmetic  1.3 us (1%)
    all_to_all x1, blocking collectives, on_device(): first = lax.all_to_all(outgoing, 'chip', 0, 0)  28.7 us
    all_to_all x1, blocking collectives, on_device(): second = lax.all_to_all(second_operand(at, first, rows_later), 'chip', 0, 0)  22.9 us
    pallas_call x1, Pallas kernels, update(): pl.pallas_call(update_body, in_specs=[SMEM] + [VMEM] * 8, out_specs=VMEM,...  12.5 us
    all_to_all x1, waiting for transfers between devices, on_device(): all_mine = lax.all_to_all(third_operand(second, row_count), 'row', 0, 0)  10.6 us
    ppermute x1, starting transfers between devices, on_device(): got = lax.ppermute(sent, 'core', swap)  8.78 us
    ppermute x1, starting transfers between devices, on_device(): all_other = lax.ppermute(all_mine, 'core', swap)  7.29 us
    all_to_all x1, starting transfers between devices, on_device(): all_mine = lax.all_to_all(third_operand(second, row_count), 'row', 0, 0)  4.01 us
    unnamed x12, local copies, waits for them, and re-layouts  3.16 us
  transfers between devices with their start and end apart: 4, of which 2 were waited for; matrix products, arithmetic and copies ran while one was open for 2% of the time, Pallas kernels for 0%

profile of v4, /device:TPU:1, one launch (start us, length us, event | category | flops | bytes accessed | tf_op | source)
XLA Modules:
  0.0 109.9 jit_solution(7220926220545124641)
XLA Ops:
  0.0 0.0 copy-start
  0.0 1.2 %copy-done = bf16[512,1024]{1,0:T(8,128)(2,1)S(1)} copy-done((bf16[512,1024]{1,0:T(8,128)(2,1)S(1)}, bf16[512,1024]{1,0:T(8,128)(2,1)}, u32[]{:S(2)}) %copy-start) | copy-done | bytes 1048600
  1.2 0.0 copy-start.2
  1.2 1.2 %copy-done.2 = f32[512,512]{1,0:T(8,128)S(1)} copy-done((f32[512,512]{1,0:T(8,128)S(1)}, f32[512,512]{1,0:T(8,128)}, u32[]{:S(2)}) %copy-start.2) | copy-done | bytes 1048600
  2.5 0.0 copy-start.4
  2.5 0.7 copy-done.4
  3.1 0.0 copy-start.5
  3.2 0.2 prep.1
  3.3 8.8 %collective-permute-start = (bf16[1088,128]{1,0:T(8,128)(2,1)S(1)}, bf16[1088,128]{1,0:T(8,128)(2,1)S(1)}, u32[]{:S(2)}, u32[]{:S(2)}) collective-permute-start(bf16[1088,128]{1,0:T(8,128)(2,1)S(1)} %get-tuple-element.10), channel_id=1, source_target_pairs={{0,4},{4,0},{1,5},{5,1},{2,6},{6,2},{3,7},{7,3},{8,12},{12,8},{9,1... | collective-permute-start | bytes 835592 | tf_op jit(solution)/shard_map/ppermute | solution.py:286
  12.1 0.0 copy-done.5
  12.1 0.6 fusion
  15.4 0.7 dynamic_slice.4
  16.8 0.1 stack.24.at_ref
  16.9 0.0 collective-permute-done.got_ref
  16.9 0.6 first_operand.1
  17.5 28.7 %all_to_all.15.came_ref = bf16[64,32,128]{2,1,0:T(8,128)(2,1)S(1)} all-to-all(bf16[64,32,128]{2,1,0:T(8,128)(2,1)S(1)} %get-tuple-element.11), channel_id=1, replica_groups=mesh['chip'=64,'core'=2,'row'=4] {'chip'}, dimensions={0} | all-to-all | bytes 1048576 | tf_op jit(solution)/shard_map/all_to_all | solution.py:289
  46.2 0.6 second_operand.1
  46.8 22.9 %all_to_all.16.came_ref = bf16[64,32,128]{2,1,0:T(8,128)(2,1)S(1)} all-to-all(bf16[64,32,128]{2,1,0:T(8,128)(2,1)S(1)} %second_operand.1), channel_id=1, replica_groups=mesh['chip'=64,'core'=2,'row'=4] {'chip'}, dimensions={0} | all-to-all | bytes 1048576 | tf_op jit(solution)/shard_map/all_to_all | solution.py:290
  69.7 1.1 %third_operand.1 = bf16[4,1024,128]{2,1,0:T(8,128)(2,1)} custom-call(bf16[64,32,128]{2,1,0:T(8,128)(2,1)S(1)} %all_to_all.16.came_ref), custom_call_target="tpu_custom_call" | custom-call | tf_op jit(solution)/shard_map/third_operand/pallas_call | solution.py:178
  70.8 4.0 %all-to-all-start.2 = ((bf16[4,1024,128]{2,1,0:T(8,128)(2,1)}), bf16[4,1024,128]{2,1,0:T(8,128)(2,1)S(1)}, u32[]{:S(2)}, u32[]{:S(2)}) async-start(bf16[4,1024,128]{2,1,0:T(8,128)(2,1)} %third_operand.1), calls=%async_computation.2 | async-start | bytes 2097152 | tf_op jit(solution)/shard_map/all_to_all | solution.py:291
  74.8 0.0 copy-start.1
  74.8 10.6 %all-to-all-done.2.mine_ref = bf16[4,1024,128]{2,1,0:T(8,128)(2,1)S(1)} async-done(((bf16[4,1024,128]{2,1,0:T(8,128)(2,1)}), bf16[4,1024,128]{2,1,0:T(8,128)(2,1)S(1)}, u32[]{:S(2)}, u32[]{:S(2)}) %all-to-all-start.2) | async-done | bytes 1048608 | tf_op jit(solution)/shard_map/all_to_all | solution.py:291
  85.5 7.3 %collective-permute-start.2 = (bf16[4,1024,128]{2,1,0:T(8,128)(2,1)S(1)}, bf16[4,1024,128]{2,1,0:T(8,128)(2,1)S(1)}, u32[]{:S(2)}, u32[]{:S(2)}) collective-permute-start(bf16[4,1024,128]{2,1,0:T(8,128)(2,1)S(1)} %all-to-all-done.2.mine_ref), channel_id=1, source_target_pairs={{0,4},{4,0},{1,5},{5,1},{2,6},{6,2},{3,7},{7,3},{8,12},{12,8},{9,1... | collective-permute-start | bytes 3145736 | tf_op jit(solution)/shard_map/ppermute | solution.py:296
  92.8 0.2 multiply_reduce_fusion.2
  93.0 0.0 copy-start.3
  93.0 2.1 %collective-permute-start.1 = (bf16[512,512]{1,0:T(8,128)(2,1)S(1)}, bf16[512,512]{1,0:T(8,128)(2,1)S(1)}, u32[]{:S(2)}, u32[]{:S(2)}) collective-permute-start(bf16[512,512]{1,0:T(8,128)(2,1)S(1)} %get-tuple-element.14.rows_own_ref), channel_id=1, source_target_pairs={{0,4},{4,0},{1,5},{5,1},{2,6},{6,2},{3,7},{7,3},{8,12},{12,8},{9,1... | collective-permute-start | bytes 1572872 | tf_op jit(solution)/shard_map/ppermute | solution.py:295
  95.0 0.0 copy-done.1
  95.1 0.3 multiply_reduce_fusion
  95.3 1.6 %collective-permute-done.1.rows_other_ref = bf16[512,512]{1,0:T(8,128)(2,1)S(1)} collective-permute-done((bf16[512,512]{1,0:T(8,128)(2,1)S(1)}, bf16[512,512]{1,0:T(8,128)(2,1)S(1)}, u32[]{:S(2)}, u32[]{:S(2)}) %collective-permute-start.1) | collective-permute-done | bytes 524320 | tf_op jit(solution)/shard_map/ppermute | solution.py:295
  96.9 0.2 multiply_reduce_fusion.1
  97.1 0.0 collective-permute-done.2.other_ref
  97.1 0.1 broadcast_in_dim.9.col_norm_ref
  97.3 0.1 broadcast_in_dim.10.row_norm_ref
  97.4 0.0 copy-done.3
  97.4 12.5 %update.1 = f32[512,512]{1,0:T(8,128)} custom-call(s32[5]{0:T(128)S(1)} %stack.24.at_ref, bf16[512,1024]{1,0:T(8,128)(2,1)S(1)} %copy-done.1, f32[512,128]{1,0:T(8,128)S(1)} %broadcast_in_dim.9.col_norm_ref, bf16[512,512]{1,0:T(8,128)(2,1)S(1)} %get-tuple-element.14.rows_own_ref, bf16[512,512]{1,0:T(8,128)(2,1)S(1)} %collective-permute-done.1.rows_other_ref, ...), custom_call_target="tpu_custom_call" | custom-call | tf_op jit(solution)/shard_map/update/pallas_call | solution.py:256
  (4 shorter events, 0.1 us)
Async XLA Ops:
  0.0 1.2 %copy-start = (bf16[512,1024]{1,0:T(8,128)(2,1)S(1)}, bf16[512,1024]{1,0:T(8,128)(2,1)}, u32[]{:S(2)}) copy-start(bf16[512,1024]{1,0:T(8,128)(2,1)} %cols_ref.1) | copy-start | bytes 3145732
  1.2 1.2 %copy-start.2 = (f32[512,512]{1,0:T(8,128)S(1)}, f32[512,512]{1,0:T(8,128)}, u32[]{:S(2)}) copy-start(f32[512,512]{1,0:T(8,128)} %inv_hbm.1) | copy-start | bytes 3145732
  2.5 0.7 copy-start.4
  3.1 9.0 %copy-start.5 = (s32[128]{0:T(128)S(1)}, s32[128]{0:T(128)}, u32[]{:S(2)}) copy-start(s32[128]{0:T(128)} %param.5) | copy-start | bytes 1540
  3.3 13.5 %collective-permute-start = (bf16[1088,128]{1,0:T(8,128)(2,1)S(1)}, bf16[1088,128]{1,0:T(8,128)(2,1)S(1)}, u32[]{:S(2)}, u32[]{:S(2)}) collective-permute-start(bf16[1088,128]{1,0:T(8,128)(2,1)S(1)} %get-tuple-element.10), channel_id=1, source_target_pairs={{0,4},{4,0},{1,5},{5,1},{2,6},{6,2},{3,7},{7,3},{8,12},{12,8},{9,1... | collective-permute-start | bytes 835592 | tf_op jit(solution)/shard_map/ppermute | solution.py:286
  70.8 14.7 %all-to-all-start.2 = ((bf16[4,1024,128]{2,1,0:T(8,128)(2,1)}), bf16[4,1024,128]{2,1,0:T(8,128)(2,1)S(1)}, u32[]{:S(2)}, u32[]{:S(2)}) async-start(bf16[4,1024,128]{2,1,0:T(8,128)(2,1)} %third_operand.1), calls=%async_computation.2 | async-start | bytes 2097152 | tf_op jit(solution)/shard_map/all_to_all | solution.py:291
  74.8 20.3 %copy-start.1 = (bf16[512,1024]{1,0:T(8,128)(2,1)S(1)}, bf16[512,1024]{1,0:T(8,128)(2,1)}, u32[]{:S(2)}) copy-start(bf16[512,1024]{1,0:T(8,128)(2,1)} %cols_ref.1) | copy-start | bytes 3145732
  85.5 11.7 %collective-permute-start.2 = (bf16[4,1024,128]{2,1,0:T(8,128)(2,1)S(1)}, bf16[4,1024,128]{2,1,0:T(8,128)(2,1)S(1)}, u32[]{:S(2)}, u32[]{:S(2)}) collective-permute-start(bf16[4,1024,128]{2,1,0:T(8,128)(2,1)S(1)} %all-to-all-done.2.mine_ref), channel_id=1, source_target_pairs={{0,4},{4,0},{1,5},{5,1},{2,6},{6,2},{3,7},{7,3},{8,12},{12,8},{9,1... | collective-permute-start | bytes 3145736 | tf_op jit(solution)/shard_map/ppermute | solution.py:296
  93.0 4.4 %copy-start.3 = (f32[512,512]{1,0:T(8,128)S(1)}, f32[512,512]{1,0:T(8,128)}, u32[]{:S(2)}) copy-start(f32[512,512]{1,0:T(8,128)} %trailing_ref.1) | copy-start | bytes 3145732
  93.0 3.9 %collective-permute-start.1 = (bf16[512,512]{1,0:T(8,128)(2,1)S(1)}, bf16[512,512]{1,0:T(8,128)(2,1)S(1)}, u32[]{:S(2)}, u32[]{:S(2)}) collective-permute-start(bf16[512,512]{1,0:T(8,128)(2,1)S(1)} %get-tuple-element.14.rows_own_ref), channel_id=1, source_target_pairs={{0,4},{4,0},{1,5},{5,1},{2,6},{6,2},{3,7},{7,3},{8,12},{12,8},{9,1... | collective-permute-start | bytes 1572872 | tf_op jit(solution)/shard_map/ppermute | solution.py:295

commit v5 on v4

--- a/solution.py
+++ b/solution.py
@@ -55,14 +55,9 @@
     return theta
 
 
-def prep_body(x_hbm, inv_hbm, rows_ref, kept_ref, sent_ref, x_ref, inv_ref, sems):
-    row, core = lax.axis_index("row"), lax.axis_index("core")
+def prep_body(x_ref, inv_ref, rows_ref, kept_ref, sent_ref):
+    core = lax.axis_index("core")
     size, width = x_ref.shape
-    take = pl.ds(pl.multiple_of(row * size, size), size)
-    copy_x = pltpu.make_async_copy(x_hbm.at[take, :], x_ref, sems.at[0])
-    copy_inv = pltpu.make_async_copy(inv_hbm.at[take, :], inv_ref, sems.at[1])
-    copy_x.start()
-    copy_inv.start()
     half, groups = width // CORES, inv_ref.shape[1] // LANES
     rows = size // CORES
     base = size * (half // LANES)
@@ -78,12 +73,10 @@
                     to = end + CORES * count * i + count * which
                     out_ref[to : to + count, :] = rows_ref[:, LANES * i : LANES * (i + 1)]
 
-    copy_x.wait()
     for out_ref, which in ((kept_ref, core), (sent_ref, 1 - core)):
         for i in range(half // LANES):
             at = pl.multiple_of(which * half + LANES * i, LANES)
             out_ref[size * i : size * (i + 1), :] = x_ref[:, pl.ds(at, LANES)]
-    copy_inv.wait()
     for out_ref, which in ((kept_ref, core), (sent_ref, 1 - core)):
         for i in range(groups):
             at = pl.multiple_of(which * rows, rows)
@@ -94,38 +87,39 @@
 
 
 VMEM = pl.BlockSpec(memory_space=pltpu.VMEM)
-SMEM = pl.BlockSpec(memory_space=pltpu.SMEM)
-HBM = pl.BlockSpec(memory_space=pltpu.HBM)
 SMALL = pltpu.CompilerParams(vmem_limit_bytes=4 * 2**20)
 
 
-def prep(centres_cols, diag_inverse, centres_rows, quarter):
-    size, width = centres_cols.shape
-    total = (quarter * width // CORES + 2 * quarter // CORES * size + CORES * centres_rows.size) // LANES
+def prep(x, inverse, rows):
+    size, width = x.shape
+    total = (width * size // CORES + 2 * inverse.size // CORES + CORES * rows.size) // LANES
     out = jax.ShapeDtypeStruct((total, LANES), jnp.bfloat16)
     return pl.pallas_call(
         prep_body,
-        in_specs=[HBM, HBM, VMEM],
+        in_specs=[VMEM, VMEM, VMEM],
         out_specs=[VMEM, VMEM],
         out_shape=[out, out],
-        scratch_shapes=[
-            pltpu.VMEM((quarter, width), jnp.bfloat16),
-            pltpu.VMEM((quarter, size), jnp.float32),
-            pltpu.SemaphoreType.DMA((2,)),
-        ],
         compiler_params=SMALL,
         name="prep",
-    )(centres_cols, diag_inverse, centres_rows)
-
-
-def first_body(at_ref, kept_ref, got_ref, out_ref, later_ref):
+    )(x, inverse, rows)
+
+
+def owner_of(panel_ref):
+    blocks = panel_ref.shape[1]
+    at = lax.broadcasted_iota(jnp.int32, (1, blocks), 1)
+    found = jnp.where(panel_ref[...] == blocks // 4, at, 0).astype(jnp.float32)
+    return jnp.sum(found).astype(jnp.int32)
+
+
+def first_body(panel_ref, kept_ref, got_ref, out_ref, later_ref):
     chips, length, _ = out_ref.shape
     per_chip = length // 2
     total = chips * per_chip
-    kept = at_ref[3] > 0
+    core = lax.axis_index("core")
+    kept = owner_of(panel_ref) % CORES == core
     out_ref[:, :per_chip, :] = jnp.where(kept, kept_ref[:total], got_ref[:total]).reshape(chips, per_chip, LANES)
     for n in range(2):
-        at = pl.ds(pl.multiple_of(total + (2 * at_ref[1] + n) * per_chip, per_chip), per_chip)
+        at = pl.ds(pl.multiple_of(total + (2 * core + n) * per_chip, per_chip), per_chip)
         rows = (kept_ref[at, :].astype(jnp.float32) + got_ref[at, :].astype(jnp.float32)).astype(jnp.bfloat16)
         if n == 0:
             out_ref[:, per_chip:, :] = jnp.broadcast_to(rows[None], (chips, per_chip, LANES))
@@ -133,10 +127,10 @@
             later_ref[...] = rows
 
 
-def first_operand(at, kept, got, chips, per_chip):
+def first_operand(panel, kept, got, chips, per_chip):
     return pl.pallas_call(
         first_body,
-        in_specs=[SMEM, VMEM, VMEM],
+        in_specs=[VMEM, VMEM, VMEM],
         out_specs=[VMEM, VMEM],
         out_shape=[
             jax.ShapeDtypeStruct((chips, 2 * per_chip, LANES), jnp.bfloat16),
@@ -144,26 +138,26 @@
         ],
         compiler_params=SMALL,
         name="first_operand",
-    )(at, kept, got)
-
-
-def second_body(at_ref, came_ref, rows_ref, out_ref):
+    )(panel, kept, got)
+
+
+def second_body(panel_ref, came_ref, rows_ref, out_ref):
     chips, length, _ = out_ref.shape
     per_chip = length // 2
-    piece = came_ref[at_ref[4], :per_chip, :]
+    piece = came_ref[owner_of(panel_ref) // CORES, :per_chip, :]
     out_ref[:, :per_chip, :] = jnp.broadcast_to(piece[None], (chips, per_chip, LANES))
     out_ref[:, per_chip:, :] = jnp.broadcast_to(rows_ref[...][None], (chips, per_chip, LANES))
 
 
-def second_operand(at, came, rows):
+def second_operand(panel, came, rows):
     return pl.pallas_call(
         second_body,
-        in_specs=[SMEM, VMEM, VMEM],
+        in_specs=[VMEM, VMEM, VMEM],
         out_specs=VMEM,
         out_shape=jax.ShapeDtypeStruct(came.shape, came.dtype),
         compiler_params=SMALL,
         name="second_operand",
-    )(at, came, rows)
+    )(panel, came, rows)
 
 
 def third_body(came_ref, out_ref):
@@ -185,7 +179,7 @@
     )(came)
 
 
-def update_body(at_ref, cols_ref, col_norm_ref, rows_own_ref, rows_other_ref, row_norm_ref, mine_ref, other_ref, trailing_ref, out_ref,
+def update_body(panel_ref, cols_ref, col_norm_ref, rows_own_ref, rows_other_ref, row_norm_ref, mine_ref, other_ref, trailing_ref, out_ref,
                 x_ref, high_ref, low_ref, left_ref, left_low_ref, right_ref, right_low_ref,
                 rows_ref, k_ref, k_low_ref, gram_ref, norm_ref, inv_ref):
     size, width = cols_ref.shape
@@ -194,7 +188,7 @@
     quarter = size // quarters
     part = quarter // CORES
     groups, inv_groups = half // LANES, size // LANES
-    core = at_ref[1]
+    core = lax.axis_index("core")
     for k, (got, which) in enumerate(((mine_ref, core), (other_ref, 1 - core))):
         for q in range(quarters):
             for i in range(groups):
@@ -237,8 +231,11 @@
         to_low_ref[...] = solved_low
 
     update = dot_t(left_ref[...], right_ref[...]) + (dot_t(left_ref[...], right_low_ref[...]) + dot_t(left_low_ref[...], right_ref[...]))
+    blocks = panel_ref.shape[1]
+    here = lax.broadcasted_iota(jnp.int32, (1, blocks), 1) == CORES * lax.axis_index("chip") + core
+    own_rank = jnp.sum(jnp.where(here, panel_ref[...], 0).astype(jnp.float32))
     old = trailing_ref[...]
-    out_ref[...] = jnp.where(at_ref[2] > 0, old - update, old)
+    out_ref[...] = jnp.where(own_rank > blocks // 4, old - update, old)
 
 
 def norms(*pieces):
@@ -249,13 +246,13 @@
     return jnp.broadcast_to(jnp.sqrt(total), (pieces[0].shape[0], LANES))
 
 
-def update(at, cols, rows_own, rows_other, mine, other, trailing):
+def update(panel, cols, rows_own, rows_other, mine, other, trailing):
     size, width = cols.shape
     square = pltpu.VMEM((size, size), jnp.bfloat16)
     vectors = pltpu.VMEM((size, width), jnp.bfloat16)
     return pl.pallas_call(
         update_body,
-        in_specs=[SMEM] + [VMEM] * 8,
+        in_specs=[VMEM] * 9,
         out_specs=VMEM,
         out_shape=jax.ShapeDtypeStruct(trailing.shape, trailing.dtype),
         scratch_shapes=[vectors]
@@ -266,35 +263,32 @@
         + [pltpu.VMEM((STEP, size), jnp.float32)] * 2,
         compiler_params=pltpu.CompilerParams(vmem_limit_bytes=20 * 2**20),
         name="update",
-    )(at, cols, norms(cols), rows_own, rows_other, norms(rows_own, rows_other), mine, other, trailing)
+    )(panel, cols, norms(cols), rows_own, rows_other, norms(rows_own, rows_other), mine, other, trailing)
 
 
 def on_device(chips, row_count, panel, centres_cols, centres_rows, diag_inverse, trailing):
     size, width = centres_cols.shape
-    blocks = panel.shape[0]
-    target_rank = blocks // 4
     quarter = size // row_count
-    panel_at = jnp.sum(jnp.where(panel == target_rank, jnp.arange(blocks, dtype=jnp.int32), 0))
-    owner_chip, owner_core = panel_at // CORES, panel_at % CORES
-    chip, core, row = lax.axis_index("chip"), lax.axis_index("core"), lax.axis_index("row")
-    own_rank = lax.dynamic_index_in_dim(panel, chip * CORES + core, 0, keepdims=False)
-    flags = [row, core, own_rank > target_rank, core == owner_core, owner_chip]
-    at = jnp.stack([flag.astype(jnp.int32) for flag in flags])
+    row = lax.axis_index("row")
+    panel = panel[None]
     swap = [(0, 1), (1, 0)]
 
-    kept, sent = prep(centres_cols, diag_inverse, centres_rows, quarter)
+    x = lax.dynamic_slice_in_dim(centres_cols, row * quarter, quarter, 0)
+    inverse = lax.dynamic_slice_in_dim(diag_inverse, row * quarter, quarter, 0)
+    kept, sent = prep(x, inverse, centres_rows)
     got = lax.ppermute(sent, "core", swap)
     per_chip = (2 * width * quarter // CORES) // (LANES * chips)
-    outgoing, rows_later = first_operand(at, kept, got, chips, per_chip)
+    outgoing, rows_later = first_operand(panel, kept, got, chips, per_chip)
     first = lax.all_to_all(outgoing, "chip", 0, 0)
-    second = lax.all_to_all(second_operand(at, first, rows_later), "chip", 0, 0)
+    second = lax.all_to_all(second_operand(panel, first, rows_later), "chip", 0, 0)
     all_mine = lax.all_to_all(third_operand(second, row_count), "row", 0, 0)
 
     tiles = [got_rows[:, i : i + 8] for got_rows in (first, second) for i in range(per_chip, 2 * per_chip, 8)]
     rows_own = jnp.concatenate([tile.reshape(size, LANES) for tile in tiles], axis=1)
     rows_other = lax.ppermute(rows_own, "core", swap)
+    all_mine, rows_other = lax.optimization_barrier((all_mine, rows_other))
     all_other = lax.ppermute(all_mine, "core", swap)
-    return update(at, centres_cols, rows_own, rows_other, all_mine, all_other, trailing)
+    return update(panel, centres_cols, rows_own, rows_other, all_mine, all_other, trailing)
 
 
 def solution(mesh):

time: 110 us -> 104 us (0.945)
  blocking collectives: 51.6 us -> 28.3 us
  starting transfers between devices: 22.1 us -> 33.5 us
  waiting for transfers between devices: 12.2 us -> 20.2 us
  between operations: 3.46 us -> 0.14 us
    all_to_all x1 -> x0, blocking collectives: 22.9 us -> none  [on_device(): second = lax.all_to_all(second_operand(at, first, rows_later), 'chip', 0, 0)]
    all_to_all x0 -> x1, waiting for transfers between devices: none -> 16.4 us  [on_device(): lax.all_to_all(second_operand(panel, first, rows_later), 'chip', 0, 0)]
    all_to_all x1, waiting for transfers between devices: 10.6 us -> 1.11 us  [on_device(): all_mine = lax.all_to_all(third_operand(second, row_count), 'row', 0, 0)]
    all_to_all x0 -> x1, starting transfers between devices: none -> 6.62 us  [on_device(): lax.all_to_all(second_operand(panel, first, rows_later), 'chip', 0, 0)]
    ppermute x1, starting transfers between devices: 2.05 us -> 6.35 us  [on_device(): rows_other = lax.ppermute(rows_own, 'core', swap)]
    ppermute x1, waiting for transfers between devices: 0.01 us -> 1.16 us  [on_device(): got = lax.ppermute(sent, 'core', swap)]
    unnamed x12 -> x16, local copies, waits for them, and re-layouts: 3.16 us -> 2.01 us
  transfers between devices with their start and end apart: 4 -> 5, of which waited for: 2 -> 5; matrix products, arithmetic and copies ran while one was open for 2% -> 3% of each run, Pallas kernels for 0% -> 0%
where the time goes in v5:
time: 104 us
  starting transfers between devices  33.5 us (32%)
  blocking collectives  28.3 us (27%)
  waiting for transfers between devices  20.2 us (19%)
  Pallas kernels  15.4 us (15%)
  local copies, waits for them, and re-layouts  4.35 us (4%)
  other arithmetic  1.72 us (2%)
    all_to_all x1, blocking collectives, on_device(): first = lax.all_to_all(outgoing, 'chip', 0, 0)  28.3 us
    all_to_all x1, waiting for transfers between devices, on_device(): lax.all_to_all(second_operand(panel, first, rows_later), 'chip', 0, 0)  16.4 us
    pallas_call x1, Pallas kernels, update(): pl.pallas_call(update_body, in_specs=[VMEM] * 9, out_specs=VMEM, out_shap...  13 us
    ppermute x1, starting transfers between devices, on_device(): got = lax.ppermute(sent, 'core', swap)  8.78 us
    ppermute x1, starting transfers between devices, on_device(): all_other = lax.ppermute(all_mine, 'core', swap)  7.69 us
    all_to_all x1, starting transfers between devices, on_device(): lax.all_to_all(second_operand(panel, first, rows_later), 'chip', 0, 0)  6.62 us
    ppermute x1, starting transfers between devices, on_device(): rows_other = lax.ppermute(rows_own, 'core', swap)  6.35 us
    all_to_all x1, starting transfers between devices, on_device(): all_mine = lax.all_to_all(third_operand(second, row_count), 'row', 0, 0)  4.01 us
  transfers between devices with their start and end apart: 5, of which 5 were waited for; matrix products, arithmetic and copies ran while one was open for 3% of the time, Pallas kernels for 0%

profile of v5, /device:TPU:1, one launch (start us, length us, event | category | flops | bytes accessed | tf_op | source)
XLA Modules:
  0.0 103.6 jit_solution(13309086298614573726)
XLA Ops:
  0.0 0.0 copy-start
  0.0 0.0 copy-start.6
  0.0 0.0 copy-start.7
  0.0 1.2 %copy-done = f32[512,512]{1,0:T(8,128)S(1)} copy-done((f32[512,512]{1,0:T(8,128)S(1)}, f32[512,512]{1,0:T(8,128)}, u32[]{:S(2)}) %copy-start) | copy-done | bytes 1048600
  1.2 1.0 constant_dynamic-slice_fusion.1.x_ref
  2.2 0.0 copy-done.6
  2.2 0.1 prep.1
  2.4 8.8 %collective-permute-start = (bf16[1088,128]{1,0:T(8,128)(2,1)S(1)}, bf16[1088,128]{1,0:T(8,128)(2,1)S(1)}, u32[]{:S(2)}, u32[]{:S(2)}) collective-permute-start(bf16[1088,128]{1,0:T(8,128)(2,1)S(1)} %get-tuple-element.12), channel_id=1, source_target_pairs={{0,4},{4,0},{1,5},{5,1},{2,6},{6,2},{3,7},{7,3},{8,12},{12,8},{9,1... | collective-permute-start | bytes 835592 | tf_op jit(solution)/shard_map/ppermute | solution.py:279
  11.2 1.2 %collective-permute-done.got_ref = bf16[1088,128]{1,0:T(8,128)(2,1)S(1)} collective-permute-done((bf16[1088,128]{1,0:T(8,128)(2,1)S(1)}, bf16[1088,128]{1,0:T(8,128)(2,1)S(1)}, u32[]{:S(2)}, u32[]{:S(2)}) %collective-permute-start) | collective-permute-done | bytes 278560 | tf_op jit(solution)/shard_map/ppermute | solution.py:279
  12.3 0.0 copy-done.7
  12.3 0.2 first_operand.1
  12.5 28.3 %all_to_all.15.came_ref = bf16[64,32,128]{2,1,0:T(8,128)(2,1)S(1)} all-to-all(bf16[64,32,128]{2,1,0:T(8,128)(2,1)S(1)} %get-tuple-element.13), channel_id=1, replica_groups=mesh['chip'=64,'core'=2,'row'=4] {'chip'}, dimensions={0} | all-to-all | bytes 1048576 | tf_op jit(solution)/shard_map/all_to_all | solution.py:282
  40.8 1.0 second_operand.1
  41.8 6.6 %all-to-all-start.1 = ((bf16[64,32,128]{2,1,0:T(8,128)(2,1)}), bf16[64,32,128]{2,1,0:T(8,128)(2,1)S(1)}, u32[]{:S(2)}, u32[]{:S(2)}) async-start(bf16[64,32,128]{2,1,0:T(8,128)(2,1)} %second_operand.1), calls=%async_computation.1 | async-start | bytes 1048576 | tf_op jit(solution)/shard_map/all_to_all | solution.py:283
  48.5 16.4 %all-to-all-done.1.came_ref = bf16[64,32,128]{2,1,0:T(8,128)(2,1)S(1)} async-done(((bf16[64,32,128]{2,1,0:T(8,128)(2,1)}), bf16[64,32,128]{2,1,0:T(8,128)(2,1)S(1)}, u32[]{:S(2)}, u32[]{:S(2)}) %all-to-all-start.1) | async-done | bytes 524320 | tf_op jit(solution)/shard_map/all_to_all | solution.py:283
  64.8 0.0 copy-start.2
  64.8 1.1 %third_operand.1 = bf16[4,1024,128]{2,1,0:T(8,128)(2,1)} custom-call(bf16[64,32,128]{2,1,0:T(8,128)(2,1)S(1)} %all-to-all-done.1.came_ref), custom_call_target="tpu_custom_call" | custom-call | tf_op jit(solution)/shard_map/third_operand/pallas_call | solution.py:172
  66.0 0.0 copy-done.2
  66.0 4.0 %all-to-all-start.2 = ((bf16[4,1024,128]{2,1,0:T(8,128)(2,1)}), bf16[4,1024,128]{2,1,0:T(8,128)(2,1)S(1)}, u32[]{:S(2)}, u32[]{:S(2)}) async-start(bf16[4,1024,128]{2,1,0:T(8,128)(2,1)} %third_operand.1), calls=%async_computation.2 | async-start | bytes 2097152 | tf_op jit(solution)/shard_map/all_to_all | solution.py:284
  70.0 0.0 copy-start.1
  70.0 1.1 %slice_bitcast_fusion.1 = (bf16[512,128]{1,0:T(8,128)(2,1)S(1)}, bf16[512,128]{1,0:T(8,128)(2,1)S(1)}) fusion(bf16[64,32,128]{2,1,0:T(8,128)(2,1)} %copy-done.2), kind=kLoop, calls=%fused_computation.5 | loop fusion | bytes 524288 | tf_op jit(solution)/shard_map/reshape | solution.py:287
  71.1 0.2 multiply_reduce_fusion.2
  71.3 6.3 %collective-permute-start.1 = (bf16[512,512]{1,0:T(8,128)(2,1)S(1)}, bf16[512,512]{1,0:T(8,128)(2,1)}, u32[]{:S(2)}, u32[]{:S(2)}) collective-permute-start(bf16[512,512]{1,0:T(8,128)(2,1)S(1)} %get-tuple-element.18.rows_own_ref), channel_id=1, source_target_pairs={{0,4},{4,0},{1,5},{5,1},{2,6},{6,2},{3,7},{7,3},{8,12},{12,8},{9,1... | collective-permute-start | bytes 1572872 | tf_op jit(solution)/shard_map/ppermute | solution.py:288
  77.6 0.0 copy-start.3
  77.7 0.8 copy-done.3
  78.4 0.9 collective-permute-done.1.rows_other_ref
  79.3 1.1 %all-to-all-done.2.mine_ref = bf16[4,1024,128]{2,1,0:T(8,128)(2,1)S(1)} async-done(((bf16[4,1024,128]{2,1,0:T(8,128)(2,1)}), bf16[4,1024,128]{2,1,0:T(8,128)(2,1)S(1)}, u32[]{:S(2)}, u32[]{:S(2)}) %all-to-all-start.2) | async-done | bytes 1048608 | tf_op jit(solution)/shard_map/all_to_all | solution.py:284
  80.4 0.0 copy-start.4
  80.4 0.0 copy-start.5
  80.4 7.7 %collective-permute-start.2 = (bf16[4,1024,128]{2,1,0:T(8,128)(2,1)S(1)}, bf16[4,1024,128]{2,1,0:T(8,128)(2,1)S(1)}, u32[]{:S(2)}, u32[]{:S(2)}) collective-permute-start(bf16[4,1024,128]{2,1,0:T(8,128)(2,1)S(1)} %all-to-all-done.2.mine_ref), channel_id=1, source_target_pairs={{0,4},{4,0},{1,5},{5,1},{2,6},{6,2},{3,7},{7,3},{8,12},{12,8},{9,1... | collective-permute-start | bytes 3145736 | tf_op jit(solution)/shard_map/ppermute | solution.py:290
  88.1 0.0 copy-done.1
  88.1 0.3 multiply_reduce_fusion
  88.4 1.2 %multiply_reduce_fusion.1 = f32[512]{0:T(512)S(1)} fusion(bf16[512,512]{1,0:T(8,128)(2,1)} %collective-permute-done.1.rows_other_ref), kind=kLoop, calls=%fused_computation.1 | loop fusion | flops 785920 | bytes 526336 | tf_op jit(solution)/shard_map/reduce_sum | solution.py:245
  89.6 0.7 collective-permute-done.2.other_ref
  90.4 0.1 broadcast_in_dim.7.col_norm_ref
  90.5 0.1 broadcast_in_dim.8.row_norm_ref
  90.6 0.0 copy-done.4
  90.6 0.0 copy-done.5
  90.6 13.0 %update.1 = f32[512,512]{1,0:T(8,128)} custom-call(s32[1,128]{1,0:T(1,128)S(1)} %bitcast.11, bf16[512,1024]{1,0:T(8,128)(2,1)S(1)} %copy-done.1, f32[512,128]{1,0:T(8,128)S(1)} %broadcast_in_dim.7.col_norm_ref, bf16[512,512]{1,0:T(8,128)(2,1)S(1)} %copy-done.4, bf16[512,512]{1,0:T(8,128)(2,1)} %collective-permute-done.1.rows_other_ref, ...), custom_call_target="tpu_custom_call" | custom-call | tf_op jit(solution)/shard_map/update/pallas_call | solution.py:253
  (4 shorter events, 0.1 us)
Async XLA Ops:
  0.0 1.2 %copy-start = (f32[512,512]{1,0:T(8,128)S(1)}, f32[512,512]{1,0:T(8,128)}, u32[]{:S(2)}) copy-start(f32[512,512]{1,0:T(8,128)} %param.8) | copy-start | bytes 3145732
  0.0 2.2 %copy-start.6 = (bf16[4,1024]{1,0:T(4,128)(2,1)S(1)}, bf16[4,1024]{1,0:T(4,128)(2,1)}, u32[]{:S(2)}) copy-start(bf16[4,1024]{1,0:T(4,128)(2,1)} %rows_ref.1) | copy-start | bytes 24580
  0.0 12.3 %copy-start.7 = (s32[128]{0:T(128)S(1)}, s32[128]{0:T(128)}, u32[]{:S(2)}) copy-start(s32[128]{0:T(128)} %param.5) | copy-start | bytes 1540
  2.4 10.0 %collective-permute-start = (bf16[1088,128]{1,0:T(8,128)(2,1)S(1)}, bf16[1088,128]{1,0:T(8,128)(2,1)S(1)}, u32[]{:S(2)}, u32[]{:S(2)}) collective-permute-start(bf16[1088,128]{1,0:T(8,128)(2,1)S(1)} %get-tuple-element.12), channel_id=1, source_target_pairs={{0,4},{4,0},{1,5},{5,1},{2,6},{6,2},{3,7},{7,3},{8,12},{12,8},{9,1... | collective-permute-start | bytes 835592 | tf_op jit(solution)/shard_map/ppermute | solution.py:279
  41.8 23.0 %all-to-all-start.1 = ((bf16[64,32,128]{2,1,0:T(8,128)(2,1)}), bf16[64,32,128]{2,1,0:T(8,128)(2,1)S(1)}, u32[]{:S(2)}, u32[]{:S(2)}) async-start(bf16[64,32,128]{2,1,0:T(8,128)(2,1)} %second_operand.1), calls=%async_computation.1 | async-start | bytes 1048576 | tf_op jit(solution)/shard_map/all_to_all | solution.py:283
  64.8 1.1 %copy-start.2 = (bf16[64,32,128]{2,1,0:T(8,128)(2,1)}, bf16[64,32,128]{2,1,0:T(8,128)(2,1)S(1)}, u32[]{:S(2)}) copy-start(bf16[64,32,128]{2,1,0:T(8,128)(2,1)S(1)} %all-to-all-done.1.came_ref) | copy-start | bytes 1572868
  66.0 14.4 %all-to-all-start.2 = ((bf16[4,1024,128]{2,1,0:T(8,128)(2,1)}), bf16[4,1024,128]{2,1,0:T(8,128)(2,1)S(1)}, u32[]{:S(2)}, u32[]{:S(2)}) async-start(bf16[4,1024,128]{2,1,0:T(8,128)(2,1)} %third_operand.1), calls=%async_computation.2 | async-start | bytes 2097152 | tf_op jit(solution)/shard_map/all_to_all | solution.py:284
  70.0 18.1 %copy-start.1 = (bf16[512,1024]{1,0:T(8,128)(2,1)S(1)}, bf16[512,1024]{1,0:T(8,128)(2,1)}, u32[]{:S(2)}) copy-start(bf16[512,1024]{1,0:T(8,128)(2,1)} %cols_ref.1) | copy-start | bytes 3145732
  71.3 8.0 %collective-permute-start.1 = (bf16[512,512]{1,0:T(8,128)(2,1)S(1)}, bf16[512,512]{1,0:T(8,128)(2,1)}, u32[]{:S(2)}, u32[]{:S(2)}) collective-permute-start(bf16[512,512]{1,0:T(8,128)(2,1)S(1)} %get-tuple-element.18.rows_own_ref), channel_id=1, source_target_pairs={{0,4},{4,0},{1,5},{5,1},{2,6},{6,2},{3,7},{7,3},{8,12},{12,8},{9,1... | collective-permute-start | bytes 1572872 | tf_op jit(solution)/shard_map/ppermute | solution.py:288
  77.6 0.8 copy-start.3
  80.4 10.2 %copy-start.4 = (bf16[512,512]{1,0:T(8,128)(2,1)S(1)}, bf16[512,512]{1,0:T(8,128)(2,1)}, u32[]{:S(2)}) copy-start(bf16[512,512]{1,0:T(8,128)(2,1)} %copy-done.3) | copy-start | bytes 1572868
  80.4 10.2 %copy-start.5 = (f32[512,512]{1,0:T(8,128)S(1)}, f32[512,512]{1,0:T(8,128)}, u32[]{:S(2)}) copy-start(f32[512,512]{1,0:T(8,128)} %trailing_ref.1) | copy-start | bytes 3145732
  80.4 10.0 %collective-permute-start.2 = (bf16[4,1024,128]{2,1,0:T(8,128)(2,1)S(1)}, bf16[4,1024,128]{2,1,0:T(8,128)(2,1)S(1)}, u32[]{:S(2)}, u32[]{:S(2)}) collective-permute-start(bf16[4,1024,128]{2,1,0:T(8,128)(2,1)S(1)} %all-to-all-done.2.mine_ref), channel_id=1, source_target_pairs={{0,4},{4,0},{1,5},{5,1},{2,6},{6,2},{3,7},{7,3},{8,12},{12,8},{9,1... | collective-permute-start | bytes 3145736 | tf_op jit(solution)/shard_map/ppermute | solution.py:290

commit v6 on v5

--- a/solution.py
+++ b/solution.py
@@ -10,7 +10,7 @@
 LAYERS = 3
 CORES = 2
 LANES = 128
-STEP = 64
+STEP = 128
 WIDE = (0.4999999720071538, -0.06830646500676399, 0.028277340639243406, -0.01566003030791659,
         0.008837209300279753, -0.003820798788545866, 0.0008313362870811599)
 NARROW = (0.4999769000530011, -0.06803611787881512, 0.026989768593852003, -0.012483028758839653,
@@ -57,11 +57,11 @@
 
 def prep_body(x_ref, inv_ref, rows_ref, kept_ref, sent_ref):
     core = lax.axis_index("core")
-    size, width = x_ref.shape
-    half, groups = width // CORES, inv_ref.shape[1] // LANES
-    rows = size // CORES
-    base = size * (half // LANES)
-    end = base + 2 * rows * groups
+    _, part, width = x_ref.shape
+    groups, inv_groups = width // LANES, inv_ref.shape[2] // LANES
+    base = part * groups
+    shift = base + part * inv_groups
+    end = shift + part * inv_groups
     count = rows_ref.shape[0]
     for out_ref in (kept_ref, sent_ref):
         out_ref[end:, :] = jnp.zeros((kept_ref.shape[0] - end, LANES), jnp.bfloat16)
@@ -69,21 +69,17 @@
 
             @pl.when(core == which)
             def _():
-                for i in range(width // LANES):
+                for i in range(groups):
                     to = end + CORES * count * i + count * which
                     out_ref[to : to + count, :] = rows_ref[:, LANES * i : LANES * (i + 1)]
 
     for out_ref, which in ((kept_ref, core), (sent_ref, 1 - core)):
-        for i in range(half // LANES):
-            at = pl.multiple_of(which * half + LANES * i, LANES)
-            out_ref[size * i : size * (i + 1), :] = x_ref[:, pl.ds(at, LANES)]
-    for out_ref, which in ((kept_ref, core), (sent_ref, 1 - core)):
         for i in range(groups):
-            at = pl.multiple_of(which * rows, rows)
-            high, low = split(inv_ref[pl.ds(at, rows), LANES * i : LANES * (i + 1)])
-            out_ref[base + rows * i : base + rows * (i + 1), :] = high
-            shift = base + rows * groups
-            out_ref[shift + rows * i : shift + rows * (i + 1), :] = low
+            out_ref[part * i : part * (i + 1), :] = x_ref[which, :, LANES * i : LANES * (i + 1)]
+        for i in range(inv_groups):
+            high, low = split(inv_ref[which, :, LANES * i : LANES * (i + 1)])
+            out_ref[base + part * i : base + part * (i + 1), :] = high
+            out_ref[shift + part * i : shift + part * (i + 1), :] = low
 
 
 VMEM = pl.BlockSpec(memory_space=pltpu.VMEM)
@@ -91,8 +87,7 @@
 
 
 def prep(x, inverse, rows):
-    size, width = x.shape
-    total = (width * size // CORES + 2 * inverse.size // CORES + CORES * rows.size) // LANES
+    total = (x.size // CORES + 2 * inverse.size // CORES + CORES * rows.size) // LANES
     out = jax.ShapeDtypeStruct((total, LANES), jnp.bfloat16)
     return pl.pallas_call(
         prep_body,
@@ -179,111 +174,174 @@
     )(came)
 
 
-def update_body(panel_ref, cols_ref, col_norm_ref, rows_own_ref, rows_other_ref, row_norm_ref, mine_ref, other_ref, trailing_ref, out_ref,
-                x_ref, high_ref, low_ref, left_ref, left_low_ref, right_ref, right_low_ref,
-                rows_ref, k_ref, k_low_ref, gram_ref, norm_ref, inv_ref):
-    size, width = cols_ref.shape
-    half = width // CORES
-    quarters = mine_ref.shape[0]
-    quarter = size // quarters
-    part = quarter // CORES
-    groups, inv_groups = half // LANES, size // LANES
+def triple(ref, rows, at, values, swapped):
+    high, low = split(values)
+    width = values.shape[1]
+    for i, part in enumerate((high, low, high) if swapped else (high, high, low)):
+        ref[rows, at + width * i : at + width * (i + 1)] = part
+
+
+def unpack(got_ref, x_ref, inverse_ref):
+    count, width = x_ref.shape
+    quarters = got_ref.shape[0]
+    part = count // quarters
+    groups, inv_groups = width // LANES, inverse_ref.shape[1] // (3 * LANES)
+    each = inv_groups // 2
+    for q in range(quarters):
+        to = slice(part * q, part * (q + 1))
+        for i in range(groups):
+            x_ref[to, LANES * i : LANES * (i + 1)] = got_ref[q, part * i : part * (i + 1), :]
+        for n in range(2):
+            for i in range(inv_groups):
+                at = part * (groups + n * inv_groups + i)
+                block = got_ref[q, at : at + part, :]
+                for place in (0, 2) if n == 0 else (1,):
+                    lane = LANES * (each * (3 * (i // each) + place) + i % each)
+                    inverse_ref[to, lane : lane + LANES] = block
+
+
+def kernel_half(x_ref, cols_ref, col_norm_ref, rows_own_ref, rows_other_ref, row_norm_ref, to_cols_ref, to_rows_ref,
+                gram_ref, norm_ref, inv_ref):
+    count, width = x_ref.shape
+    size, half = rows_own_ref.shape
     core = lax.axis_index("core")
-    for k, (got, which) in enumerate(((mine_ref, core), (other_ref, 1 - core))):
-        for q in range(quarters):
-            for i in range(groups):
-                at = pl.multiple_of(which * half + LANES * i, LANES)
-                x_ref[quarter * q : quarter * (q + 1), pl.ds(at, LANES)] = got[q, quarter * i : quarter * (i + 1), :]
-            to = (k * quarters + q) * part
-            for n, part_ref in enumerate((high_ref, low_ref)):
-                for i in range(inv_groups):
-                    base = quarter * groups + (n * inv_groups + i) * part
-                    part_ref[to : to + part, LANES * i : LANES * (i + 1)] = got[q, base : base + part, :]
-
-    for got, which in ((rows_own_ref, core), (rows_other_ref, 1 - core)):
-        rows_ref[:, pl.ds(pl.multiple_of(which * half, half), half)] = got[...]
-
     wide = x_ref[...].astype(jnp.float32)
-    norm_x = jnp.sqrt(jnp.sum(wide * wide, axis=1, keepdims=True) + 1e-06)
-    norm_x = jnp.broadcast_to(norm_x, (size, LANES)).T[:STEP]
-    norm_ref[...] = norm_x
-    inv_ref[...] = 1.0 / norm_x
-
-    for from_ref, from_norm_ref, to_ref, to_low_ref in (
-        (cols_ref, col_norm_ref, right_ref, right_low_ref),
-        (rows_ref, row_norm_ref, left_ref, left_low_ref),
-    ):
-        gram_ref[...] = dot_t(from_ref[...], x_ref[...])
+    norm = jnp.sqrt(jnp.sum(wide * wide, axis=1, keepdims=True) + 1e-06)
+    norm = jnp.broadcast_to(norm, (count, LANES)).T
+    norm_ref[...] = norm[:STEP]
+    inv_ref[...] = 1.0 / norm[:STEP]
+    own = pl.ds(pl.multiple_of(core * half, half), half)
+    theirs = pl.ds(pl.multiple_of((1 - core) * half, half), half)
+    for side, (from_norm_ref, to_ref) in enumerate(((col_norm_ref, to_cols_ref), (row_norm_ref, to_rows_ref))):
+        if side == 0:
+            gram_ref[...] = dot_t(cols_ref[...], x_ref[...])
+        else:
+            gram_ref[...] = dot_t(rows_own_ref[...], x_ref[:, own]) + dot_t(rows_other_ref[...], x_ref[:, theirs])
 
         @pl.loop(0, size // STEP)
         def _(i):
             at = pl.ds(pl.multiple_of(i * STEP, STEP), STEP)
-            norm = jnp.concatenate([from_norm_ref[at, :]] * (size // LANES), axis=1)
+            norm = jnp.concatenate([from_norm_ref[at, :]] * (count // LANES), axis=1)
             cosine = gram_ref[at, :] * (1.0 / norm) * inv_ref[...]
             values = layers(jnp.clip(cosine, -1.0, 1.0)) * (norm * norm_ref[...])
-            values, values_low = split(values)
-            k_ref[at, :] = values
-            k_low_ref[at, :] = values_low
-
-        solved = dot_t(k_ref[...], high_ref[...]) + (dot_t(k_ref[...], low_ref[...]) + dot_t(k_low_ref[...], high_ref[...]))
-        solved, solved_low = split(solved)
-        to_ref[...] = solved
-        to_low_ref[...] = solved_low
-
-    update = dot_t(left_ref[...], right_ref[...]) + (dot_t(left_ref[...], right_low_ref[...]) + dot_t(left_low_ref[...], right_ref[...]))
+            triple(to_ref, at, 0, values, False)
+
+
+def half_body(cols_ref, rows_own_ref, rows_other_ref, mine_hbm,
+              col_norm_ref, row_norm_ref, to_cols_ref, to_rows_ref, inverse_ref,
+              x_ref, gram_ref, norm_ref, inv_ref, mine_ref, sem):
+    copy = pltpu.make_async_copy(mine_hbm, mine_ref, sem)
+    copy.start()
+    for pieces, to_ref in (((cols_ref,), col_norm_ref), ((rows_own_ref, rows_other_ref), row_norm_ref)):
+
+        @pl.loop(0, to_ref.shape[0] // STEP)
+        def _(i):
+            at = pl.ds(pl.multiple_of(i * STEP, STEP), STEP)
+            total = 1e-06
+            for piece_ref in pieces:
+                wide = piece_ref[at, :].astype(jnp.float32)
+                total += jnp.sum(wide * wide, axis=1, keepdims=True)
+            to_ref[at, :] = jnp.broadcast_to(jnp.sqrt(total), (STEP, LANES))
+
+    copy.wait()
+    unpack(mine_ref, x_ref, inverse_ref)
+    kernel_half(x_ref, cols_ref, col_norm_ref, rows_own_ref, rows_other_ref, row_norm_ref, to_cols_ref, to_rows_ref,
+                gram_ref, norm_ref, inv_ref)
+
+
+def half_scratch(size, width):
+    count = size // CORES
+    return [pltpu.VMEM((count, width), jnp.bfloat16), pltpu.VMEM((size, count), jnp.float32)] + [
+        pltpu.VMEM((STEP, count), jnp.float32)
+    ] * 2
+
+
+def half_step(cols, rows_own, rows_other, mine):
+    size, width = cols.shape
+    values = jax.ShapeDtypeStruct((size, 3 * size // CORES), jnp.bfloat16)
+    norm = jax.ShapeDtypeStruct((size, LANES), jnp.float32)
+    return pl.pallas_call(
+        half_body,
+        in_specs=[VMEM] * 3 + [pl.BlockSpec(memory_space=pl.ANY)],
+        out_specs=[VMEM] * 5,
+        out_shape=[norm, norm, values, values, jax.ShapeDtypeStruct((size // CORES, 3 * size), jnp.bfloat16)],
+        scratch_shapes=half_scratch(size, width) + [pltpu.VMEM(mine.shape, mine.dtype), pltpu.SemaphoreType.DMA],
+        compiler_params=pltpu.CompilerParams(vmem_limit_bytes=9 * 2**20),
+        cost_estimate=pl.CostEstimate(
+            flops=2 * size * size * width, bytes_accessed=8 * 2**20, transcendentals=6 * size * size
+        ),
+        name="half_step",
+    )(cols, rows_own, rows_other, mine)
+
+
+def update_body(panel_ref, cols_ref, col_norm_ref, rows_own_ref, rows_other_ref, row_norm_ref, own_cols_ref, own_rows_ref,
+                own_inverse_ref, other_ref, trailing_ref, out_ref,
+                x_ref, gram_ref, norm_ref, inv_ref, other_cols_ref, other_rows_ref, other_inverse_ref,
+                k_cols_ref, k_rows_ref, inverse_ref, left_ref, right_ref):
+    count, thrice = other_inverse_ref.shape
+    core = lax.axis_index("core")
+    unpack(other_ref, x_ref, other_inverse_ref)
+    kernel_half(x_ref, cols_ref, col_norm_ref, rows_own_ref, rows_other_ref, row_norm_ref, other_cols_ref, other_rows_ref,
+                gram_ref, norm_ref, inv_ref)
+    each = thrice // 2
+    for which, cols_of, rows_of, inverse_of in (
+        (core, own_cols_ref, own_rows_ref, own_inverse_ref),
+        (1 - core, other_cols_ref, other_rows_ref, other_inverse_ref),
+    ):
+        lanes = pl.ds(pl.multiple_of(which * each, each), each)
+        k_cols_ref[:, lanes] = cols_of[...]
+        k_rows_ref[:, lanes] = rows_of[...]
+        inverse_ref[pl.ds(pl.multiple_of(which * count, count), count), :] = inverse_of[...]
+    for k_ref, to_ref, swapped in ((k_cols_ref, right_ref, True), (k_rows_ref, left_ref, False)):
+        every = slice(0, k_ref.shape[0])
+        triple(to_ref, every, 0, dot_t(k_ref[:, :each], inverse_ref[:count, :each]), swapped)
+        triple(to_ref, every, each, dot_t(k_ref[...], inverse_ref[count:, :]), swapped)
     blocks = panel_ref.shape[1]
     here = lax.broadcasted_iota(jnp.int32, (1, blocks), 1) == CORES * lax.axis_index("chip") + core
     own_rank = jnp.sum(jnp.where(here, panel_ref[...], 0).astype(jnp.float32))
     old = trailing_ref[...]
-    out_ref[...] = jnp.where(own_rank > blocks // 4, old - update, old)
-
-
-def norms(*pieces):
-    total = 1e-06
-    for piece in pieces:
-        wide = piece.astype(jnp.float32)
-        total += jnp.sum(wide * wide, axis=1, keepdims=True)
-    return jnp.broadcast_to(jnp.sqrt(total), (pieces[0].shape[0], LANES))
+    out_ref[...] = jnp.where(own_rank > blocks // 4, old - dot_t(left_ref[...], right_ref[...]), old)
 
 
 def update(panel, cols, rows_own, rows_other, mine, other, trailing):
     size, width = cols.shape
-    square = pltpu.VMEM((size, size), jnp.bfloat16)
-    vectors = pltpu.VMEM((size, width), jnp.bfloat16)
+    col_norm, row_norm, *own = half_step(cols, rows_own, rows_other, mine)
+    values = pltpu.VMEM((size, 3 * size // CORES), jnp.bfloat16)
+    whole = pltpu.VMEM((size, 3 * size), jnp.bfloat16)
     return pl.pallas_call(
         update_body,
-        in_specs=[VMEM] * 9,
+        in_specs=[VMEM] * 11,
         out_specs=VMEM,
         out_shape=jax.ShapeDtypeStruct(trailing.shape, trailing.dtype),
-        scratch_shapes=[vectors]
-        + [square] * 6
-        + [vectors]
-        + [square] * 2
-        + [pltpu.VMEM((size, size), jnp.float32)]
-        + [pltpu.VMEM((STEP, size), jnp.float32)] * 2,
+        scratch_shapes=half_scratch(size, width)
+        + [values] * 2
+        + [pltpu.VMEM((size // CORES, 3 * size), jnp.bfloat16)]
+        + [whole] * 5,
         compiler_params=pltpu.CompilerParams(vmem_limit_bytes=20 * 2**20),
         name="update",
-    )(panel, cols, norms(cols), rows_own, rows_other, norms(rows_own, rows_other), mine, other, trailing)
+    )(panel, cols, col_norm, rows_own, rows_other, row_norm, *own, other, trailing)
 
 
 def on_device(chips, row_count, panel, centres_cols, centres_rows, diag_inverse, trailing):
     size, width = centres_cols.shape
-    quarter = size // row_count
+    part = size // (CORES * row_count)
+    half = width // CORES
     row = lax.axis_index("row")
     panel = panel[None]
     swap = [(0, 1), (1, 0)]
 
-    x = lax.dynamic_slice_in_dim(centres_cols, row * quarter, quarter, 0)
-    inverse = lax.dynamic_slice_in_dim(diag_inverse, row * quarter, quarter, 0)
-    kept, sent = prep(x, inverse, centres_rows)
+    def parts(block):
+        return lax.dynamic_index_in_dim(block.reshape(CORES, row_count, part, -1), row, 1, keepdims=False)
+
+    kept, sent = prep(parts(centres_cols), parts(diag_inverse), centres_rows)
     got = lax.ppermute(sent, "core", swap)
-    per_chip = (2 * width * quarter // CORES) // (LANES * chips)
+    per_chip = part * (width + 2 * size) // (LANES * chips)
     outgoing, rows_later = first_operand(panel, kept, got, chips, per_chip)
     first = lax.all_to_all(outgoing, "chip", 0, 0)
     second = lax.all_to_all(second_operand(panel, first, rows_later), "chip", 0, 0)
     all_mine = lax.all_to_all(third_operand(second, row_count), "row", 0, 0)
 
-    tiles = [got_rows[:, i : i + 8] for got_rows in (first, second) for i in range(per_chip, 2 * per_chip, 8)]
+    tiles = [came[:, i : i + 8] for came in (first, second) for i in range(per_chip, 2 * per_chip, 8)]
     rows_own = jnp.concatenate([tile.reshape(size, LANES) for tile in tiles], axis=1)
     rows_other = lax.ppermute(rows_own, "core", swap)
     all_mine, rows_other = lax.optimization_barrier((all_mine, rows_other))

time: 104 us -> 104 us (level)
  other arithmetic: 1.72 us -> 0.06 us
  waiting for transfers between devices: 20.2 us -> 21.8 us
  Pallas kernels: 15.4 us -> 16.9 us
  local copies, waits for them, and re-layouts: 4.35 us -> 2.93 us
    reduce_sum x3 -> x0, other arithmetic: 1.7 us -> none  [norms(): total += jnp.sum(wide * wide, axis=1, keepdims=True)]
    all_to_all x1, waiting for transfers between devices: 1.11 us -> 2.77 us  [on_device(): all_mine = lax.all_to_all(third_operand(second, row_count), 'row', 0, 0)]
    pallas_call x1 -> x2, Pallas kernels: 13 us -> 14.6 us  [the longest x1 8.59 us: update(): pl.pallas_call(update_body, in_specs=[VMEM] * 11, out_specs=VMEM, out_sha...]
    reshape x2, local copies, waits for them, and re-layouts: 1.1 us -> 0.04 us  [on_device(): tile.reshape(size, LANES)]
  transfers between devices with their start and end apart: 5 -> 5, of which waited for: 5 -> 4; matrix products, arithmetic and copies ran while one was open for 3% -> 0% of each run, Pallas kernels for 0% -> 6%
where the time goes in v6:
time: 104 us
  starting transfers between devices  33.4 us (32%)
  blocking collectives  28.3 us (27%)
  waiting for transfers between devices  21.8 us (21%)
  Pallas kernels  16.9 us (16%)
  local copies, waits for them, and re-layouts  2.93 us (3%)
    all_to_all x1, blocking collectives, on_device(): first = lax.all_to_all(outgoing, 'chip', 0, 0)  28.3 us
    all_to_all x1, waiting for transfers between devices, on_device(): lax.all_to_all(second_operand(panel, first, rows_later), 'chip', 0, 0)  16.4 us
    ppermute x1, starting transfers between devices, on_device(): got = lax.ppermute(sent, 'core', swap)  8.78 us
    pallas_call x1, Pallas kernels, update(): pl.pallas_call(update_body, in_specs=[VMEM] * 11, out_specs=VMEM, out_sha...  8.59 us
    ppermute x1, starting transfers between devices, on_device(): all_other = lax.ppermute(all_mine, 'core', swap)  7.5 us
    all_to_all x1, starting transfers between devices, on_device(): lax.all_to_all(second_operand(panel, first, rows_later), 'chip', 0, 0)  6.62 us
    ppermute x1, starting transfers between devices, on_device(): rows_other = lax.ppermute(rows_own, 'core', swap)  6.23 us
    pallas_call x1, Pallas kernels, half_step(): pl.pallas_call(half_body, in_specs=[VMEM] * 3 + [pl.BlockSpec(memory_spac...  6.01 us
  transfers between devices with their start and end apart: 5, of which 4 were waited for; matrix products, arithmetic and copies ran while one was open for 0% of the time, Pallas kernels for 6%

profile of v6, /device:TPU:1, one launch (start us, length us, event | category | flops | bytes accessed | tf_op | source)
XLA Modules:
  0.0 103.6 jit_solution(11769091916168373477)
XLA Ops:
  0.0 0.0 copy-start
  0.0 1.2 %copy-done = f32[512,512]{1,0:T(8,128)S(1)} copy-done((f32[512,512]{1,0:T(8,128)S(1)}, f32[512,512]{1,0:T(8,128)}, u32[]{:S(2)}) %copy-start) | copy-done | bytes 1048600
  1.2 0.0 copy-start.3
  1.3 1.0 dynamic-slice_bitcast_fusion.1.x_ref
  2.2 0.0 copy-done.3
  2.3 0.1 prep.1
  2.4 8.8 %collective-permute-start = (bf16[1088,128]{1,0:T(8,128)(2,1)S(1)}, bf16[1088,128]{1,0:T(8,128)(2,1)S(1)}, u32[]{:S(2)}, u32[]{:S(2)}) collective-permute-start(bf16[1088,128]{1,0:T(8,128)(2,1)S(1)} %get-tuple-element.17), channel_id=1, source_target_pairs={{0,4},{4,0},{1,5},{5,1},{2,6},{6,2},{3,7},{7,3},{8,12},{12,8},{9,1... | collective-permute-start | bytes 835592 | tf_op jit(solution)/shard_map/ppermute | solution.py:337
  11.1 1.2 %collective-permute-done.got_ref = bf16[1088,128]{1,0:T(8,128)(2,1)S(1)} collective-permute-done((bf16[1088,128]{1,0:T(8,128)(2,1)S(1)}, bf16[1088,128]{1,0:T(8,128)(2,1)S(1)}, u32[]{:S(2)}, u32[]{:S(2)}) %collective-permute-start) | collective-permute-done | bytes 278560 | tf_op jit(solution)/shard_map/ppermute | solution.py:337
  12.3 0.0 copy-start.4
  12.3 0.7 copy-done.4
  13.0 0.2 first_operand.1
  13.2 28.3 %all_to_all.15.came_ref = bf16[64,32,128]{2,1,0:T(8,128)(2,1)S(1)} all-to-all(bf16[64,32,128]{2,1,0:T(8,128)(2,1)S(1)} %get-tuple-element.18), channel_id=1, replica_groups=mesh['chip'=64,'core'=2,'row'=4] {'chip'}, dimensions={0} | all-to-all | bytes 1048576 | tf_op jit(solution)/shard_map/all_to_all | solution.py:340
  41.5 1.0 second_operand.1
  42.4 6.6 %all-to-all-start.1 = ((bf16[64,32,128]{2,1,0:T(8,128)(2,1)}), bf16[64,32,128]{2,1,0:T(8,128)(2,1)S(1)}, u32[]{:S(2)}, u32[]{:S(2)}) async-start(bf16[64,32,128]{2,1,0:T(8,128)(2,1)} %second_operand.1), calls=%async_computation.1 | async-start | bytes 1048576 | tf_op jit(solution)/shard_map/all_to_all | solution.py:341
  49.1 16.4 %all-to-all-done.1.came_ref = bf16[64,32,128]{2,1,0:T(8,128)(2,1)S(1)} async-done(((bf16[64,32,128]{2,1,0:T(8,128)(2,1)}), bf16[64,32,128]{2,1,0:T(8,128)(2,1)S(1)}, u32[]{:S(2)}, u32[]{:S(2)}) %all-to-all-start.1) | async-done | bytes 524320 | tf_op jit(solution)/shard_map/all_to_all | solution.py:341
  65.5 1.1 %third_operand.1 = bf16[4,1024,128]{2,1,0:T(8,128)(2,1)} custom-call(bf16[64,32,128]{2,1,0:T(8,128)(2,1)S(1)} %all-to-all-done.1.came_ref), custom_call_target="tpu_custom_call" | custom-call | tf_op jit(solution)/shard_map/third_operand/pallas_call | solution.py:167
  66.6 4.2 %all-to-all-start.2 = ((bf16[4,1024,128]{2,1,0:T(8,128)(2,1)}), bf16[4,1024,128]{2,1,0:T(8,128)(2,1)}, u32[]{:S(2)}, u32[]{:S(2)}) async-start(bf16[4,1024,128]{2,1,0:T(8,128)(2,1)} %third_operand.1), calls=%async_computation.2 | async-start | bytes 2097152 | tf_op jit(solution)/shard_map/all_to_all | solution.py:342
  70.8 0.0 copy-start.1
  70.9 0.1 pad_maximum_fusion.rows_own_ref
  70.9 6.2 %collective-permute-start.1 = (bf16[512,512]{1,0:T(8,128)(2,1)S(1)}, bf16[512,512]{1,0:T(8,128)(2,1)S(1)}, u32[]{:S(2)}, u32[]{:S(2)}) collective-permute-start(bf16[512,512]{1,0:T(8,128)(2,1)S(1)} %pad_maximum_fusion.rows_own_ref), channel_id=1, source_target_pairs={{0,4},{4,0},{1,5},{5,1},{2,6},{6,2},{3,7},{7,3},{8,12},{12,8},{9,1... | collective-permute-start | bytes 1572872 | tf_op jit(solution)/shard_map/ppermute | solution.py:346
  77.2 1.5 %collective-permute-done.1.rows_other_ref = bf16[512,512]{1,0:T(8,128)(2,1)S(1)} collective-permute-done((bf16[512,512]{1,0:T(8,128)(2,1)S(1)}, bf16[512,512]{1,0:T(8,128)(2,1)S(1)}, u32[]{:S(2)}, u32[]{:S(2)}) %collective-permute-start.1) | collective-permute-done | bytes 524320 | tf_op jit(solution)/shard_map/ppermute | solution.py:346
  78.7 2.8 %all-to-all-done.2.mine_hbm = bf16[4,1024,128]{2,1,0:T(8,128)(2,1)} async-done(((bf16[4,1024,128]{2,1,0:T(8,128)(2,1)}), bf16[4,1024,128]{2,1,0:T(8,128)(2,1)}, u32[]{:S(2)}, u32[]{:S(2)}) %all-to-all-start.2) | async-done | bytes 1048608 | tf_op jit(solution)/shard_map/all_to_all | solution.py:342
  81.5 0.0 copy-start.2
  81.5 7.5 %collective-permute-start.2 = (bf16[4,1024,128]{2,1,0:T(8,128)(2,1)}, bf16[4,1024,128]{2,1,0:T(8,128)(2,1)S(1)}, u32[]{:S(2)}, u32[]{:S(2)}) collective-permute-start(bf16[4,1024,128]{2,1,0:T(8,128)(2,1)} %all-to-all-done.2.mine_hbm), channel_id=1, source_target_pairs={{0,4},{4,0},{1,5},{5,1},{2,6},{6,2},{3,7},{7,3},{8,12},{12,8},{9,1... | collective-permute-start | bytes 3145736 | tf_op jit(solution)/shard_map/ppermute | solution.py:348
  89.0 0.0 copy-done.1
  89.0 6.0 %half_step.1 = (f32[512,128]{1,0:T(8,128)S(1)}, f32[512,128]{1,0:T(8,128)S(1)}, bf16[512,768]{1,0:T(8,128)(2,1)S(1)}, bf16[512,768]{1,0:T(8,128)(2,1)S(1)}, bf16[256,1536]{1,0:T(8,128)(2,1)S(1)}) custom-call(bf16[512,1024]{1,0:T(8,128)(2,1)S(1)} %copy-done.1, bf16[512,512]{1,0:T(8,128)(2,1)S(1)} %pad_maximum_fusion.rows_own_ref, ...), custom_call_target="tpu_custom_call" | custom-call | flops 536870912 | bytes 8388608 | tf_op jit(solution)/shard_map/half_step/pallas_call | solution.py:263
  95.0 0.0 collective-permute-done.2.other_ref
  95.0 0.0 copy-done.2
  95.0 8.6 %update.1 = f32[512,512]{1,0:T(8,128)} custom-call(s32[1,128]{1,0:T(1,128)S(1)} %bitcast.23, bf16[512,1024]{1,0:T(8,128)(2,1)S(1)} %copy-done.1, f32[512,128]{1,0:T(8,128)S(1)} %get-tuple-element.22.col_norm_ref, bf16[512,512]{1,0:T(8,128)(2,1)S(1)} %pad_maximum_fusion.rows_own_ref, bf16[512,512]{1,0:T(8,128)(2,1)S(1)} %collective-permute-done.1.rows_other_ref, ...), custom_call_target="tpu_custom_call" | custom-call | tf_op jit(solution)/shard_map/update/pallas_call | solution.py:311
  (3 shorter events, 0.1 us)
Async XLA Ops:
  0.0 1.2 %copy-start = (f32[512,512]{1,0:T(8,128)S(1)}, f32[512,512]{1,0:T(8,128)}, u32[]{:S(2)}) copy-start(f32[512,512]{1,0:T(8,128)} %param.8) | copy-start | bytes 3145732
  1.2 1.0 copy-start.3
  2.4 10.0 %collective-permute-start = (bf16[1088,128]{1,0:T(8,128)(2,1)S(1)}, bf16[1088,128]{1,0:T(8,128)(2,1)S(1)}, u32[]{:S(2)}, u32[]{:S(2)}) collective-permute-start(bf16[1088,128]{1,0:T(8,128)(2,1)S(1)} %get-tuple-element.17), channel_id=1, source_target_pairs={{0,4},{4,0},{1,5},{5,1},{2,6},{6,2},{3,7},{7,3},{8,12},{12,8},{9,1... | collective-permute-start | bytes 835592 | tf_op jit(solution)/shard_map/ppermute | solution.py:337
  12.3 0.7 copy-start.4
  42.4 23.0 %all-to-all-start.1 = ((bf16[64,32,128]{2,1,0:T(8,128)(2,1)}), bf16[64,32,128]{2,1,0:T(8,128)(2,1)S(1)}, u32[]{:S(2)}, u32[]{:S(2)}) async-start(bf16[64,32,128]{2,1,0:T(8,128)(2,1)} %second_operand.1), calls=%async_computation.1 | async-start | bytes 1048576 | tf_op jit(solution)/shard_map/all_to_all | solution.py:341
  66.6 14.9 %all-to-all-start.2 = ((bf16[4,1024,128]{2,1,0:T(8,128)(2,1)}), bf16[4,1024,128]{2,1,0:T(8,128)(2,1)}, u32[]{:S(2)}, u32[]{:S(2)}) async-start(bf16[4,1024,128]{2,1,0:T(8,128)(2,1)} %third_operand.1), calls=%async_computation.2 | async-start | bytes 2097152 | tf_op jit(solution)/shard_map/all_to_all | solution.py:342
  70.8 18.1 %copy-start.1 = (bf16[512,1024]{1,0:T(8,128)(2,1)S(1)}, bf16[512,1024]{1,0:T(8,128)(2,1)}, u32[]{:S(2)}) copy-start(bf16[512,1024]{1,0:T(8,128)(2,1)} %cols_ref.3) | copy-start | bytes 3145732
  70.9 7.8 %collective-permute-start.1 = (bf16[512,512]{1,0:T(8,128)(2,1)S(1)}, bf16[512,512]{1,0:T(8,128)(2,1)S(1)}, u32[]{:S(2)}, u32[]{:S(2)}) collective-permute-start(bf16[512,512]{1,0:T(8,128)(2,1)S(1)} %pad_maximum_fusion.rows_own_ref), channel_id=1, source_target_pairs={{0,4},{4,0},{1,5},{5,1},{2,6},{6,2},{3,7},{7,3},{8,12},{12,8},{9,1... | collective-permute-start | bytes 1572872 | tf_op jit(solution)/shard_map/ppermute | solution.py:346
  81.5 13.6 %copy-start.2 = (f32[512,512]{1,0:T(8,128)S(1)}, f32[512,512]{1,0:T(8,128)}, u32[]{:S(2)}) copy-start(f32[512,512]{1,0:T(8,128)} %trailing_ref.1) | copy-start | bytes 3145732
  81.5 13.5 %collective-permute-start.2 = (bf16[4,1024,128]{2,1,0:T(8,128)(2,1)}, bf16[4,1024,128]{2,1,0:T(8,128)(2,1)S(1)}, u32[]{:S(2)}, u32[]{:S(2)}) collective-permute-start(bf16[4,1024,128]{2,1,0:T(8,128)(2,1)} %all-to-all-done.2.mine_hbm), channel_id=1, source_target_pairs={{0,4},{4,0},{1,5},{5,1},{2,6},{6,2},{3,7},{7,3},{8,12},{12,8},{9,1... | collective-permute-start | bytes 3145736 | tf_op jit(solution)/shard_map/ppermute | solution.py:348

commit v7 on v6

--- a/solution.py
+++ b/solution.py
@@ -106,30 +106,25 @@
     return jnp.sum(found).astype(jnp.int32)
 
 
-def first_body(panel_ref, kept_ref, got_ref, out_ref, later_ref):
-    chips, length, _ = out_ref.shape
-    per_chip = length // 2
-    total = chips * per_chip
+def first_body(panel_ref, kept_ref, got_ref, out_ref, rows_ref):
+    total = out_ref.shape[0] * out_ref.shape[1]
+    count = rows_ref.shape[0]
     core = lax.axis_index("core")
     kept = owner_of(panel_ref) % CORES == core
-    out_ref[:, :per_chip, :] = jnp.where(kept, kept_ref[:total], got_ref[:total]).reshape(chips, per_chip, LANES)
-    for n in range(2):
-        at = pl.ds(pl.multiple_of(total + (2 * core + n) * per_chip, per_chip), per_chip)
-        rows = (kept_ref[at, :].astype(jnp.float32) + got_ref[at, :].astype(jnp.float32)).astype(jnp.bfloat16)
-        if n == 0:
-            out_ref[:, per_chip:, :] = jnp.broadcast_to(rows[None], (chips, per_chip, LANES))
-        else:
-            later_ref[...] = rows
+    out_ref[...] = jnp.where(kept, kept_ref[:total], got_ref[:total]).reshape(out_ref.shape)
+    at = pl.ds(pl.multiple_of(total + core * count, count), count)
+    rows_ref[...] = (kept_ref[at, :].astype(jnp.float32) + got_ref[at, :].astype(jnp.float32)).astype(jnp.bfloat16)
 
 
 def first_operand(panel, kept, got, chips, per_chip):
+    count = (kept.shape[0] - chips * per_chip) // CORES
     return pl.pallas_call(
         first_body,
         in_specs=[VMEM, VMEM, VMEM],
         out_specs=[VMEM, VMEM],
         out_shape=[
-            jax.ShapeDtypeStruct((chips, 2 * per_chip, LANES), jnp.bfloat16),
-            jax.ShapeDtypeStruct((per_chip, LANES), jnp.bfloat16),
+            jax.ShapeDtypeStruct((chips, per_chip, LANES), jnp.bfloat16),
+            jax.ShapeDtypeStruct((count, LANES), jnp.bfloat16),
         ],
         compiler_params=SMALL,
         name="first_operand",
@@ -137,38 +132,37 @@
 
 
 def second_body(panel_ref, came_ref, rows_ref, out_ref):
-    chips, length, _ = out_ref.shape
-    per_chip = length // 2
-    piece = came_ref[owner_of(panel_ref) // CORES, :per_chip, :]
+    chips, per_chip, _ = came_ref.shape
+    piece = came_ref[owner_of(panel_ref) // CORES]
     out_ref[:, :per_chip, :] = jnp.broadcast_to(piece[None], (chips, per_chip, LANES))
-    out_ref[:, per_chip:, :] = jnp.broadcast_to(rows_ref[...][None], (chips, per_chip, LANES))
+    out_ref[:, per_chip:, :] = jnp.broadcast_to(rows_ref[...][None], (chips,) + rows_ref.shape)
 
 
 def second_operand(panel, came, rows):
+    chips, per_chip, _ = came.shape
     return pl.pallas_call(
         second_body,
         in_specs=[VMEM, VMEM, VMEM],
         out_specs=VMEM,
-        out_shape=jax.ShapeDtypeStruct(came.shape, came.dtype),
+        out_shape=jax.ShapeDtypeStruct((chips, per_chip + rows.shape[0], LANES), came.dtype),
         compiler_params=SMALL,
         name="second_operand",
     )(panel, came, rows)
 
 
 def third_body(came_ref, out_ref):
-    per_chip = came_ref.shape[1] // 2
+    per_chip = out_ref.shape[1] // came_ref.shape[0]
     piece = came_ref[:, :per_chip, :].reshape(out_ref.shape[1:])
     for q in range(out_ref.shape[0]):
         out_ref[q] = piece
 
 
-def third_operand(came, row_count):
-    chips, length, _ = came.shape
+def third_operand(came, row_count, per_chip):
     return pl.pallas_call(
         third_body,
         in_specs=[VMEM],
         out_specs=VMEM,
-        out_shape=jax.ShapeDtypeStruct((row_count, chips * length // 2, LANES), came.dtype),
+        out_shape=jax.ShapeDtypeStruct((row_count, came.shape[0] * per_chip, LANES), came.dtype),
         compiler_params=SMALL,
         name="third_operand",
     )(came)
@@ -336,12 +330,12 @@
     kept, sent = prep(parts(centres_cols), parts(diag_inverse), centres_rows)
     got = lax.ppermute(sent, "core", swap)
     per_chip = part * (width + 2 * size) // (LANES * chips)
-    outgoing, rows_later = first_operand(panel, kept, got, chips, per_chip)
+    outgoing, rows_chip = first_operand(panel, kept, got, chips, per_chip)
     first = lax.all_to_all(outgoing, "chip", 0, 0)
-    second = lax.all_to_all(second_operand(panel, first, rows_later), "chip", 0, 0)
-    all_mine = lax.all_to_all(third_operand(second, row_count), "row", 0, 0)
-
-    tiles = [came[:, i : i + 8] for came in (first, second) for i in range(per_chip, 2 * per_chip, 8)]
+    second = lax.all_to_all(second_operand(panel, first, rows_chip), "chip", 0, 0)
+    all_mine = lax.all_to_all(third_operand(second, row_count, per_chip), "row", 0, 0)
+
+    tiles = [second[:, i : i + 8] for i in range(per_chip, second.shape[1], 8)]
     rows_own = jnp.concatenate([tile.reshape(size, LANES) for tile in tiles], axis=1)
     rows_other = lax.ppermute(rows_own, "core", swap)
     all_mine, rows_other = lax.optimization_barrier((all_mine, rows_other))

time: 104 us -> 102 us (0.981)
  blocking collectives: 28.3 us -> 50.2 us
  waiting for transfers between devices: 21.8 us -> 4.52 us
  starting transfers between devices: 33.4 us -> 27.6 us
    all_to_all x0 -> x1, blocking collectives: none -> 26.4 us  [on_device(): lax.all_to_all(second_operand(panel, first, rows_chip), 'chip', 0, 0)]
    all_to_all x2 -> x1, waiting for transfers between devices: 19.2 us -> 1.84 us  [on_device(): lax.all_to_all(third_operand(second, row_count, per_chip), 'row', 0, 0)]
    all_to_all x2 -> x1, starting transfers between devices: 10.9 us -> 4.24 us  [on_device(): lax.all_to_all(third_operand(second, row_count, per_chip), 'row', 0, 0)]
    all_to_all x1, blocking collectives: 28.3 us -> 23.8 us  [on_device(): first = lax.all_to_all(outgoing, 'chip', 0, 0)]
  transfers between devices with their start and end apart: 5 -> 4, of which waited for: 4 -> 3; matrix products, arithmetic and copies ran while one was open for 0% -> 0% of each run, Pallas kernels for 6% -> 6%
where the time goes in v7:
time: 102 us
  blocking collectives  50.2 us (49%)
  starting transfers between devices  27.6 us (27%)
  Pallas kernels  16.2 us (16%)
  waiting for transfers between devices  4.52 us (4%)
  local copies, waits for them, and re-layouts  2.98 us (3%)
    all_to_all x1, blocking collectives, on_device(): lax.all_to_all(second_operand(panel, first, rows_chip), 'chip', 0, 0)  26.4 us
    all_to_all x1, blocking collectives, on_device(): first = lax.all_to_all(outgoing, 'chip', 0, 0)  23.8 us
    ppermute x1, starting transfers between devices, on_device(): got = lax.ppermute(sent, 'core', swap)  8.78 us
    pallas_call x1, Pallas kernels, update(): pl.pallas_call(update_body, in_specs=[VMEM] * 11, out_specs=VMEM, out_sha...  8.58 us
    ppermute x1, starting transfers between devices, on_device(): all_other = lax.ppermute(all_mine, 'core', swap)  7.93 us
    ppermute x1, starting transfers between devices, on_device(): rows_other = lax.ppermute(rows_own, 'core', swap)  6.66 us
    pallas_call x1, Pallas kernels, half_step(): pl.pallas_call(half_body, in_specs=[VMEM] * 3 + [pl.BlockSpec(memory_spac...  6.01 us
    all_to_all x1, starting transfers between devices, on_device(): lax.all_to_all(third_operand(second, row_count, per_chip), 'row', 0, 0)  4.24 us
  transfers between devices with their start and end apart: 4, of which 3 were waited for; matrix products, arithmetic and copies ran while one was open for 0% of the time, Pallas kernels for 6%

profile of v7, /device:TPU:1, one launch (start us, length us, event | category | flops | bytes accessed | tf_op | source)
XLA Modules:
  0.0 101.7 jit_solution(1483670801683616874)
XLA Ops:
  0.0 0.0 copy-start
  0.0 1.2 %copy-done = f32[512,512]{1,0:T(8,128)S(1)} copy-done((f32[512,512]{1,0:T(8,128)S(1)}, f32[512,512]{1,0:T(8,128)}, u32[]{:S(2)}) %copy-start) | copy-done | bytes 1048600
  1.2 0.0 copy-start.3
  1.3 1.0 dynamic-slice_bitcast_fusion.1.x_ref
  2.2 0.0 copy-done.3
  2.3 0.1 prep.1
  2.4 8.8 %collective-permute-start = (bf16[1088,128]{1,0:T(8,128)(2,1)S(1)}, bf16[1088,128]{1,0:T(8,128)(2,1)S(1)}, u32[]{:S(2)}, u32[]{:S(2)}) collective-permute-start(bf16[1088,128]{1,0:T(8,128)(2,1)S(1)} %get-tuple-element.17), channel_id=1, source_target_pairs={{0,4},{4,0},{1,5},{5,1},{2,6},{6,2},{3,7},{7,3},{8,12},{12,8},{9,1... | collective-permute-start | bytes 835592 | tf_op jit(solution)/shard_map/ppermute | solution.py:331
  11.1 1.2 %collective-permute-done.got_ref = bf16[1088,128]{1,0:T(8,128)(2,1)S(1)} collective-permute-done((bf16[1088,128]{1,0:T(8,128)(2,1)S(1)}, bf16[1088,128]{1,0:T(8,128)(2,1)S(1)}, u32[]{:S(2)}, u32[]{:S(2)}) %collective-permute-start) | collective-permute-done | bytes 278560 | tf_op jit(solution)/shard_map/ppermute | solution.py:331
  12.3 0.0 copy-start.4
  12.3 0.7 copy-done.4
  13.0 0.2 first_operand.1
  13.2 23.8 %all_to_all.15.came_ref = bf16[64,16,128]{2,1,0:T(8,128)(2,1)S(1)} all-to-all(bf16[64,16,128]{2,1,0:T(8,128)(2,1)S(1)} %get-tuple-element.18), channel_id=1, replica_groups=mesh['chip'=64,'core'=2,'row'=4] {'chip'}, dimensions={0} | all-to-all | bytes 524288 | tf_op jit(solution)/shard_map/all_to_all | solution.py:334
  36.9 0.2 second_operand.1
  37.1 26.4 %all_to_all.16.came_ref = bf16[64,48,128]{2,1,0:T(8,128)(2,1)S(1)} all-to-all(bf16[64,48,128]{2,1,0:T(8,128)(2,1)S(1)} %second_operand.1), channel_id=1, replica_groups=mesh['chip'=64,'core'=2,'row'=4] {'chip'}, dimensions={0} | all-to-all | bytes 1572864 | tf_op jit(solution)/shard_map/all_to_all | solution.py:335
  63.5 1.1 %third_operand.1 = bf16[4,1024,128]{2,1,0:T(8,128)(2,1)} custom-call(bf16[64,48,128]{2,1,0:T(8,128)(2,1)S(1)} %all_to_all.16.came_ref), custom_call_target="tpu_custom_call" | custom-call | tf_op jit(solution)/shard_map/third_operand/pallas_call | solution.py:161
  64.6 4.2 %all-to-all-start.2 = ((bf16[4,1024,128]{2,1,0:T(8,128)(2,1)}), bf16[4,1024,128]{2,1,0:T(8,128)(2,1)}, u32[]{:S(2)}, u32[]{:S(2)}) async-start(bf16[4,1024,128]{2,1,0:T(8,128)(2,1)} %third_operand.1), calls=%async_computation.2 | async-start | bytes 2097152 | tf_op jit(solution)/shard_map/all_to_all | solution.py:336
  68.9 0.0 copy-start.1
  68.9 0.1 slice_bitcast_fusion.3
  69.0 0.1 pad_maximum_fusion.rows_own_ref
  69.1 6.7 %collective-permute-start.1 = (bf16[512,512]{1,0:T(8,128)(2,1)S(1)}, bf16[512,512]{1,0:T(8,128)(2,1)S(1)}, u32[]{:S(2)}, u32[]{:S(2)}) collective-permute-start(bf16[512,512]{1,0:T(8,128)(2,1)S(1)} %pad_maximum_fusion.rows_own_ref), channel_id=1, source_target_pairs={{0,4},{4,0},{1,5},{5,1},{2,6},{6,2},{3,7},{7,3},{8,12},{12,8},{9,1... | collective-permute-start | bytes 1572872 | tf_op jit(solution)/shard_map/ppermute | solution.py:340
  75.7 1.5 %collective-permute-done.1.rows_other_ref = bf16[512,512]{1,0:T(8,128)(2,1)S(1)} collective-permute-done((bf16[512,512]{1,0:T(8,128)(2,1)S(1)}, bf16[512,512]{1,0:T(8,128)(2,1)S(1)}, u32[]{:S(2)}, u32[]{:S(2)}) %collective-permute-start.1) | collective-permute-done | bytes 524320 | tf_op jit(solution)/shard_map/ppermute | solution.py:340
  77.3 1.8 %all-to-all-done.2.mine_hbm = bf16[4,1024,128]{2,1,0:T(8,128)(2,1)} async-done(((bf16[4,1024,128]{2,1,0:T(8,128)(2,1)}), bf16[4,1024,128]{2,1,0:T(8,128)(2,1)}, u32[]{:S(2)}, u32[]{:S(2)}) %all-to-all-start.2) | async-done | bytes 1048608 | tf_op jit(solution)/shard_map/all_to_all | solution.py:336
  79.1 0.0 copy-start.2
  79.1 7.9 %collective-permute-start.2 = (bf16[4,1024,128]{2,1,0:T(8,128)(2,1)}, bf16[4,1024,128]{2,1,0:T(8,128)(2,1)S(1)}, u32[]{:S(2)}, u32[]{:S(2)}) collective-permute-start(bf16[4,1024,128]{2,1,0:T(8,128)(2,1)} %all-to-all-done.2.mine_hbm), channel_id=1, source_target_pairs={{0,4},{4,0},{1,5},{5,1},{2,6},{6,2},{3,7},{7,3},{8,12},{12,8},{9,1... | collective-permute-start | bytes 3145736 | tf_op jit(solution)/shard_map/ppermute | solution.py:342
  87.0 0.0 copy-done.1
  87.0 6.0 %half_step.1 = (f32[512,128]{1,0:T(8,128)S(1)}, f32[512,128]{1,0:T(8,128)S(1)}, bf16[512,768]{1,0:T(8,128)(2,1)S(1)}, bf16[512,768]{1,0:T(8,128)(2,1)S(1)}, bf16[256,1536]{1,0:T(8,128)(2,1)S(1)}) custom-call(bf16[512,1024]{1,0:T(8,128)(2,1)S(1)} %copy-done.1, bf16[512,512]{1,0:T(8,128)(2,1)S(1)} %pad_maximum_fusion.rows_own_ref, ...), custom_call_target="tpu_custom_call" | custom-call | flops 536870912 | bytes 8388608 | tf_op jit(solution)/shard_map/half_step/pallas_call | solution.py:257
  93.1 0.0 collective-permute-done.2.other_ref
  93.1 0.0 copy-done.2
  93.1 8.6 %update.1 = f32[512,512]{1,0:T(8,128)} custom-call(s32[1,128]{1,0:T(1,128)S(1)} %bitcast.23, bf16[512,1024]{1,0:T(8,128)(2,1)S(1)} %copy-done.1, f32[512,128]{1,0:T(8,128)S(1)} %get-tuple-element.22.col_norm_ref, bf16[512,512]{1,0:T(8,128)(2,1)S(1)} %pad_maximum_fusion.rows_own_ref, bf16[512,512]{1,0:T(8,128)(2,1)S(1)} %collective-permute-done.1.rows_other_ref, ...), custom_call_target="tpu_custom_call" | custom-call | tf_op jit(solution)/shard_map/update/pallas_call | solution.py:305
  (1 shorter events, 0.0 us)
Async XLA Ops:
  0.0 1.2 %copy-start = (f32[512,512]{1,0:T(8,128)S(1)}, f32[512,512]{1,0:T(8,128)}, u32[]{:S(2)}) copy-start(f32[512,512]{1,0:T(8,128)} %param.8) | copy-start | bytes 3145732
  1.2 1.0 copy-start.3
  2.4 10.0 %collective-permute-start = (bf16[1088,128]{1,0:T(8,128)(2,1)S(1)}, bf16[1088,128]{1,0:T(8,128)(2,1)S(1)}, u32[]{:S(2)}, u32[]{:S(2)}) collective-permute-start(bf16[1088,128]{1,0:T(8,128)(2,1)S(1)} %get-tuple-element.17), channel_id=1, source_target_pairs={{0,4},{4,0},{1,5},{5,1},{2,6},{6,2},{3,7},{7,3},{8,12},{12,8},{9,1... | collective-permute-start | bytes 835592 | tf_op jit(solution)/shard_map/ppermute | solution.py:331
  12.3 0.7 copy-start.4
  64.6 14.5 %all-to-all-start.2 = ((bf16[4,1024,128]{2,1,0:T(8,128)(2,1)}), bf16[4,1024,128]{2,1,0:T(8,128)(2,1)}, u32[]{:S(2)}, u32[]{:S(2)}) async-start(bf16[4,1024,128]{2,1,0:T(8,128)(2,1)} %third_operand.1), calls=%async_computation.2 | async-start | bytes 2097152 | tf_op jit(solution)/shard_map/all_to_all | solution.py:336
  68.9 18.1 %copy-start.1 = (bf16[512,1024]{1,0:T(8,128)(2,1)S(1)}, bf16[512,1024]{1,0:T(8,128)(2,1)}, u32[]{:S(2)}) copy-start(bf16[512,1024]{1,0:T(8,128)(2,1)} %cols_ref.3) | copy-start | bytes 3145732
  69.1 8.2 %collective-permute-start.1 = (bf16[512,512]{1,0:T(8,128)(2,1)S(1)}, bf16[512,512]{1,0:T(8,128)(2,1)S(1)}, u32[]{:S(2)}, u32[]{:S(2)}) collective-permute-start(bf16[512,512]{1,0:T(8,128)(2,1)S(1)} %pad_maximum_fusion.rows_own_ref), channel_id=1, source_target_pairs={{0,4},{4,0},{1,5},{5,1},{2,6},{6,2},{3,7},{7,3},{8,12},{12,8},{9,1... | collective-permute-start | bytes 1572872 | tf_op jit(solution)/shard_map/ppermute | solution.py:340
  79.1 14.0 %copy-start.2 = (f32[512,512]{1,0:T(8,128)S(1)}, f32[512,512]{1,0:T(8,128)}, u32[]{:S(2)}) copy-start(f32[512,512]{1,0:T(8,128)} %trailing_ref.1) | copy-start | bytes 3145732
  79.1 14.0 %collective-permute-start.2 = (bf16[4,1024,128]{2,1,0:T(8,128)(2,1)}, bf16[4,1024,128]{2,1,0:T(8,128)(2,1)S(1)}, u32[]{:S(2)}, u32[]{:S(2)}) collective-permute-start(bf16[4,1024,128]{2,1,0:T(8,128)(2,1)} %all-to-all-done.2.mine_hbm), channel_id=1, source_target_pairs={{0,4},{4,0},{1,5},{5,1},{2,6},{6,2},{3,7},{7,3},{8,12},{12,8},{9,1... | collective-permute-start | bytes 3145736 | tf_op jit(solution)/shard_map/ppermute | solution.py:342

commit v8 on v7

v8 whole, which is shorter than its diff:
```python
import math

import jax
import jax.numpy as jnp
from jax import lax
from jax.experimental import pallas as pl
from jax.experimental.pallas import tpu as pltpu
from jax.sharding import Mesh, PartitionSpec as P

LAYERS = 3
CORES = 2
LANES = 128
STEP = 64
WIDE = (0.4999999720071538, -0.06830646500676399, 0.028277340639243406, -0.01566003030791659,
        0.008837209300279753, -0.003820798788545866, 0.0008313362870811599)
NARROW = (0.4999769000530011, -0.06803611787881512, 0.026989768593852003, -0.012483028758839653,
          0.004564983607401579, -0.0008544733222650566)


def repeat_gather(piece, axis, count):
    return lax.all_to_all(jnp.broadcast_to(piece[None], (count,) + piece.shape), axis, 0, 0)


def split(values):
    high = values.astype(jnp.bfloat16)
    return high, (values - high.astype(jnp.float32)).astype(jnp.bfloat16)


def dot_t(left, right):
    return lax.dot_general(left, right, (((1,), (1,)), ((), ())), preferred_element_type=jnp.float32)


def poly(x, coefs):
    total = coefs[-1]
    for coef in coefs[-2::-1]:
        total = total * x + coef
    return total


def layers(rho):
    theta = rho
    for layer in range(LAYERS):
        size = jnp.abs(rho) if layer == 0 else rho
        rest = jnp.maximum(1.0 - size, 1e-30)
        below = rest * lax.rsqrt(rest)
        above = 1.0 + size
        above = above * lax.rsqrt(above) * (1.0 / math.pi)
        angle = below * poly(size, NARROW if layer == 2 else WIDE)
        zero_order = 1.0 - angle
        if layer == 0:
            zero_order = jnp.where(rho < 0.0, angle, zero_order)
        rho_next = below * above + zero_order * rho
        theta = theta * zero_order + rho_next
        rho = rho_next
    return theta


def prep_body(panel_ref, x_ref, inv_ref, rows_ref, kept_ref, sent_ref):
    core = lax.axis_index("core")
    size, width = x_ref.shape
    half, groups = width // CORES, inv_ref.shape[1] // LANES
    rows = size // CORES
    base = size * (half // LANES)
    end = base + 2 * rows * groups
    count = rows_ref.shape[0]
    for out_ref in (kept_ref, sent_ref):
        out_ref[end:, :] = jnp.zeros((kept_ref.shape[0] - end, LANES), jnp.bfloat16)
        for which in range(CORES):

            @pl.when(core == which)
            def _():
                for i in range(width // LANES):
                    to = end + CORES * count * i + count * which
                    out_ref[to : to + count, :] = rows_ref[:, LANES * i : LANES * (i + 1)]

    for out_ref, which in ((kept_ref, core), (sent_ref, 1 - core)):
        for i in range(half // LANES):
            at = pl.multiple_of(which * half + LANES * i, LANES)
            out_ref[size * i : size * (i + 1), :] = x_ref[:, pl.ds(at, LANES)]
    for out_ref, which in ((kept_ref, core), (sent_ref, 1 - core)):
        for i in range(groups):
            at = pl.multiple_of(which * rows, rows)
            high, low = split(inv_ref[pl.ds(at, rows), LANES * i : LANES * (i + 1)])
            out_ref[base + rows * i : base + rows * (i + 1), :] = high
            shift = base + rows * groups
            out_ref[shift + rows * i : shift + rows * (i + 1), :] = low


VMEM = pl.BlockSpec(memory_space=pltpu.VMEM)
SMALL = pltpu.CompilerParams(vmem_limit_bytes=4 * 2**20)


def prep(panel, x, inverse, rows):
    size, width = x.shape
    total = (width * size // CORES + 2 * inverse.size // CORES + CORES * rows.size) // LANES
    out = jax.ShapeDtypeStruct((total, LANES), jnp.bfloat16)
    return pl.pallas_call(
        prep_body,
        in_specs=[VMEM] * 4,
        out_specs=[VMEM, VMEM],
        out_shape=[out, out],
        compiler_params=SMALL,
        name="prep",
    )(panel, x, inverse, rows)


def owner_of(panel_ref):
    blocks = panel_ref.shape[1]
    at = lax.broadcasted_iota(jnp.int32, (1, blocks), 1)
    found = jnp.where(panel_ref[...] == blocks // 4, at, 0).astype(jnp.float32)
    return jnp.sum(found).astype(jnp.int32)


def first_body(panel_ref, kept_ref, got_ref, out_ref, rows_ref):
    total = out_ref.shape[0] * out_ref.shape[1]
    count = rows_ref.shape[0]
    core = lax.axis_index("core")
    kept = owner_of(panel_ref) % CORES == core
    out_ref[...] = jnp.where(kept, kept_ref[:total], got_ref[:total]).reshape(out_ref.shape)
    at = pl.ds(pl.multiple_of(total + core * count, count), count)
    rows_ref[...] = (kept_ref[at, :].astype(jnp.float32) + got_ref[at, :].astype(jnp.float32)).astype(jnp.bfloat16)


def first_operand(panel, kept, got, chips, per_chip):
    count = (kept.shape[0] - chips * per_chip) // CORES
    return pl.pallas_call(
        first_body,
        in_specs=[VMEM, VMEM, VMEM],
        out_specs=[VMEM, VMEM],
        out_shape=[
            jax.ShapeDtypeStruct((chips, per_chip, LANES), jnp.bfloat16),
            jax.ShapeDtypeStruct((count, LANES), jnp.bfloat16),
        ],
        compiler_params=SMALL,
        name="first_operand",
    )(panel, kept, got)


def second_body(panel_ref, came_ref, rows_ref, out_ref):
    chips, per_chip, _ = came_ref.shape
    piece = came_ref[owner_of(panel_ref) // CORES]
    out_ref[:, :per_chip, :] = jnp.broadcast_to(piece[None], (chips, per_chip, LANES))
    out_ref[:, per_chip:, :] = jnp.broadcast_to(rows_ref[...][None], (chips,) + rows_ref.shape)


def second_operand(panel, came, rows):
    chips, per_chip, _ = came.shape
    return pl.pallas_call(
        second_body,
        in_specs=[VMEM, VMEM, VMEM],
        out_specs=VMEM,
        out_shape=jax.ShapeDtypeStruct((chips, per_chip + rows.shape[0], LANES), came.dtype),
        compiler_params=SMALL,
        name="second_operand",
    )(panel, came, rows)


def third_body(came_ref, out_ref):
    per_chip = out_ref.shape[1] // came_ref.shape[0]
    piece = came_ref[:, :per_chip, :].reshape(out_ref.shape[1:])
    for q in range(out_ref.shape[0]):
        out_ref[q] = piece


def third_operand(came, row_count, per_chip):
    return pl.pallas_call(
        third_body,
        in_specs=[VMEM],
        out_specs=VMEM,
        out_shape=jax.ShapeDtypeStruct((row_count, came.shape[0] * per_chip, LANES), came.dtype),
        compiler_params=SMALL,
        name="third_operand",
    )(came)


def triple(ref, rows, at, values, swapped):
    high, low = split(values)
    width = values.shape[1]
    for i, part in enumerate((high, low, high) if swapped else (high, high, low)):
        ref[rows, at + width * i : at + width * (i + 1)] = part


def unpack(got_ref, x_ref, inverse_ref, places):
    quarters = got_ref.shape[0]
    size, half = x_ref.shape
    quarter = size // quarters
    part = quarter // CORES
    groups, inv_groups = half // LANES, size // LANES
    each = inv_groups // 2
    for q in range(quarters):
        for i in range(groups):
            x_ref[quarter * q : quarter * (q + 1), LANES * i : LANES * (i + 1)] = got_ref[q, quarter * i : quarter * (i + 1), :]
        to = places[q]
        for n in range(2):
            for i in range(inv_groups):
                at = quarter * groups + (n * inv_groups + i) * part
                block = got_ref[q, at : at + part, :]
                for place in (0, 2) if n == 0 else (1,):
                    lane = LANES * (inv_groups * place + i)
                    inverse_ref[to : to + part, lane : lane + LANES] = block


def squares(x_ref):
    wide = x_ref[...].astype(jnp.float32)
    total = jnp.sum(wide * wide, axis=1, keepdims=True)
    return jnp.broadcast_to(total, (x_ref.shape[0], LANES)).T[:8]


def half_body(cols_ref, rows_own_ref, rows_other_ref, mine_hbm,
              col_norm_ref, row_norm_ref, gram_cols_ref, gram_rows_ref, square_ref, inverse_ref,
              x_ref, mine_ref, sem):
    copy = pltpu.make_async_copy(mine_hbm, mine_ref, sem)
    copy.start()
    for pieces, to_ref in (((cols_ref,), col_norm_ref), ((rows_own_ref, rows_other_ref), row_norm_ref)):

        @pl.loop(0, to_ref.shape[0] // LANES)
        def _(i):
            at = pl.ds(pl.multiple_of(i * LANES, LANES), LANES)
            total = 1e-06
            for piece_ref in pieces:
                wide = piece_ref[at, :].astype(jnp.float32)
                total += jnp.sum(wide * wide, axis=1, keepdims=True)
            to_ref[at, :] = jnp.broadcast_to(jnp.sqrt(total), (LANES, LANES))

    copy.wait()
    half, count = x_ref.shape[1], inverse_ref.shape[0]
    quarters = mine_ref.shape[0]
    unpack(mine_ref, x_ref, inverse_ref, [count // quarters * q for q in range(quarters)])
    own = pl.ds(pl.multiple_of(lax.axis_index("core") * half, half), half)
    gram_cols_ref[...] = dot_t(cols_ref[:, own], x_ref[...])
    gram_rows_ref[...] = dot_t(rows_own_ref[...], x_ref[...])
    square_ref[...] = squares(x_ref)


def half_step(cols, rows_own, rows_other, mine):
    size, width = cols.shape
    norm = jax.ShapeDtypeStruct((size, LANES), jnp.float32)
    square = jax.ShapeDtypeStruct((size, size), jnp.float32)
    return pl.pallas_call(
        half_body,
        in_specs=[VMEM] * 3 + [pl.BlockSpec(memory_space=pl.ANY)],
        out_specs=[VMEM] * 6,
        out_shape=[
            norm,
            norm,
            square,
            square,
            jax.ShapeDtypeStruct((8, size), jnp.float32),
            jax.ShapeDtypeStruct((size // CORES, 3 * size), jnp.bfloat16),
        ],
        scratch_shapes=[
            pltpu.VMEM((size, width // CORES), jnp.bfloat16),
            pltpu.VMEM(mine.shape, mine.dtype),
            pltpu.SemaphoreType.DMA,
        ],
        compiler_params=pltpu.CompilerParams(vmem_limit_bytes=9 * 2**20),
        cost_estimate=pl.CostEstimate(
            flops=4 * size * size * (width // CORES), bytes_accessed=8 * 2**20, transcendentals=0
        ),
        name="half_step",
    )(cols, rows_own, rows_other, mine)


def update_body(panel_ref, cols_ref, col_norm_ref, rows_ref, row_norm_ref, gram_cols_ref, gram_rows_ref, square_ref,
                inverse_own_ref, other_ref, trailing_ref, out_ref,
                x_ref, inverse_ref, gram_ref, gram_sum_ref, norm_ref, inv_ref, k_cols_ref, k_rows_ref, left_ref, right_ref):
    size, half = x_ref.shape
    core = lax.axis_index("core")
    quarters, count = other_ref.shape[0], inverse_own_ref.shape[0]
    pair, part = count // 2, count // quarters
    unpack(other_ref, x_ref, inverse_ref, [count * (q // 2) + pair + part * (q % 2) for q in range(quarters)])
    for n in range(2):
        inverse_ref[count * n : count * n + pair, :] = inverse_own_ref[pair * n : pair * (n + 1), :]
    norm = jnp.sqrt(square_ref[...] + squares(x_ref) + 1e-06)
    norm_ref[...] = jnp.concatenate([norm] * (STEP // 8), axis=0)
    inv_ref[...] = jnp.concatenate([1.0 / norm] * (STEP // 8), axis=0)

    def values_of(gram, from_norm, to_ref, at):
        norm = jnp.concatenate([from_norm] * (size // LANES), axis=1)
        cosine = gram * (1.0 / norm) * inv_ref[...]
        values = layers(jnp.clip(cosine, -1.0, 1.0)) * (norm * norm_ref[...])
        triple(to_ref, at, 0, values, False)

    theirs = pl.ds(pl.multiple_of((1 - core) * half, half), half)
    gram_ref[...] = gram_cols_ref[...] + dot_t(cols_ref[:, theirs], x_ref[...])
    n_steps = size // STEP

    def block(i, extent):
        return pl.ds(pl.multiple_of(i * extent, extent), extent)

    gram_sum_ref[...] = gram_rows_ref[...] + dot_t(rows_ref[...], x_ref[...])

    for gram, from_norm, k_ref, to_ref, swapped in (
        (gram_ref, col_norm_ref, k_cols_ref, right_ref, True),
        (gram_sum_ref, row_norm_ref, k_rows_ref, left_ref, False),
    ):

        @pl.loop(0, n_steps)
        def _(i):
            at = block(i, STEP)
            values_of(gram[at, :], from_norm[at, :], k_ref, at)

        triple(to_ref, slice(0, size), 0, dot_t(k_ref[...], inverse_ref[...]), swapped)

    blocks = panel_ref.shape[1]
    here = lax.broadcasted_iota(jnp.int32, (1, blocks), 1) == CORES * lax.axis_index("chip") + core
    own_rank = jnp.sum(jnp.where(here, panel_ref[...], 0).astype(jnp.float32))
    old = trailing_ref[...]
    out_ref[...] = jnp.where(own_rank > blocks // 4, old - dot_t(left_ref[...], right_ref[...]), old)


def update(panel, cols, rows_own, rows_other, mine, other, trailing):
    size, width = cols.shape
    col_norm, row_norm, gram_cols, gram_rows, square, inverse_own = half_step(cols, rows_own, rows_other, mine)
    thrice = pltpu.VMEM((size, 3 * size), jnp.bfloat16)
    lanes = pltpu.VMEM((STEP, size), jnp.float32)
    return pl.pallas_call(
        update_body,
        in_specs=[VMEM] * 11,
        out_specs=VMEM,
        out_shape=jax.ShapeDtypeStruct(trailing.shape, trailing.dtype),
        scratch_shapes=[pltpu.VMEM((size, width // CORES), jnp.bfloat16), thrice]
        + [pltpu.VMEM((size, size), jnp.float32)] * 2
        + [lanes] * 2
        + [thrice] * 4,
        compiler_params=pltpu.CompilerParams(vmem_limit_bytes=22 * 2**20),
        name="update",
    )(panel, cols, col_norm, rows_other, row_norm, gram_cols, gram_rows, square, inverse_own,
      other, trailing)


def on_device(chips, row_count, panel, centres_cols, centres_rows, diag_inverse, trailing):
    size, width = centres_cols.shape
    quarter = size // row_count
    row = lax.axis_index("row")
    panel = panel[None]
    swap = [(0, 1), (1, 0)]

    x = lax.dynamic_slice_in_dim(centres_cols, row * quarter, quarter, 0)
    inverse = lax.dynamic_slice_in_dim(diag_inverse, row * quarter, quarter, 0)
    kept, sent = prep(panel, x, inverse, centres_rows)
    got = lax.ppermute(sent, "core", swap)
    per_chip = (2 * width * quarter // CORES) // (LANES * chips)
    outgoing, rows_chip = first_operand(panel, kept, got, chips, per_chip)
    first = lax.all_to_all(outgoing, "chip", 0, 0)
    second = lax.all_to_all(second_operand(panel, first, rows_chip), "chip", 0, 0)
    all_mine = lax.all_to_all(third_operand(second, row_count, per_chip), "row", 0, 0)

    tiles = [second[:, i : i + 8] for i in range(per_chip, second.shape[1], 8)]
    rows_own = jnp.concatenate([tile.reshape(size, LANES) for tile in tiles], axis=1)
    rows_other = lax.ppermute(rows_own, "core", swap)
    all_mine, rows_other = lax.optimization_barrier((all_mine, rows_other))
    all_other = lax.ppermute(all_mine, "core", swap)
    return update(panel, centres_cols, rows_own, rows_other, all_mine, all_other, trailing)


def solution(mesh):
    col_count, row_count = mesh.devices.shape
    chips = col_count // CORES
    fine = Mesh(mesh.devices.reshape(chips, CORES, row_count), ("chip", "core", "row"))

    def step(*arrays):
        return on_device(chips, row_count, *arrays)

    col = ("chip", "core")
    return jax.shard_map(
        step,
        mesh=fine,
        in_specs=(P(), P(col, None), P(("row",) + col, None), P(col, None), P("row", col)),
        out_specs=P("row", col),
        check_vma=False,
    )
```

time: 102 us -> 101 us (level)
  Pallas kernels: 16.2 us -> 14.8 us
    pallas_call x1, Pallas kernels: 6.01 us -> 2.12 us  [half_step(): pl.pallas_call(half_body, in_specs=[VMEM] * 3 + [pl.BlockSpec(memory_spac...]
    pallas_call x1, Pallas kernels: 8.58 us -> 11.1 us  [update(): pl.pallas_call(update_body, in_specs=[VMEM] * 11, out_specs=VMEM, out_sha...]
  transfers between devices with their start and end apart: 4 -> 4, of which waited for: 3 -> 4; matrix products, arithmetic and copies ran while one was open for 0% -> 0% of each run, Pallas kernels for 6% -> 2%
where the time goes in v8:
time: 101 us
  blocking collectives  50.2 us (50%)
  starting transfers between devices  27.6 us (27%)
  Pallas kernels  14.8 us (15%)
  waiting for transfers between devices  4.86 us (5%)
  local copies, waits for them, and re-layouts  2.97 us (3%)
    all_to_all x1, blocking collectives, on_device(): lax.all_to_all(second_operand(panel, first, rows_chip), 'chip', 0, 0)  26.4 us
    all_to_all x1, blocking collectives, on_device(): first = lax.all_to_all(outgoing, 'chip', 0, 0)  23.8 us
    pallas_call x1, Pallas kernels, update(): pl.pallas_call(update_body, in_specs=[VMEM] * 11, out_specs=VMEM, out_sha...  11.1 us
    ppermute x1, starting transfers between devices, on_device(): got = lax.ppermute(sent, 'core', swap)  8.78 us
    ppermute x1, starting transfers between devices, on_device(): all_other = lax.ppermute(all_mine, 'core', swap)  7.93 us
    ppermute x1, starting transfers between devices, on_device(): rows_other = lax.ppermute(rows_own, 'core', swap)  6.66 us
    all_to_all x1, starting transfers between devices, on_device(): lax.all_to_all(third_operand(second, row_count, per_chip), 'row', 0, 0)  4.24 us
    pallas_call x1, Pallas kernels, half_step(): pl.pallas_call(half_body, in_specs=[VMEM] * 3 + [pl.BlockSpec(memory_spac...  2.12 us
  transfers between devices with their start and end apart: 4, of which 4 were waited for; matrix products, arithmetic and copies ran while one was open for 0% of the time, Pallas kernels for 2%

profile of v8, /device:TPU:1, one launch (start us, length us, event | category | flops | bytes accessed | tf_op | source)
XLA Modules:
  0.0 100.6 jit_solution(12528457654099131353)
XLA Ops:
  0.0 0.0 copy-start
  0.0 1.2 %copy-done = f32[512,512]{1,0:T(8,128)S(1)} copy-done((f32[512,512]{1,0:T(8,128)S(1)}, f32[512,512]{1,0:T(8,128)}, u32[]{:S(2)}) %copy-start) | copy-done | bytes 1048600
  1.2 0.0 copy-start.3
  1.3 1.0 constant_dynamic-slice_fusion.1.x_ref
  2.2 0.0 copy-start.4
  2.2 0.0 copy-done.3
  2.3 0.6 copy-done.4
  2.9 0.1 prep.1
  3.0 8.8 %collective-permute-start = (bf16[1088,128]{1,0:T(8,128)(2,1)S(1)}, bf16[1088,128]{1,0:T(8,128)(2,1)S(1)}, u32[]{:S(2)}, u32[]{:S(2)}) collective-permute-start(bf16[1088,128]{1,0:T(8,128)(2,1)S(1)} %get-tuple-element.18), channel_id=1, source_target_pairs={{0,4},{4,0},{1,5},{5,1},{2,6},{6,2},{3,7},{7,3},{8,12},{12,8},{9,1... | collective-permute-start | bytes 835592 | tf_op jit(solution)/shard_map/ppermute | solution.py:342
  11.8 1.2 %collective-permute-done.got_ref = bf16[1088,128]{1,0:T(8,128)(2,1)S(1)} collective-permute-done((bf16[1088,128]{1,0:T(8,128)(2,1)S(1)}, bf16[1088,128]{1,0:T(8,128)(2,1)S(1)}, u32[]{:S(2)}, u32[]{:S(2)}) %collective-permute-start) | collective-permute-done | bytes 278560 | tf_op jit(solution)/shard_map/ppermute | solution.py:342
  13.0 0.2 first_operand.1
  13.2 23.8 %all_to_all.15.came_ref = bf16[64,16,128]{2,1,0:T(8,128)(2,1)S(1)} all-to-all(bf16[64,16,128]{2,1,0:T(8,128)(2,1)S(1)} %get-tuple-element.19), channel_id=1, replica_groups=mesh['chip'=64,'core'=2,'row'=4] {'chip'}, dimensions={0} | all-to-all | bytes 524288 | tf_op jit(solution)/shard_map/all_to_all | solution.py:345
  36.9 0.2 second_operand.1
  37.1 26.4 %all_to_all.16.came_ref = bf16[64,48,128]{2,1,0:T(8,128)(2,1)S(1)} all-to-all(bf16[64,48,128]{2,1,0:T(8,128)(2,1)S(1)} %second_operand.1), channel_id=1, replica_groups=mesh['chip'=64,'core'=2,'row'=4] {'chip'}, dimensions={0} | all-to-all | bytes 1572864 | tf_op jit(solution)/shard_map/all_to_all | solution.py:346
  63.5 1.1 %third_operand.1 = bf16[4,1024,128]{2,1,0:T(8,128)(2,1)} custom-call(bf16[64,48,128]{2,1,0:T(8,128)(2,1)S(1)} %all_to_all.16.came_ref), custom_call_target="tpu_custom_call" | custom-call | tf_op jit(solution)/shard_map/third_operand/pallas_call | solution.py:166
  64.6 4.2 %all-to-all-start.2 = ((bf16[4,1024,128]{2,1,0:T(8,128)(2,1)}), bf16[4,1024,128]{2,1,0:T(8,128)(2,1)}, u32[]{:S(2)}, u32[]{:S(2)}) async-start(bf16[4,1024,128]{2,1,0:T(8,128)(2,1)} %third_operand.1), calls=%async_computation.2 | async-start | bytes 2097152 | tf_op jit(solution)/shard_map/all_to_all | solution.py:347
  68.9 0.0 copy-start.1
  68.9 0.1 slice_bitcast_fusion.3
  69.0 0.1 pad_maximum_fusion.rows_own_ref
  69.1 6.7 %collective-permute-start.1 = (bf16[512,512]{1,0:T(8,128)(2,1)S(1)}, bf16[512,512]{1,0:T(8,128)(2,1)S(1)}, u32[]{:S(2)}, u32[]{:S(2)}) collective-permute-start(bf16[512,512]{1,0:T(8,128)(2,1)S(1)} %pad_maximum_fusion.rows_own_ref), channel_id=1, source_target_pairs={{0,4},{4,0},{1,5},{5,1},{2,6},{6,2},{3,7},{7,3},{8,12},{12,8},{9,1... | collective-permute-start | bytes 1572872 | tf_op jit(solution)/shard_map/ppermute | solution.py:351
  75.7 1.5 %collective-permute-done.1.rows_other_ref.rows_ref = bf16[512,512]{1,0:T(8,128)(2,1)S(1)} collective-permute-done((bf16[512,512]{1,0:T(8,128)(2,1)S(1)}, bf16[512,512]{1,0:T(8,128)(2,1)S(1)}, u32[]{:S(2)}, u32[]{:S(2)}) %collective-permute-start.1) | collective-permute-done | bytes 524320 | tf_op jit(solution)/shard_map/ppermute | solution.py:351
  77.3 1.8 %all-to-all-done.2.mine_hbm = bf16[4,1024,128]{2,1,0:T(8,128)(2,1)} async-done(((bf16[4,1024,128]{2,1,0:T(8,128)(2,1)}), bf16[4,1024,128]{2,1,0:T(8,128)(2,1)}, u32[]{:S(2)}, u32[]{:S(2)}) %all-to-all-start.2) | async-done | bytes 1048608 | tf_op jit(solution)/shard_map/all_to_all | solution.py:347
  79.1 0.0 copy-start.2
  79.1 7.9 %collective-permute-start.2 = (bf16[4,1024,128]{2,1,0:T(8,128)(2,1)}, bf16[4,1024,128]{2,1,0:T(8,128)(2,1)S(1)}, u32[]{:S(2)}, u32[]{:S(2)}) collective-permute-start(bf16[4,1024,128]{2,1,0:T(8,128)(2,1)} %all-to-all-done.2.mine_hbm), channel_id=1, source_target_pairs={{0,4},{4,0},{1,5},{5,1},{2,6},{6,2},{3,7},{7,3},{8,12},{12,8},{9,1... | collective-permute-start | bytes 3145736 | tf_op jit(solution)/shard_map/ppermute | solution.py:353
  87.0 0.0 copy-done.1
  87.0 2.1 %half_step.1 = (f32[512,128]{1,0:T(8,128)S(1)}, f32[512,128]{1,0:T(8,128)S(1)}, f32[512,512]{1,0:T(8,128)S(1)}, f32[512,512]{1,0:T(8,128)S(1)}, f32[8,512]{1,0:T(8,128)S(1)}, /*index=5*/bf16[256,1536]{1,0:T(8,128)(2,1)S(1)}) custom-call(bf16[512,1024]{1,0:T(8,128)(2,1)S(1)} %copy-done.1, bf16[512,512]{1,0:T(8,128)(2,1)S(1)} %pad_maximum_fusion.rows_own_ref, ...), custom_call_target="tpu_custom_call" | custom-call | flops 536870912 | bytes 8388608 | tf_op jit(solution)/shard_map/half_step/pallas_call | solution.py:239
  89.2 0.3 collective-permute-done.2.other_ref
  89.5 0.0 copy-done.2
  89.5 11.1 %update.1 = f32[512,512]{1,0:T(8,128)} custom-call(s32[1,128]{1,0:T(1,128)S(1)} %bitcast.12, bf16[512,1024]{1,0:T(8,128)(2,1)S(1)} %copy-done.1, f32[512,128]{1,0:T(8,128)S(1)} %get-tuple-element.23.col_norm_ref, bf16[512,512]{1,0:T(8,128)(2,1)S(1)} %collective-permute-done.1.rows_other_ref.rows_ref, f32[512,128]{1,0:T(8,128)S(1)} %get-tuple-element.24.row_norm_ref, ...), custom_call_target="tpu_custom_call" | custom-call | tf_op jit(solution)/shard_map/update/pallas_call | solution.py:317
  (1 shorter events, 0.0 us)
Async XLA Ops:
  0.0 1.2 %copy-start = (f32[512,512]{1,0:T(8,128)S(1)}, f32[512,512]{1,0:T(8,128)}, u32[]{:S(2)}) copy-start(f32[512,512]{1,0:T(8,128)} %param.8) | copy-start | bytes 3145732
  1.2 1.0 copy-start.3
  2.2 0.7 copy-start.4
  3.0 10.0 %collective-permute-start = (bf16[1088,128]{1,0:T(8,128)(2,1)S(1)}, bf16[1088,128]{1,0:T(8,128)(2,1)S(1)}, u32[]{:S(2)}, u32[]{:S(2)}) collective-permute-start(bf16[1088,128]{1,0:T(8,128)(2,1)S(1)} %get-tuple-element.18), channel_id=1, source_target_pairs={{0,4},{4,0},{1,5},{5,1},{2,6},{6,2},{3,7},{7,3},{8,12},{12,8},{9,1... | collective-permute-start | bytes 835592 | tf_op jit(solution)/shard_map/ppermute | solution.py:342
  64.6 14.5 %all-to-all-start.2 = ((bf16[4,1024,128]{2,1,0:T(8,128)(2,1)}), bf16[4,1024,128]{2,1,0:T(8,128)(2,1)}, u32[]{:S(2)}, u32[]{:S(2)}) async-start(bf16[4,1024,128]{2,1,0:T(8,128)(2,1)} %third_operand.1), calls=%async_computation.2 | async-start | bytes 2097152 | tf_op jit(solution)/shard_map/all_to_all | solution.py:347
  68.9 18.1 %copy-start.1 = (bf16[512,1024]{1,0:T(8,128)(2,1)S(1)}, bf16[512,1024]{1,0:T(8,128)(2,1)}, u32[]{:S(2)}) copy-start(bf16[512,1024]{1,0:T(8,128)(2,1)} %cols_ref.3) | copy-start | bytes 3145732
  69.1 8.2 %collective-permute-start.1 = (bf16[512,512]{1,0:T(8,128)(2,1)S(1)}, bf16[512,512]{1,0:T(8,128)(2,1)S(1)}, u32[]{:S(2)}, u32[]{:S(2)}) collective-permute-start(bf16[512,512]{1,0:T(8,128)(2,1)S(1)} %pad_maximum_fusion.rows_own_ref), channel_id=1, source_target_pairs={{0,4},{4,0},{1,5},{5,1},{2,6},{6,2},{3,7},{7,3},{8,12},{12,8},{9,1... | collective-permute-start | bytes 1572872 | tf_op jit(solution)/shard_map/ppermute | solution.py:351
  79.1 10.4 %copy-start.2 = (f32[512,512]{1,0:T(8,128)S(1)}, f32[512,512]{1,0:T(8,128)}, u32[]{:S(2)}) copy-start(f32[512,512]{1,0:T(8,128)} %trailing_ref.1) | copy-start | bytes 3145732
  79.1 10.4 %collective-permute-start.2 = (bf16[4,1024,128]{2,1,0:T(8,128)(2,1)}, bf16[4,1024,128]{2,1,0:T(8,128)(2,1)S(1)}, u32[]{:S(2)}, u32[]{:S(2)}) collective-permute-start(bf16[4,1024,128]{2,1,0:T(8,128)(2,1)} %all-to-all-done.2.mine_hbm), channel_id=1, source_target_pairs={{0,4},{4,0},{1,5},{5,1},{2,6},{6,2},{3,7},{7,3},{8,12},{12,8},{9,1... | collective-permute-start | bytes 3145736 | tf_op jit(solution)/shard_map/ppermute | solution.py:353

commit v9 on v8

--- a/solution.py
+++ b/solution.py
@@ -55,9 +55,14 @@
     return theta
 
 
-def prep_body(panel_ref, x_ref, inv_ref, rows_ref, kept_ref, sent_ref):
-    core = lax.axis_index("core")
+def prep_body(x_hbm, inv_hbm, rows_ref, kept_ref, sent_ref, x_ref, inv_ref, sems):
+    row, core = lax.axis_index("row"), lax.axis_index("core")
     size, width = x_ref.shape
+    take = pl.ds(pl.multiple_of(row * size, size), size)
+    copy_x = pltpu.make_async_copy(x_hbm.at[take, :], x_ref, sems.at[0])
+    copy_inv = pltpu.make_async_copy(inv_hbm.at[take, :], inv_ref, sems.at[1])
+    copy_x.start()
+    copy_inv.start()
     half, groups = width // CORES, inv_ref.shape[1] // LANES
     rows = size // CORES
     base = size * (half // LANES)
@@ -73,6 +78,8 @@
                     to = end + CORES * count * i + count * which
                     out_ref[to : to + count, :] = rows_ref[:, LANES * i : LANES * (i + 1)]
 
+    copy_x.wait()
+    copy_inv.wait()
     for out_ref, which in ((kept_ref, core), (sent_ref, 1 - core)):
         for i in range(half // LANES):
             at = pl.multiple_of(which * half + LANES * i, LANES)
@@ -87,21 +94,27 @@
 
 
 VMEM = pl.BlockSpec(memory_space=pltpu.VMEM)
+ANY = pl.BlockSpec(memory_space=pl.ANY)
 SMALL = pltpu.CompilerParams(vmem_limit_bytes=4 * 2**20)
 
 
-def prep(panel, x, inverse, rows):
-    size, width = x.shape
-    total = (width * size // CORES + 2 * inverse.size // CORES + CORES * rows.size) // LANES
+def prep(vectors, inverse, rows, quarter):
+    size, width = vectors.shape
+    total = (width * quarter // CORES + 2 * quarter * size // CORES + CORES * rows.size) // LANES
     out = jax.ShapeDtypeStruct((total, LANES), jnp.bfloat16)
     return pl.pallas_call(
         prep_body,
-        in_specs=[VMEM] * 4,
+        in_specs=[ANY, ANY, VMEM],
         out_specs=[VMEM, VMEM],
         out_shape=[out, out],
-        compiler_params=SMALL,
+        scratch_shapes=[
+            pltpu.VMEM((quarter, width), jnp.bfloat16),
+            pltpu.VMEM((quarter, size), jnp.float32),
+            pltpu.SemaphoreType.DMA((2,)),
+        ],
+        compiler_params=pltpu.CompilerParams(vmem_limit_bytes=211 * 2**18),
         name="prep",
-    )(panel, x, inverse, rows)
+    )(vectors, inverse, rows)
 
 
 def owner_of(panel_ref):
@@ -332,13 +345,10 @@
 def on_device(chips, row_count, panel, centres_cols, centres_rows, diag_inverse, trailing):
     size, width = centres_cols.shape
     quarter = size // row_count
-    row = lax.axis_index("row")
     panel = panel[None]
     swap = [(0, 1), (1, 0)]
 
-    x = lax.dynamic_slice_in_dim(centres_cols, row * quarter, quarter, 0)
-    inverse = lax.dynamic_slice_in_dim(diag_inverse, row * quarter, quarter, 0)
-    kept, sent = prep(panel, x, inverse, centres_rows)
+    kept, sent = prep(centres_cols, diag_inverse, centres_rows, quarter)
     got = lax.ppermute(sent, "core", swap)
     per_chip = (2 * width * quarter // CORES) // (LANES * chips)
     outgoing, rows_chip = first_operand(panel, kept, got, chips, per_chip)

time: 101 us -> 100 us (0.990)
  local copies, waits for them, and re-layouts: 2.97 us -> 1.45 us
    pallas_call x1, Pallas kernels: 0.11 us -> 1.14 us  [prep(): pl.pallas_call(prep_body, in_specs=[ANY, ANY, VMEM], out_specs=[VMEM, VME...]
where the time goes in v9:
time: 100 us; the launch traced here: 99.6 us
  blocking collectives  50.2 us (50%)
  starting transfers between devices  27.8 us (28%)
  Pallas kernels  15.8 us (16%)
  waiting for transfers between devices  4.23 us (4%)
  local copies, waits for them, and re-layouts  1.45 us (1%)
    all_to_all x1, blocking collectives, on_device(): lax.all_to_all(second_operand(panel, first, rows_chip), 'chip', 0, 0)  26.4 us
    all_to_all x1, blocking collectives, on_device(): first = lax.all_to_all(outgoing, 'chip', 0, 0)  23.8 us
    pallas_call x1, Pallas kernels, update(): pl.pallas_call(update_body, in_specs=[VMEM] * 11, out_specs=VMEM, out_sha...  11.1 us
    ppermute x1, starting transfers between devices, on_device(): got = lax.ppermute(sent, 'core', swap)  8.79 us
    ppermute x1, starting transfers between devices, on_device(): all_other = lax.ppermute(all_mine, 'core', swap)  8.12 us
    ppermute x1, starting transfers between devices, on_device(): rows_other = lax.ppermute(rows_own, 'core', swap)  6.91 us
    all_to_all x1, starting transfers between devices, on_device(): lax.all_to_all(third_operand(second, row_count, per_chip), 'row', 0, 0)  4.01 us
    pallas_call x1, Pallas kernels, half_step(): pl.pallas_call(half_body, in_specs=[VMEM] * 3 + [pl.BlockSpec(memory_spac...  2.06 us
  transfers between devices with their start and end apart: 4, of which 4 were waited for; matrix products, arithmetic and copies ran while one was open for 0% of the time, Pallas kernels for 2%

profile of v9, /device:TPU:1, one launch (start us, length us, event | category | flops | bytes accessed | tf_op | source)
XLA Modules:
  0.0 99.6 jit_solution(11626459500581552008)
XLA Ops:
  0.0 0.0 copy-start.2
  0.0 0.7 copy-done.2
  0.7 1.1 %prep.1 = (bf16[1088,128]{1,0:T(8,128)(2,1)S(1)}, bf16[1088,128]{1,0:T(8,128)(2,1)S(1)}) custom-call(bf16[512,1024]{1,0:T(8,128)(2,1)} %cols_ref.3, f32[512,512]{1,0:T(8,128)} %inv_hbm.1, bf16[4,1024]{1,0:T(4,128)(2,1)S(1)} %copy-done.2), custom_call_target="tpu_custom_call" | custom-call | tf_op jit(solution)/shard_map/prep/pallas_call | solution.py:105
  1.8 8.8 %collective-permute-start = (bf16[1088,128]{1,0:T(8,128)(2,1)S(1)}, bf16[1088,128]{1,0:T(8,128)(2,1)S(1)}, u32[]{:S(2)}, u32[]{:S(2)}) collective-permute-start(bf16[1088,128]{1,0:T(8,128)(2,1)S(1)} %get-tuple-element.18), channel_id=1, source_target_pairs={{0,4},{4,0},{1,5},{5,1},{2,6},{6,2},{3,7},{7,3},{8,12},{12,8},{9,1... | collective-permute-start | bytes 835592 | tf_op jit(solution)/shard_map/ppermute | solution.py:352
  10.6 1.2 %collective-permute-done.got_ref = bf16[1088,128]{1,0:T(8,128)(2,1)S(1)} collective-permute-done((bf16[1088,128]{1,0:T(8,128)(2,1)S(1)}, bf16[1088,128]{1,0:T(8,128)(2,1)S(1)}, u32[]{:S(2)}, u32[]{:S(2)}) %collective-permute-start) | collective-permute-done | bytes 278560 | tf_op jit(solution)/shard_map/ppermute | solution.py:352
  11.8 0.0 copy-start.3
  11.8 0.7 copy-done.3
  12.5 0.2 first_operand.1
  12.7 23.8 %all_to_all.15.came_ref = bf16[64,16,128]{2,1,0:T(8,128)(2,1)S(1)} all-to-all(bf16[64,16,128]{2,1,0:T(8,128)(2,1)S(1)} %get-tuple-element.19), channel_id=1, replica_groups=mesh['chip'=64,'core'=2,'row'=4] {'chip'}, dimensions={0} | all-to-all | bytes 524288 | tf_op jit(solution)/shard_map/all_to_all | solution.py:355
  36.4 0.2 second_operand.1
  36.6 26.4 %all_to_all.16.came_ref = bf16[64,48,128]{2,1,0:T(8,128)(2,1)S(1)} all-to-all(bf16[64,48,128]{2,1,0:T(8,128)(2,1)S(1)} %second_operand.1), channel_id=1, replica_groups=mesh['chip'=64,'core'=2,'row'=4] {'chip'}, dimensions={0} | all-to-all | bytes 1572864 | tf_op jit(solution)/shard_map/all_to_all | solution.py:356
  63.0 1.1 %third_operand.1 = bf16[4,1024,128]{2,1,0:T(8,128)(2,1)} custom-call(bf16[64,48,128]{2,1,0:T(8,128)(2,1)S(1)} %all_to_all.16.came_ref), custom_call_target="tpu_custom_call" | custom-call | tf_op jit(solution)/shard_map/third_operand/pallas_call | solution.py:179
  64.1 4.0 %all-to-all-start.2 = ((bf16[4,1024,128]{2,1,0:T(8,128)(2,1)}), bf16[4,1024,128]{2,1,0:T(8,128)(2,1)S(1)}, u32[]{:S(2)}, u32[]{:S(2)}) async-start(bf16[4,1024,128]{2,1,0:T(8,128)(2,1)} %third_operand.1), calls=%async_computation.2 | async-start | bytes 2097152 | tf_op jit(solution)/shard_map/all_to_all | solution.py:357
  68.1 0.0 copy-start
  68.1 0.1 slice_bitcast_fusion.3
  68.2 0.1 pad_maximum_fusion.rows_own_ref
  68.3 6.9 %collective-permute-start.1 = (bf16[512,512]{1,0:T(8,128)(2,1)S(1)}, bf16[512,512]{1,0:T(8,128)(2,1)S(1)}, u32[]{:S(2)}, u32[]{:S(2)}) collective-permute-start(bf16[512,512]{1,0:T(8,128)(2,1)S(1)} %pad_maximum_fusion.rows_own_ref), channel_id=1, source_target_pairs={{0,4},{4,0},{1,5},{5,1},{2,6},{6,2},{3,7},{7,3},{8,12},{12,8},{9,1... | collective-permute-start | bytes 1572872 | tf_op jit(solution)/shard_map/ppermute | solution.py:361
  75.2 1.5 %collective-permute-done.1.rows_other_ref.rows_ref = bf16[512,512]{1,0:T(8,128)(2,1)S(1)} collective-permute-done((bf16[512,512]{1,0:T(8,128)(2,1)S(1)}, bf16[512,512]{1,0:T(8,128)(2,1)S(1)}, u32[]{:S(2)}, u32[]{:S(2)}) %collective-permute-start.1) | collective-permute-done | bytes 524320 | tf_op jit(solution)/shard_map/ppermute | solution.py:361
  76.7 1.4 %all-to-all-done.2.mine_hbm = bf16[4,1024,128]{2,1,0:T(8,128)(2,1)S(1)} async-done(((bf16[4,1024,128]{2,1,0:T(8,128)(2,1)}), bf16[4,1024,128]{2,1,0:T(8,128)(2,1)S(1)}, u32[]{:S(2)}, u32[]{:S(2)}) %all-to-all-start.2) | async-done | bytes 1048608 | tf_op jit(solution)/shard_map/all_to_all | solution.py:357
  78.1 0.0 copy-start.1
  78.1 8.1 %collective-permute-start.2 = (bf16[4,1024,128]{2,1,0:T(8,128)(2,1)S(1)}, bf16[4,1024,128]{2,1,0:T(8,128)(2,1)S(1)}, u32[]{:S(2)}, u32[]{:S(2)}) collective-permute-start(bf16[4,1024,128]{2,1,0:T(8,128)(2,1)S(1)} %all-to-all-done.2.mine_hbm), channel_id=1, source_target_pairs={{0,4},{4,0},{1,5},{5,1},{2,6},{6,2},{3,7},{7,3},{8,12},{12,8},{9,1... | collective-permute-start | bytes 3145736 | tf_op jit(solution)/shard_map/ppermute | solution.py:363
  86.2 0.0 copy-done
  86.2 2.1 %half_step.1 = (f32[512,128]{1,0:T(8,128)S(1)}, f32[512,128]{1,0:T(8,128)S(1)}, f32[512,512]{1,0:T(8,128)S(1)}, f32[512,512]{1,0:T(8,128)S(1)}, f32[8,512]{1,0:T(8,128)S(1)}, /*index=5*/bf16[256,1536]{1,0:T(8,128)(2,1)S(1)}) custom-call(bf16[512,1024]{1,0:T(8,128)(2,1)S(1)} %copy-done, bf16[512,512]{1,0:T(8,128)(2,1)S(1)} %pad_maximum_fusion.rows_own_ref, ...), custom_call_target="tpu_custom_call" | custom-call | flops 536870912 | bytes 8388608 | tf_op jit(solution)/shard_map/half_step/pallas_call | solution.py:252
  88.3 0.2 collective-permute-done.2.other_ref
  88.5 0.0 copy-done.1
  88.5 11.1 %update.1 = f32[512,512]{1,0:T(8,128)} custom-call(s32[1,128]{1,0:T(1,128)S(1)} %bitcast.11, bf16[512,1024]{1,0:T(8,128)(2,1)S(1)} %copy-done, f32[512,128]{1,0:T(8,128)S(1)} %get-tuple-element.23.col_norm_ref, bf16[512,512]{1,0:T(8,128)(2,1)S(1)} %collective-permute-done.1.rows_other_ref.rows_ref, f32[512,128]{1,0:T(8,128)S(1)} %get-tuple-element.24.row_norm_ref, ...), custom_call_target="tpu_custom_call" | custom-call | tf_op jit(solution)/shard_map/update/pallas_call | solution.py:330
Async XLA Ops:
  0.0 0.7 copy-start.2
  1.8 10.0 %collective-permute-start = (bf16[1088,128]{1,0:T(8,128)(2,1)S(1)}, bf16[1088,128]{1,0:T(8,128)(2,1)S(1)}, u32[]{:S(2)}, u32[]{:S(2)}) collective-permute-start(bf16[1088,128]{1,0:T(8,128)(2,1)S(1)} %get-tuple-element.18), channel_id=1, source_target_pairs={{0,4},{4,0},{1,5},{5,1},{2,6},{6,2},{3,7},{7,3},{8,12},{12,8},{9,1... | collective-permute-start | bytes 835592 | tf_op jit(solution)/shard_map/ppermute | solution.py:352
  11.8 0.7 copy-start.3
  64.1 14.0 %all-to-all-start.2 = ((bf16[4,1024,128]{2,1,0:T(8,128)(2,1)}), bf16[4,1024,128]{2,1,0:T(8,128)(2,1)S(1)}, u32[]{:S(2)}, u32[]{:S(2)}) async-start(bf16[4,1024,128]{2,1,0:T(8,128)(2,1)} %third_operand.1), calls=%async_computation.2 | async-start | bytes 2097152 | tf_op jit(solution)/shard_map/all_to_all | solution.py:357
  68.1 18.1 %copy-start = (bf16[512,1024]{1,0:T(8,128)(2,1)S(1)}, bf16[512,1024]{1,0:T(8,128)(2,1)}, u32[]{:S(2)}) copy-start(bf16[512,1024]{1,0:T(8,128)(2,1)} %cols_ref.3) | copy-start | bytes 3145732
  68.3 8.4 %collective-permute-start.1 = (bf16[512,512]{1,0:T(8,128)(2,1)S(1)}, bf16[512,512]{1,0:T(8,128)(2,1)S(1)}, u32[]{:S(2)}, u32[]{:S(2)}) collective-permute-start(bf16[512,512]{1,0:T(8,128)(2,1)S(1)} %pad_maximum_fusion.rows_own_ref), channel_id=1, source_target_pairs={{0,4},{4,0},{1,5},{5,1},{2,6},{6,2},{3,7},{7,3},{8,12},{12,8},{9,1... | collective-permute-start | bytes 1572872 | tf_op jit(solution)/shard_map/ppermute | solution.py:361
  78.1 10.4 %copy-start.1 = (f32[512,512]{1,0:T(8,128)S(1)}, f32[512,512]{1,0:T(8,128)}, u32[]{:S(2)}) copy-start(f32[512,512]{1,0:T(8,128)} %trailing_ref.1) | copy-start | bytes 3145732
  78.1 10.4 %collective-permute-start.2 = (bf16[4,1024,128]{2,1,0:T(8,128)(2,1)S(1)}, bf16[4,1024,128]{2,1,0:T(8,128)(2,1)S(1)}, u32[]{:S(2)}, u32[]{:S(2)}) collective-permute-start(bf16[4,1024,128]{2,1,0:T(8,128)(2,1)S(1)} %all-to-all-done.2.mine_hbm), channel_id=1, source_target_pairs={{0,4},{4,0},{1,5},{5,1},{2,6},{6,2},{3,7},{7,3},{8,12},{12,8},{9,1... | collective-permute-start | bytes 3145736 | tf_op jit(solution)/shard_map/ppermute | solution.py:363

commit v10 on v9

--- a/solution.py
+++ b/solution.py
@@ -55,14 +55,19 @@
     return theta
 
 
-def prep_body(x_hbm, inv_hbm, rows_ref, kept_ref, sent_ref, x_ref, inv_ref, sems):
+def prep_body(x_hbm, inv_hbm, rows_hbm, panel_hbm, kept_ref, sent_ref, panel_ref, x_ref, inv_ref, rows_ref, sems):
     row, core = lax.axis_index("row"), lax.axis_index("core")
     size, width = x_ref.shape
     take = pl.ds(pl.multiple_of(row * size, size), size)
     copy_x = pltpu.make_async_copy(x_hbm.at[take, :], x_ref, sems.at[0])
     copy_inv = pltpu.make_async_copy(inv_hbm.at[take, :], inv_ref, sems.at[1])
+    copy_rows = pltpu.make_async_copy(rows_hbm, rows_ref, sems.at[2])
+    copy_panel = pltpu.make_async_copy(panel_hbm, panel_ref, sems.at[3])
+    copy_rows.start()
+    copy_panel.start()
     copy_x.start()
     copy_inv.start()
+    copy_rows.wait()
     half, groups = width // CORES, inv_ref.shape[1] // LANES
     rows = size // CORES
     base = size * (half // LANES)
@@ -80,6 +85,7 @@
 
     copy_x.wait()
     copy_inv.wait()
+    copy_panel.wait()
     for out_ref, which in ((kept_ref, core), (sent_ref, 1 - core)):
         for i in range(half // LANES):
             at = pl.multiple_of(which * half + LANES * i, LANES)
@@ -98,23 +104,24 @@
 SMALL = pltpu.CompilerParams(vmem_limit_bytes=4 * 2**20)
 
 
-def prep(vectors, inverse, rows, quarter):
+def prep(panel, vectors, inverse, rows, quarter):
     size, width = vectors.shape
     total = (width * quarter // CORES + 2 * quarter * size // CORES + CORES * rows.size) // LANES
     out = jax.ShapeDtypeStruct((total, LANES), jnp.bfloat16)
     return pl.pallas_call(
         prep_body,
-        in_specs=[ANY, ANY, VMEM],
-        out_specs=[VMEM, VMEM],
-        out_shape=[out, out],
+        in_specs=[ANY] * 4,
+        out_specs=[VMEM] * 3,
+        out_shape=[out, out, jax.ShapeDtypeStruct(panel.shape, panel.dtype)],
         scratch_shapes=[
             pltpu.VMEM((quarter, width), jnp.bfloat16),
             pltpu.VMEM((quarter, size), jnp.float32),
-            pltpu.SemaphoreType.DMA((2,)),
+            pltpu.VMEM(rows.shape, rows.dtype),
+            pltpu.SemaphoreType.DMA((4,)),
         ],
         compiler_params=pltpu.CompilerParams(vmem_limit_bytes=211 * 2**18),
         name="prep",
-    )(vectors, inverse, rows)
+    )(vectors, inverse, rows, panel)
 
 
 def owner_of(panel_ref):
@@ -348,7 +355,7 @@
     panel = panel[None]
     swap = [(0, 1), (1, 0)]
 
-    kept, sent = prep(centres_cols, diag_inverse, centres_rows, quarter)
+    kept, sent, panel = prep(panel, centres_cols, diag_inverse, centres_rows, quarter)
     got = lax.ppermute(sent, "core", swap)
     per_chip = (2 * width * quarter // CORES) // (LANES * chips)
     outgoing, rows_chip = first_operand(panel, kept, got, chips, per_chip)

time: 100 us -> 100 us (level)
  no operation moved by 1% of the time
where the time goes in v10:
time: 100 us; the launch traced here: 99.7 us
  blocking collectives  50.2 us (50%)
  starting transfers between devices  27.8 us (28%)
  Pallas kernels  15.8 us (16%)
  waiting for transfers between devices  4.23 us (4%)
  local copies, waits for them, and re-layouts  1.45 us (1%)
    all_to_all x1, blocking collectives, on_device(): lax.all_to_all(second_operand(panel, first, rows_chip), 'chip', 0, 0)  26.4 us
    all_to_all x1, blocking collectives, on_device(): first = lax.all_to_all(outgoing, 'chip', 0, 0)  23.8 us
    pallas_call x1, Pallas kernels, update(): pl.pallas_call(update_body, in_specs=[VMEM] * 11, out_specs=VMEM, out_sha...  11.1 us
    ppermute x1, starting transfers between devices, on_device(): got = lax.ppermute(sent, 'core', swap)  8.79 us
    ppermute x1, starting transfers between devices, on_device(): all_other = lax.ppermute(all_mine, 'core', swap)  8.12 us
    ppermute x1, starting transfers between devices, on_device(): rows_other = lax.ppermute(rows_own, 'core', swap)  6.91 us
    all_to_all x1, starting transfers between devices, on_device(): lax.all_to_all(third_operand(second, row_count, per_chip), 'row', 0, 0)  4.01 us
    pallas_call x1, Pallas kernels, half_step(): pl.pallas_call(half_body, in_specs=[VMEM] * 3 + [pl.BlockSpec(memory_spac...  2.06 us
  transfers between devices with their start and end apart: 4, of which 4 were waited for; matrix products, arithmetic and copies ran while one was open for 0% of the time, Pallas kernels for 2%

profile of v10, /device:TPU:1, one launch (start us, length us, event | category | flops | bytes accessed | tf_op | source)
XLA Modules:
  0.0 99.7 jit_solution(6365518953830820958)
XLA Ops:
  0.0 0.0 copy-start.3
  0.0 0.7 copy-done.3
  0.7 0.0 copy-start.2
  0.7 0.7 copy-done.2
  1.4 1.2 %prep.1 = (bf16[1088,128]{1,0:T(8,128)(2,1)S(1)}, bf16[1088,128]{1,0:T(8,128)(2,1)S(1)}, s32[1,128]{1,0:T(1,128)S(1)}) custom-call(bf16[512,1024]{1,0:T(8,128)(2,1)} %cols_ref.3, f32[512,512]{1,0:T(8,128)} %inv_hbm.1, bf16[4,1024]{1,0:T(4,128)(2,1)S(1)} %copy-done.2, s32[1,128]{1,0:T(1,128)S(1)} %bitcast.9), custom_call_target="tpu_custom_call" | custom-call | tf_op jit(solution)/shard_map/prep/pallas_call | solution.py:111
  2.5 8.8 %collective-permute-start = (bf16[1088,128]{1,0:T(8,128)(2,1)S(1)}, bf16[1088,128]{1,0:T(8,128)(2,1)S(1)}, u32[]{:S(2)}, u32[]{:S(2)}) collective-permute-start(bf16[1088,128]{1,0:T(8,128)(2,1)S(1)} %get-tuple-element.20), channel_id=1, source_target_pairs={{0,4},{4,0},{1,5},{5,1},{2,6},{6,2},{3,7},{7,3},{8,12},{12,8},{9,1... | collective-permute-start | bytes 835592 | tf_op jit(solution)/shard_map/ppermute | solution.py:359
  11.3 1.2 %collective-permute-done.got_ref = bf16[1088,128]{1,0:T(8,128)(2,1)S(1)} collective-permute-done((bf16[1088,128]{1,0:T(8,128)(2,1)S(1)}, bf16[1088,128]{1,0:T(8,128)(2,1)S(1)}, u32[]{:S(2)}, u32[]{:S(2)}) %collective-permute-start) | collective-permute-done | bytes 278560 | tf_op jit(solution)/shard_map/ppermute | solution.py:359
  12.5 0.2 first_operand.1
  12.7 23.8 %all_to_all.15.came_ref = bf16[64,16,128]{2,1,0:T(8,128)(2,1)S(1)} all-to-all(bf16[64,16,128]{2,1,0:T(8,128)(2,1)S(1)} %get-tuple-element.21), channel_id=1, replica_groups=mesh['chip'=64,'core'=2,'row'=4] {'chip'}, dimensions={0} | all-to-all | bytes 524288 | tf_op jit(solution)/shard_map/all_to_all | solution.py:362
  36.4 0.2 second_operand.1
  36.6 26.4 %all_to_all.16.came_ref = bf16[64,48,128]{2,1,0:T(8,128)(2,1)S(1)} all-to-all(bf16[64,48,128]{2,1,0:T(8,128)(2,1)S(1)} %second_operand.1), channel_id=1, replica_groups=mesh['chip'=64,'core'=2,'row'=4] {'chip'}, dimensions={0} | all-to-all | bytes 1572864 | tf_op jit(solution)/shard_map/all_to_all | solution.py:363
  63.1 1.1 %third_operand.1 = bf16[4,1024,128]{2,1,0:T(8,128)(2,1)} custom-call(bf16[64,48,128]{2,1,0:T(8,128)(2,1)S(1)} %all_to_all.16.came_ref), custom_call_target="tpu_custom_call" | custom-call | tf_op jit(solution)/shard_map/third_operand/pallas_call | solution.py:186
  64.2 4.0 %all-to-all-start.2 = ((bf16[4,1024,128]{2,1,0:T(8,128)(2,1)}), bf16[4,1024,128]{2,1,0:T(8,128)(2,1)S(1)}, u32[]{:S(2)}, u32[]{:S(2)}) async-start(bf16[4,1024,128]{2,1,0:T(8,128)(2,1)} %third_operand.1), calls=%async_computation.2 | async-start | bytes 2097152 | tf_op jit(solution)/shard_map/all_to_all | solution.py:364
  68.2 0.0 copy-start
  68.2 0.1 slice_bitcast_fusion.3
  68.3 0.1 pad_maximum_fusion.rows_own_ref
  68.3 6.9 %collective-permute-start.1 = (bf16[512,512]{1,0:T(8,128)(2,1)S(1)}, bf16[512,512]{1,0:T(8,128)(2,1)S(1)}, u32[]{:S(2)}, u32[]{:S(2)}) collective-permute-start(bf16[512,512]{1,0:T(8,128)(2,1)S(1)} %pad_maximum_fusion.rows_own_ref), channel_id=1, source_target_pairs={{0,4},{4,0},{1,5},{5,1},{2,6},{6,2},{3,7},{7,3},{8,12},{12,8},{9,1... | collective-permute-start | bytes 1572872 | tf_op jit(solution)/shard_map/ppermute | solution.py:368
  75.3 1.5 %collective-permute-done.1.rows_other_ref.rows_ref = bf16[512,512]{1,0:T(8,128)(2,1)S(1)} collective-permute-done((bf16[512,512]{1,0:T(8,128)(2,1)S(1)}, bf16[512,512]{1,0:T(8,128)(2,1)S(1)}, u32[]{:S(2)}, u32[]{:S(2)}) %collective-permute-start.1) | collective-permute-done | bytes 524320 | tf_op jit(solution)/shard_map/ppermute | solution.py:368
  76.8 1.4 %all-to-all-done.2.mine_hbm = bf16[4,1024,128]{2,1,0:T(8,128)(2,1)S(1)} async-done(((bf16[4,1024,128]{2,1,0:T(8,128)(2,1)}), bf16[4,1024,128]{2,1,0:T(8,128)(2,1)S(1)}, u32[]{:S(2)}, u32[]{:S(2)}) %all-to-all-start.2) | async-done | bytes 1048608 | tf_op jit(solution)/shard_map/all_to_all | solution.py:364
  78.1 0.0 copy-start.1
  78.1 8.1 %collective-permute-start.2 = (bf16[4,1024,128]{2,1,0:T(8,128)(2,1)S(1)}, bf16[4,1024,128]{2,1,0:T(8,128)(2,1)S(1)}, u32[]{:S(2)}, u32[]{:S(2)}) collective-permute-start(bf16[4,1024,128]{2,1,0:T(8,128)(2,1)S(1)} %all-to-all-done.2.mine_hbm), channel_id=1, source_target_pairs={{0,4},{4,0},{1,5},{5,1},{2,6},{6,2},{3,7},{7,3},{8,12},{12,8},{9,1... | collective-permute-start | bytes 3145736 | tf_op jit(solution)/shard_map/ppermute | solution.py:370
  86.3 0.0 copy-done
  86.3 2.1 %half_step.1 = (f32[512,128]{1,0:T(8,128)S(1)}, f32[512,128]{1,0:T(8,128)S(1)}, f32[512,512]{1,0:T(8,128)S(1)}, f32[512,512]{1,0:T(8,128)S(1)}, f32[8,512]{1,0:T(8,128)S(1)}, /*index=5*/bf16[256,1536]{1,0:T(8,128)(2,1)S(1)}) custom-call(bf16[512,1024]{1,0:T(8,128)(2,1)S(1)} %copy-done, bf16[512,512]{1,0:T(8,128)(2,1)S(1)} %pad_maximum_fusion.rows_own_ref, ...), custom_call_target="tpu_custom_call" | custom-call | flops 536870912 | bytes 8388608 | tf_op jit(solution)/shard_map/half_step/pallas_call | solution.py:259
  88.3 0.2 collective-permute-done.2.other_ref
  88.5 0.0 copy-done.1
  88.5 11.1 %update.1 = f32[512,512]{1,0:T(8,128)} custom-call(s32[1,128]{1,0:T(1,128)S(1)} %get-tuple-element.18.panel_ref, bf16[512,1024]{1,0:T(8,128)(2,1)S(1)} %copy-done, f32[512,128]{1,0:T(8,128)S(1)} %get-tuple-element.25.col_norm_ref, bf16[512,512]{1,0:T(8,128)(2,1)S(1)} %collective-permute-done.1.rows_other_ref.rows_ref, ...), custom_call_target="tpu_custom_call" | custom-call | tf_op jit(solution)/shard_map/update/pallas_call | solution.py:337
Async XLA Ops:
  0.0 0.7 copy-start.3
  0.7 0.7 copy-start.2
  2.5 10.0 %collective-permute-start = (bf16[1088,128]{1,0:T(8,128)(2,1)S(1)}, bf16[1088,128]{1,0:T(8,128)(2,1)S(1)}, u32[]{:S(2)}, u32[]{:S(2)}) collective-permute-start(bf16[1088,128]{1,0:T(8,128)(2,1)S(1)} %get-tuple-element.20), channel_id=1, source_target_pairs={{0,4},{4,0},{1,5},{5,1},{2,6},{6,2},{3,7},{7,3},{8,12},{12,8},{9,1... | collective-permute-start | bytes 835592 | tf_op jit(solution)/shard_map/ppermute | solution.py:359
  64.2 14.0 %all-to-all-start.2 = ((bf16[4,1024,128]{2,1,0:T(8,128)(2,1)}), bf16[4,1024,128]{2,1,0:T(8,128)(2,1)S(1)}, u32[]{:S(2)}, u32[]{:S(2)}) async-start(bf16[4,1024,128]{2,1,0:T(8,128)(2,1)} %third_operand.1), calls=%async_computation.2 | async-start | bytes 2097152 | tf_op jit(solution)/shard_map/all_to_all | solution.py:364
  68.2 18.1 %copy-start = (bf16[512,1024]{1,0:T(8,128)(2,1)S(1)}, bf16[512,1024]{1,0:T(8,128)(2,1)}, u32[]{:S(2)}) copy-start(bf16[512,1024]{1,0:T(8,128)(2,1)} %cols_ref.3) | copy-start | bytes 3145732
  68.3 8.4 %collective-permute-start.1 = (bf16[512,512]{1,0:T(8,128)(2,1)S(1)}, bf16[512,512]{1,0:T(8,128)(2,1)S(1)}, u32[]{:S(2)}, u32[]{:S(2)}) collective-permute-start(bf16[512,512]{1,0:T(8,128)(2,1)S(1)} %pad_maximum_fusion.rows_own_ref), channel_id=1, source_target_pairs={{0,4},{4,0},{1,5},{5,1},{2,6},{6,2},{3,7},{7,3},{8,12},{12,8},{9,1... | collective-permute-start | bytes 1572872 | tf_op jit(solution)/shard_map/ppermute | solution.py:368
  78.1 10.4 %copy-start.1 = (f32[512,512]{1,0:T(8,128)S(1)}, f32[512,512]{1,0:T(8,128)}, u32[]{:S(2)}) copy-start(f32[512,512]{1,0:T(8,128)} %trailing_ref.1) | copy-start | bytes 3145732
  78.1 10.4 %collective-permute-start.2 = (bf16[4,1024,128]{2,1,0:T(8,128)(2,1)S(1)}, bf16[4,1024,128]{2,1,0:T(8,128)(2,1)S(1)}, u32[]{:S(2)}, u32[]{:S(2)}) collective-permute-start(bf16[4,1024,128]{2,1,0:T(8,128)(2,1)S(1)} %all-to-all-done.2.mine_hbm), channel_id=1, source_target_pairs={{0,4},{4,0},{1,5},{5,1},{2,6},{6,2},{3,7},{7,3},{8,12},{12,8},{9,1... | collective-permute-start | bytes 3145736 | tf_op jit(solution)/shard_map/ppermute | solution.py:370
